TPU v7x, 32 devices: a whole 2x2x4 slice. The times are simulated.
32 devices in a mesh: grp: 2 (over x), tm: 16 (over z, y, core).
Axes of the slice: x: 2, y: 2, z: 4, core: 2. Of those that a mesh axis runs over, the one named last changes fastest.
Arguments:
- queries: bfloat16 [2, 8192, 1120], P(None, ('grp', 'tm')), parts along dimension 1, may hold values from 0.19921875 to 3
- keys: bfloat16 [2, 8192, 1120], P(None, ('grp', 'tm')), parts along dimension 1, may hold values from 0.05 to 24
- values: bfloat16 [2, 8192, 1120], P(None, ('grp', 'tm')), parts along dimension 1, may hold values from -12 to 12
- timesteps: int32 [4], P('grp'), parts along dimension 0, may hold values from 0 to 19
- gate_table: float32 [20, 2240], replicated, may hold values from -3 to 3
- out_weight: bfloat16 [1120, 2240], replicated, may hold values from -0.1875 to 0.1875
- conv_weight: float32 [9, 1120], replicated, may hold values from -1.5 to 1.5
Outputs:
- update: float32 [2, 8192, 2240], P(None, ('grp', 'tm')), parts along dimension 1
- fresh_state: float32 [32, 70, 70], P('grp'), parts along dimension 0
- fresh_total: float32 [32, 70], P('grp'), parts along dimension 0
There are 2 independent parts, one for each index of `grp`. A program takes and returns all parts, laid end to end along the dimension named above; an argument that names none is the same for every part. Nothing has to cross between parts.
All inputs are finite; a program needn't handle non-finite values.
Results may differ from a plain program's by a relative error of at most 0.0003.
The roundings to bfloat16 on the way count: a program that leaves them out, or rounds other values in their place, can miss the bound.
Values may be sent and summed in bfloat16 or wider, within the bound.
No kernel may reach another device: no remote copies, remote signals or barrier semaphores. Data moves between devices by JAX's collectives and lax.ppermute only.
A program may use at most 64 MiB of HBM per device.

v0:
```python
import jax
import jax.numpy as jnp
from jax import lax
from jax.sharding import PartitionSpec as P

NH = 16
HD = 70
COLS = 64
ROWS_DEV = 4


EXACT = lax.Precision.HIGHEST


def extended(cells, sides, width):
    for axis, dim in sides:
        count = lax.axis_size(axis)
        ends = count - 1
        head = lax.slice_in_dim(cells, 0, width, axis=dim)
        tail = lax.slice_in_dim(cells, cells.shape[dim] - width, cells.shape[dim], axis=dim)
        cells = jnp.concatenate(
            [
                lax.ppermute(tail, axis, [(i, (i + 1) % count) for i in range(ends)]),
                cells,
                lax.ppermute(head, axis, [((i + 1) % count, i) for i in range(ends)]),
            ],
            axis=dim,
        )
    return cells


def select_gate(gate_table, position):
    step_ids = jnp.arange(gate_table.shape[0], dtype=jnp.int32)
    return jnp.sum(
        jnp.where((step_ids == position)[:, None], gate_table, jnp.zeros_like(gate_table)), axis=0
    )


def key_value_state(key_rows, values):
    key_grid = key_rows.reshape(-1, NH, HD)
    value_grid = values.reshape(-1, NH, HD)
    key_state = jnp.einsum("rhd,rhe->hde", key_grid, value_grid, preferred_element_type=jnp.float32)
    key_total = jnp.sum(key_grid.astype(jnp.float32), axis=0)
    return (key_state, key_total)


def spread(queries, key_state, key_total):
    query_grid = queries.astype(jnp.float32).reshape(-1, NH, HD)
    numer = jnp.einsum("rhd,hde->rhe", query_grid, key_state, precision=EXACT)
    denom = jnp.einsum("rhd,hd->rh", query_grid, key_total, precision=EXACT)
    return (numer / denom[..., None]).reshape(query_grid.shape[0], NH * HD)


def convolve(padded, conv_weight):
    widened = jnp.pad(padded.astype(jnp.float32), ((0, 0), (1, 1), (0, 0)))
    summed = jnp.zeros((ROWS_DEV, COLS, padded.shape[-1]), jnp.float32)
    for tap_row in range(3):
        for tap_col in range(3):
            summed = (
                summed
                + widened[tap_row : tap_row + ROWS_DEV, tap_col : tap_col + COLS]
                * conv_weight[3 * tap_row + tap_col]
            )
    return summed.reshape(ROWS_DEV * COLS, padded.shape[-1])


def local(queries, keys, values, timesteps, gate_table, out_weight, conv_weight):
    channels = NH * HD
    row_count = queries.shape[1]
    total_tokens = row_count * lax.axis_size("tm")
    gates = [select_gate(gate_table, timesteps[section]) for section in range(2)]
    state_one, total_one = key_value_state(keys[0], values[0])
    fresh_state = None
    fresh_total = None
    whole_state, whole_total = lax.psum((state_one, total_one), "tm")
    state_two, total_two = key_value_state(keys[1], values[1])
    grid_one = values[0].reshape(ROWS_DEV, COLS, channels)
    rim_values = extended(grid_one, (("tm", 0),), 1)
    position = lax.axis_index("tm")
    per_frame = lax.axis_size("tm")
    upper_rim = jnp.where(position % per_frame != 0, rim_values[0], jnp.zeros_like(rim_values[0]))
    lower_rim = jnp.where(
        (position + 1) % per_frame != 0, rim_values[-1], jnp.zeros_like(rim_values[-1])
    )
    padded_one = jnp.concatenate([upper_rim[None], grid_one, lower_rim[None]], axis=0)
    mixed_one = (
        spread(queries[0], whole_state, whole_total) + convolve(padded_one, conv_weight)
    ).astype(jnp.bfloat16)
    update_one = gates[0] * jnp.dot(mixed_one, out_weight, preferred_element_type=jnp.float32)
    fresh_state, fresh_total = lax.psum((state_two, total_two), "tm")
    moved_state = whole_state - state_one + state_two
    moved_total = whole_total - total_one + total_two
    grid_two = values[1].reshape(ROWS_DEV, COLS, channels)
    padded_two = jnp.concatenate([upper_rim[None], grid_two, lower_rim[None]], axis=0)
    mixed_two = (
        spread(queries[1], moved_state, moved_total) + convolve(padded_two, conv_weight)
    ).astype(jnp.bfloat16)
    update_two = gates[1] * jnp.dot(mixed_two, out_weight, preferred_element_type=jnp.float32)
    return (
        jnp.stack([update_one, update_two]),
        fresh_state / total_tokens,
        fresh_total / total_tokens,
    )


def solution(mesh):
    placed = (
        P(None, ("grp", "tm"), None),
        P(None, ("grp", "tm"), None),
        P(None, ("grp", "tm"), None),
        P("grp"),
        P(),
        P(),
        P(),
    )
    return jax.shard_map(
        local,
        mesh=mesh,
        in_specs=placed,
        out_specs=(P(None, ("grp", "tm"), None), P("grp", None, None), P("grp", None)),
        check_vma=False,
    )
```

profile of v0, /device:TPU:1, one launch (start us, length us, event | category | flops | bytes accessed | tf_op | source)
XLA Modules:
  0.0 144.7 jit_solution(6171141517174413717)
XLA Ops:
  7.2 0.0 all-reduce.6.cloned.1.call-start
  7.2 1.3 fusion.37
  8.5 0.8 copy.36
  9.3 1.9 %collective-permute-start.1 = (bf16[1,64,1120]{2,1,0:T(8,128)(2,1)}, bf16[1,64,1120]{2,1,0:T(8,128)(2,1)}, u32[]{:S(2)}, u32[]{:S(2)}) collective-permute-start(bf16[1,64,1120]{2,1,0:T(8,128)(2,1)} %copy.36), channel_id=1, source_target_pairs={{1,0},{2,1},{3,2},{4,3},{5,4},{6,5},{7,6},{8,7},{9,8},{10,9},{11,1... | collective-permute-start | bytes 430088 | tf_op jit(solution)/shard_map/ppermute | solution.py:25
  11.2 0.8 copy.35
  12.1 4.6 %collective-permute-start = (bf16[1,64,1120]{2,1,0:T(8,128)(2,1)}, bf16[1,64,1120]{2,1,0:T(8,128)(2,1)}, u32[]{:S(2)}, u32[]{:S(2)}) collective-permute-start(bf16[1,64,1120]{2,1,0:T(8,128)(2,1)} %copy.35), channel_id=1, source_target_pairs={{0,1},{1,2},{2,3},{3,4},{4,5},{5,6},{6,7},{7,8},{8,9},{9,10},{10,1... | collective-permute-start | bytes 430088 | tf_op jit(solution)/shard_map/ppermute | solution.py:23
  16.7 0.1 fusion.38
  16.8 0.9 fusion.39
  17.7 0.2 reshape_squeeze.18
  17.9 1.2 reshape_squeeze.21
  19.1 1.0 reshape_squeeze.19
  20.0 2.2 %fusion.41 = f32[16,70,70]{2,1,0:T(8,128)} fusion(bf16[256,16,70]{0,2,1:T(8,128)(2,1)S(1)} %reshape_squeeze.18, bf16[256,16,70]{0,2,1:T(8,128)(2,1)} %reshape_squeeze.19), kind=kOutput, calls=%fused_computation.92 | convolution fusion | flops 40140800 | bytes 1460480 | tf_op jit(solution)/shard_map/rhd,rhe->hde/dot_general | solution.py:42
  22.3 0.2 reshape_squeeze.22
  22.4 1.2 fusion.43
  23.6 0.4 convert_reduce_fusion.1
  24.0 0.2 copy-done.9
  24.2 0.6 fusion.40
  24.8 0.1 reduce_sum.42
  24.9 0.1 reduce_sum.45
  25.0 56.6 %all-reduce.2 = (f32[16,70]{1,0:T(8,128)S(1)}, f32[16,70]{1,0:T(8,128)S(1)}) all-reduce(f32[16,70]{1,0:T(8,128)S(1)} %reduce_sum.42, f32[16,70]{1,0:T(8,128)S(1)} %reduce_sum.45), channel_id=1, replica_groups=mesh['grp'=2,'tm'=16] {'tm'}, use_global_device_ids=true, to_apply=%region_3.4 | all-reduce | flops 2240 | bytes 17920 | tf_op jit(solution)/shard_map/psum | solution.py:75
  81.6 0.6 broadcast_multiply_fusion.1
  82.2 0.1 slice_reduce_fusion.8
  82.3 1.3 fusion.36
  83.6 0.2 reshape.51
  83.8 0.2 reshape.54
  84.0 0.4 fusion.42
  84.3 0.4 fusion.44
  84.7 1.2 iota_compare_fusion
  86.0 0.3 copy.34
  86.3 0.3 copy.37
  86.6 0.6 copy.40
  87.2 0.1 select_reduce_fusion.1
  87.4 0.9 broadcast_select_fusion
  88.3 0.9 broadcast_select_fusion.1
  89.3 0.3 fusion.32
  89.5 2.4 %fusion.12 = (f32[4,64,1120]{2,1,0:T(8,128)S(1)}, f32[4,64,1120]{2,1,0:T(8,128)S(1)}) fusion(f32[6,64,1120]{2,1,0:T(8,128)S(1)} %get-tuple-element.34, f32[1120]{0:T(1024)S(1)} %get-tuple-element.20, f32[1120]{0:T(1024)S(1)} %get-tuple-element.21, f32[1120]{0:T(1024)S(1)} %get-tuple-element.14, f32[1120]{0:T(1024)S(1)} %get-tuple-element.15, ...), kind=kLoop, calls=%fused_computation.29 | loop fusion | flops 9748480 | bytes 12984320 | tf_op jit(solution)/shard_map/add | solution.py:60
  91.9 0.4 copy.22
  92.3 0.4 copy.26
  92.7 25.0 %all-reduce.6.cloned.1.call-done = (f32[16,70,70]{2,1,0:T(8,128)}, f32[16,70,70]{2,1,0:T(8,128)}) async-done(((f32[16,70,70]{2,1,0:T(8,128)}, f32[16,70,70]{2,1,0:T(8,128)}), (f32[16,70,70]{2,1,0:T(8,128)}, f32[16,70,70]{2,1,0:T(8,128)})) %all-reduce.6.cloned.1.call-update) | async-done | bytes 627216 | tf_op jit(solution)/shard_map/psum | solution.py:75
  117.7 2.3 %fusion.3 = f32[256,16,70]{0,2,1:T(8,128)S(1)} fusion(bf16[256,16,70]{0,2,1:T(8,128)(2,1)} %copy-done.5, f32[256,16]{0,1:T(8,128)S(1)} %bitcast.72, f32[16,70,70]{2,1,0:T(8,128)} %fusion.43, f32[16,70,70]{2,1,0:T(8,128)} %get-tuple-element.24, f32[16,70,70]{2,1,0:T(8,128)} %fusion.41), kind=kOutput, calls=%fused_computation.20 | convolution fusion | flops 241288320 | bytes 2677504 | tf_op jit(solution)/shard_map/rhd,hde->rhe/dot_general | solution.py:49
  119.9 1.2 reshape.55
  121.1 1.2 broadcast_multiply_fusion
  122.3 0.9 copy.27
  123.2 1.7 %fusion.2 = f32[256,16,70]{0,2,1:T(8,128)} fusion(f32[16,70,70]{2,1,0:T(8,128)S(1)} %copy-done.10, bf16[256,16,70]{0,2,1:T(8,128)(2,1)S(1)} %copy-done.4, f32[256,16]{0,1:T(8,128)S(1)} %bitcast.71), kind=kOutput, calls=%fused_computation.19 | convolution fusion | flops 241131520 | bytes 2050304 | tf_op jit(solution)/shard_map/rhd,hde->rhe/dot_general | solution.py:49
  124.9 2.5 %reshape.52 = f32[256,1120]{0,1:T(8,128)} reshape(f32[256,16,70]{0,2,1:T(8,128)} %fusion.2) | data formatting | bytes 2293760 | tf_op jit(solution)/shard_map/reshape | solution.py:51
  127.4 5.4 %fusion = f32[1,256,2240]{1,2,0:T(8,128)S(1)} fusion(bf16[1120,2240]{1,0:T(8,128)(2,1)} %param.12, f32[2240]{0:T(1024)S(1)} %get-tuple-element.11, f32[256,1120]{0,1:T(8,128)} %reshape.52, f32[256,1120]{0,1:T(8,128)S(1)} %copy.22), kind=kOutput, calls=%fused_computation.3 | convolution fusion | flops 1285652480 | bytes 9614080 | tf_op jit(solution)/shard_map/dot_general | solution.py:89
  132.9 2.5 %fusion.1 = f32[1,256,2240]{1,2,0:T(8,128)S(1)} fusion(bf16[1120,2240]{1,0:T(8,128)(2,1)S(1)} %bitcast.64, f32[2240]{0:T(1024)S(1)} %get-tuple-element.12, f32[256,1120]{0,1:T(8,128)S(1)} %copy-done, f32[256,1120]{0,1:T(8,128)S(1)} %copy.26), kind=kOutput, calls=%fused_computation.4 | convolution fusion | flops 1285652480 | bytes 9614080 | tf_op jit(solution)/shard_map/dot_general | solution.py:98
  135.4 2.4 %pad_maximum_fusion = f32[2,256,2240]{1,2,0:T(8,128)} fusion(f32[1,256,2240]{1,2,0:T(8,128)S(1)} %fusion.1, f32[1,256,2240]{1,2,0:T(8,128)S(1)} %fusion), kind=kLoop, calls=%fused_computation | loop fusion | flops 1146880 | bytes 9175040 | tf_op jit(solution)/shard_map/stack | solution.py:100
  (31 shorter events, 0.1 us)
Async XLA Ops:
  7.2 9.6 %copy-start.2 = (bf16[2,256,1120]{1,2,0:T(8,128)(2,1)S(1)}, bf16[2,256,1120]{1,2,0:T(8,128)(2,1)}, u32[]{:S(2)}) copy-start(bf16[2,256,1120]{1,2,0:T(8,128)(2,1)} %param.9) | copy-start | bytes 3440644
  7.2 110.5 %all-reduce.6.cloned.1.call-start = ((), (), s32[]{:S(2)}) async-start(), calls=%async_computation | async-start | bytes 2359296 | tf_op jit(solution)/shard_map/psum | solution.py:75
  9.3 78.0 %collective-permute-start.1 = (bf16[1,64,1120]{2,1,0:T(8,128)(2,1)}, bf16[1,64,1120]{2,1,0:T(8,128)(2,1)}, u32[]{:S(2)}, u32[]{:S(2)}) collective-permute-start(bf16[1,64,1120]{2,1,0:T(8,128)(2,1)} %copy.36), channel_id=1, source_target_pairs={{1,0},{2,1},{3,2},{4,3},{5,4},{6,5},{7,6},{8,7},{9,8},{10,9},{11,1... | collective-permute-start | bytes 430088 | tf_op jit(solution)/shard_map/ppermute | solution.py:25
  12.1 4.7 %copy-start.1 = (bf16[2,256,1120]{1,2,0:T(8,128)(2,1)S(1)}, bf16[2,256,1120]{1,2,0:T(8,128)(2,1)}, u32[]{:S(2)}) copy-start(bf16[2,256,1120]{1,2,0:T(8,128)(2,1)} %param.8) | copy-start | bytes 3440644
  12.1 76.2 %collective-permute-start = (bf16[1,64,1120]{2,1,0:T(8,128)(2,1)}, bf16[1,64,1120]{2,1,0:T(8,128)(2,1)}, u32[]{:S(2)}, u32[]{:S(2)}) collective-permute-start(bf16[1,64,1120]{2,1,0:T(8,128)(2,1)} %copy.35), channel_id=1, source_target_pairs={{0,1},{1,2},{2,3},{3,4},{4,5},{5,6},{6,7},{7,8},{8,9},{9,10},{10,1... | collective-permute-start | bytes 430088 | tf_op jit(solution)/shard_map/ppermute | solution.py:23
  23.6 0.7 copy-start.9
  23.6 58.6 %copy-start.7 = (f32[9,1120]{1,0:T(8,128)S(1)}, f32[9,1120]{1,0:T(8,128)}, u32[]{:S(2)}) copy-start(f32[9,1120]{1,0:T(8,128)} %param.13) | copy-start | bytes 120964
  83.8 0.9 copy-start.3
  83.9 2.0 %copy-start.5 = (bf16[256,16,70]{0,2,1:T(8,128)(2,1)}, bf16[256,16,70]{0,2,1:T(8,128)(2,1)S(1)}, u32[]{:S(2)}) copy-start(bf16[256,16,70]{0,2,1:T(8,128)(2,1)S(1)} %reshape.54) | copy-start | bytes 1720324
  86.0 1.2 copy-start.6
  92.3 25.4 %copy-start.8 = (f32[16,1,256]{2,0,1:T(8,128)S(1)}, f32[16,1,256]{2,0,1:T(8,128)}, u32[]{:S(2)}) copy-start(f32[16,1,256]{2,0,1:T(8,128)} %copy.40) | copy-start | bytes 49156
  121.1 2.1 %copy-start.4 = (bf16[256,16,70]{0,2,1:T(8,128)(2,1)S(1)}, bf16[256,16,70]{0,2,1:T(8,128)(2,1)}, u32[]{:S(2)}) copy-start(bf16[256,16,70]{0,2,1:T(8,128)(2,1)} %copy-done.3) | copy-start | bytes 1720324
  121.1 2.1 %copy-start.10 = (f32[16,70,70]{2,1,0:T(8,128)S(1)}, f32[16,70,70]{2,1,0:T(8,128)}, u32[]{:S(2)}) copy-start(f32[16,70,70]{2,1,0:T(8,128)} %get-tuple-element.24) | copy-start | bytes 940804
  124.9 7.9 %slice-start = ((s8[5160960]{0:T(1024)(128)(4,1)}), s8[966656]{0:T(1024)(128)(4,1)S(1)}, s32[]{:S(2)}) async-start(s8[5160960]{0:T(1024)(128)(4,1)} %bitcast.63), calls=%async_computation.1 | async-start | bytes 1933312
  127.4 5.4 %slice-start.1 = ((s8[5160960]{0:T(1024)(128)(4,1)}), s8[4194304]{0:T(1024)(128)(4,1)S(1)}, s32[]{:S(2)}) async-start(s8[5160960]{0:T(1024)(128)(4,1)} %bitcast.63), calls=%async_computation.2 | async-start | bytes 8388608
  127.4 5.4 %copy-start = (f32[256,1120]{0,1:T(8,128)S(1)}, f32[256,1120]{0,1:T(8,128)}, u32[]{:S(2)}) copy-start(f32[256,1120]{0,1:T(8,128)} %reshape.55) | copy-start | bytes 3440644
Sparse Core Ops, SparseCore 0:
  23.7 93.8 all-reduce.5
where the time goes:
time: 147 us; the launch traced here: 145 us
  blocking collectives  56.6 us (39%)
  waiting for transfers between devices  25 us (17%)
  matrix products  16 us (11%)
  local copies, waits for them, and re-layouts  15.6 us (11%)
  between operations  14.3 us (10%)
  other arithmetic  10.5 us (7%)
  starting transfers between devices  6.59 us (4%)
    psum x1, blocking collectives, local(): whole_state, whole_total = lax.psum((state_one, total_one), 'tm')  56.6 us
    psum x1, waiting for transfers between devices, local(): whole_state, whole_total = lax.psum((state_one, total_one), 'tm')  25 us
    dot_general x1, matrix products, local(): jnp.dot(mixed_one, out_weight, preferred_element_type=jnp.float32)  5.41 us
    ppermute x1, starting transfers between devices, extended(): lax.ppermute(tail, axis, [(i, (i + 1) % count) for i in range(ends)])  4.64 us
    dot_general x2, matrix products, spread(): numer = jnp.einsum('rhd,hde->rhe', query_grid, key_state, precision=EXACT)  3.98 us
    reshape x2, local copies, waits for them, and re-layouts, spread(): return (numer / denom[..., None]).reshape(query_grid.shape[0], NH * HD)  3.66 us
    unnamed x31, local copies, waits for them, and re-layouts  3.45 us
    dot_general x2, matrix products, key_value_state(): jnp.einsum('rhd,rhe->hde', key_grid, value_grid, preferred_element_type=j...  3.38 us
  transfers between devices with their start and end apart: 3, of which 1 were waited for; matrix products, arithmetic and copies ran while one was open for 14% of the time, Pallas kernels for 0%

commit v1 on v0

v1 whole, which is shorter than its diff:
```python
import functools

import jax
import jax.numpy as jnp
from jax import lax
from jax.experimental import pallas as pl
from jax.experimental.pallas import tpu as pltpu
from jax.sharding import PartitionSpec as P

NH = 16
HD = 70
COLS = 64
ROWS_DEV = 4

F32 = jnp.float32
BF16 = jnp.bfloat16
LANES = 128
HALF_HEADS = NH // 2
HALF = HALF_HEADS * HD
TOK = ROWS_DEV * COLS
FULL_TILES = HALF // LANES
TILE_BASE = [LANES * j for j in range(FULL_TILES)] + [HALF - LANES]
REST = HALF - LANES * FULL_TILES
TROWS = 72
FOLD = 40
PACKED = FULL_TILES * TROWS + FOLD
LIMIT = 48 << 20


def tiles_of(head):
    first, last = HD * head, HD * head + HD
    return [j for j in range(FULL_TILES + 1) if first < min(LANES * j + LANES, HALF) and last > LANES * j]


def lane_mask(shape, tile, head):
    chan = TILE_BASE[tile] + lax.broadcasted_iota(jnp.int32, shape, 1)
    low = max(HD * head, LANES * tile)
    return (chan >= low) & (chan < HD * head + HD)


def nt_dot(a, b):
    return lax.dot_general(a, b, (((1,), (1,)), ((), ())), preferred_element_type=F32)


def pack_states(keys, values, out_ref):
    acc = [jnp.zeros((TROWS, LANES), F32) for _ in TILE_BASE]
    rows = lax.broadcasted_iota(jnp.int32, (TROWS, LANES), 0)
    for head in range(HALF_HEADS):
        start = HD * head // 16 * 16
        stop = min(HALF, -(-(HD * head + HD) // 16) * 16)
        shift = HD * head - start
        for tile in tiles_of(head):
            base = TILE_BASE[tile]
            prod = nt_dot(values[start:stop], keys[base : base + LANES])
            part = jnp.concatenate([prod[shift : shift + HD], jnp.zeros((TROWS - HD, LANES), F32)], axis=0)
            acc[tile] = jnp.where(lane_mask((TROWS, LANES), tile, head), part, acc[tile])
    ones = jnp.ones((16, TOK), BF16)
    for tile, base in enumerate(TILE_BASE):
        total = nt_dot(ones, keys[base : base + LANES])[:1]
        acc[tile] = jnp.where(rows == HD, jnp.broadcast_to(total, (TROWS, LANES)), acc[tile])
    for tile in range(FULL_TILES):
        out_ref[tile * TROWS : (tile + 1) * TROWS] = acc[tile]
    last = acc[FULL_TILES]
    low = jnp.concatenate([last[FOLD:], jnp.zeros((2 * FOLD - TROWS, LANES), F32)], axis=0)
    lanes = lax.broadcasted_iota(jnp.int32, (FOLD, LANES), 1)
    out_ref[FULL_TILES * TROWS :] = jnp.where(lanes >= LANES - REST, last[:FOLD], pltpu.roll(low, LANES // 2, 1))


def unpack_tiles(packed):
    tiles = [packed[j * TROWS : (j + 1) * TROWS] for j in range(FULL_TILES)]
    fold = packed[FULL_TILES * TROWS :]
    tiles.append(jnp.concatenate([fold, pltpu.roll(fold, LANES // 2, 1)[: TROWS - FOLD]], axis=0))
    return tiles


def split3(x):
    one = x.astype(BF16)
    rest = x - one.astype(F32)
    two = rest.astype(BF16)
    three = (rest - two.astype(F32)).astype(BF16)
    return one, two, three


def state_kernel(core, key_ref, value_ref, out_ref):
    pack_states(key_ref[0], value_ref[0], out_ref.at[0])


def local_states(core, keys, values, picks):
    def pick(i, core):
        step, own = 0, 0
        for n, (s, o) in enumerate(picks):
            step = jnp.where(i == n, s, step)
            own = jnp.where(i == n, o, own)
        half = jnp.where(own == 1, core[0], 1 - core[0])
        return step, half, 0

    spec = pl.BlockSpec((1, HALF, TOK), pick)
    return pl.pallas_call(
        state_kernel,
        out_shape=jax.ShapeDtypeStruct((len(picks), PACKED, LANES), F32),
        grid_spec=pltpu.PrefetchScalarGridSpec(
            num_scalar_prefetch=1,
            grid=(len(picks),),
            in_specs=[spec, spec],
            out_specs=pl.BlockSpec((1, PACKED, LANES), lambda i, core: (i, 0, 0)),
        ),
        compiler_params=pltpu.CompilerParams(vmem_limit_bytes=LIMIT),
        cost_estimate=pl.CostEstimate(flops=10_000_000, bytes_accessed=600_000 * len(picks), transcendentals=0),
        name="local_states",
    )(core, keys, values)


def rim_kernel(core_ref, value_ref, near_ref, far_ref):
    lanes = lax.broadcasted_iota(jnp.int32, (HALF, LANES), 1)
    left = lanes < COLS
    first = core_ref[0] == 0
    top = value_ref[0, :HALF, :LANES].astype(F32)
    bottom = value_ref[0, HALF:, :LANES].astype(F32)
    head = jnp.where(left, top, pltpu.roll(bottom, COLS, 1))
    top = value_ref[0, :HALF, TOK - LANES :].astype(F32)
    bottom = value_ref[0, HALF:, TOK - LANES :].astype(F32)
    tail = jnp.where(left, pltpu.roll(top, COLS, 1), bottom)
    near_ref[...] = jnp.where(first, tail, head).astype(BF16)
    far_ref[...] = jnp.where(first, head, tail).astype(BF16)


def rims(core, values):
    shape = jax.ShapeDtypeStruct((HALF, LANES), BF16)
    return pl.pallas_call(
        rim_kernel,
        out_shape=(shape, shape),
        grid_spec=pltpu.PrefetchScalarGridSpec(
            num_scalar_prefetch=1,
            grid=(1,),
            in_specs=[pl.BlockSpec((1, 2 * HALF, TOK), lambda i, core: (0, 0, 0))],
            out_specs=[pl.BlockSpec((HALF, LANES), lambda i, core: (0, 0))] * 2,
        ),
        name="rims",
    )(core, values)


GROUP = 16


def conv_kernel(core_ref, value_ref, near_ref, far_ref, weight_ref, out_ref, taps):
    half = pl.program_id(0)
    taps[...] = weight_ref[...].T
    lanes = lax.broadcasted_iota(jnp.int32, (GROUP, LANES), 1)
    left = lanes < COLS
    inner_left = (lanes != 0) & (lanes != COLS)
    inner_right = (lanes != COLS - 1) & (lanes != LANES - 1)
    first = core_ref[0] == 0
    low_half = half == 0

    def turn(x):
        return pltpu.roll(x, COLS, 1)

    def group(i, carry):
        row = pl.multiple_of(i * GROUP, GROUP)
        near = near_ref[pl.ds(row, GROUP)].astype(F32)
        far = far_ref[pl.ds(row, GROUP)].astype(F32)
        above = jnp.where(first, far, near)
        below = jnp.where(first, near, far)
        rim = jnp.where(
            left, jnp.where(low_half, above, turn(above)), jnp.where(low_half, turn(below), below)
        )
        tap = taps[pl.ds(row, GROUP)]
        weights = []
        for k in range(9):
            w = jnp.broadcast_to(tap[:, k : k + 1], (GROUP, LANES))
            if k % 3 == 0:
                w = jnp.where(inner_left, w, 0.0)
            if k % 3 == 2:
                w = jnp.where(inner_right, w, 0.0)
            weights.append(w)
        for step in range(2):
            a = value_ref[step, pl.ds(row, GROUP), :LANES].astype(F32)
            b = value_ref[step, pl.ds(row, GROUP), LANES:].astype(F32)
            ta, tb = turn(a), turn(b)
            lines = [
                jnp.where(left, rim, ta),
                a,
                jnp.where(left, ta, tb),
                b,
                jnp.where(left, tb, rim),
            ]
            wide = [(pltpu.roll(x, 1, 1), x, pltpu.roll(x, LANES - 1, 1)) for x in lines]
            for part in range(2):
                total = None
                for r in range(3):
                    for c in range(3):
                        term = wide[2 * part + r][c] * weights[3 * r + c]
                        total = term if total is None else total + term
                out_ref[step, pl.ds(row, GROUP), part * LANES : (part + 1) * LANES] = total
        return carry

    lax.fori_loop(0, HALF // GROUP, group, 0)


def convolve(core, values, near, far, weights):
    return pl.pallas_call(
        conv_kernel,
        out_shape=jax.ShapeDtypeStruct((2, 2 * HALF, TOK), F32),
        grid_spec=pltpu.PrefetchScalarGridSpec(
            num_scalar_prefetch=1,
            grid=(2,),
            in_specs=[
                pl.BlockSpec((2, HALF, TOK), lambda i, core: (0, i, 0)),
                pl.BlockSpec((HALF, LANES), lambda i, core: (0, 0)),
                pl.BlockSpec((HALF, LANES), lambda i, core: (0, 0)),
                pl.BlockSpec((None, 9, HALF), lambda i, core: (i, 0, 0)),
            ],
            out_specs=pl.BlockSpec((2, HALF, TOK), lambda i, core: (0, i, 0)),
            scratch_shapes=[pltpu.VMEM((HALF, 9), F32)],
        ),
        compiler_params=pltpu.CompilerParams(vmem_limit_bytes=LIMIT),
        cost_estimate=pl.CostEstimate(flops=12_000_000, bytes_accessed=3_500_000, transcendentals=0),
        name="convolve",
    )(core, values, near, far, weights)


def mix_kernel(chunks, core_ref, step_ref, query_hbm, conv_hbm, weight_hbm, gate_ref,
               own_ref, other_ref, keep0, send0, keep1, send1, out_hbm,
               query, acc, weight, mixed, result, sem_in, sem_out):
    loads = [
        pltpu.make_async_copy(query_hbm, query, sem_in.at[0]),
        pltpu.make_async_copy(conv_hbm, acc, sem_in.at[1]),
        pltpu.make_async_copy(weight_hbm, weight, sem_in.at[2]),
    ]
    for load in loads:
        load.start()
    gate_rows = [gate_ref[pl.ds(step_ref[s], 1), :] for s in range(2)]
    gates = jnp.concatenate(gate_rows + [gate_rows[0]] * 6, axis=0).T
    waited = False
    for part, (whole_ref, zero_ref, one_ref) in enumerate(((own_ref, keep0, keep1), (other_ref, send0, send1))):
        half = core_ref[0] if part == 0 else 1 - core_ref[0]
        base = half * HALF
        whole = whole_ref[...]
        states = (whole, whole - zero_ref[0] + one_ref[0])
        for step in range(2):
            tiles = unpack_tiles(states[step])
            if not waited:
                loads[0].wait()
                loads[1].wait()
                waited = True
            rows8 = lax.broadcasted_iota(jnp.int32, (HALF_HEADS, LANES), 0)
            den = None
            for tile, packed in enumerate(tiles):
                owner = jnp.zeros((HALF_HEADS, LANES), jnp.bool_)
                for head in range(HALF_HEADS):
                    if tile in tiles_of(head):
                        owner = owner | (lane_mask((HALF_HEADS, LANES), tile, head) & (rows8 == head))
                row = jnp.where(owner, jnp.broadcast_to(packed[HD : HD + 1], (HALF_HEADS, LANES)), 0.0)
                q = query[step, pl.ds(pl.multiple_of(base + TILE_BASE[tile], 16), LANES)]
                left = jnp.concatenate([x.astype(F32) for x in split3(row)] + [jnp.zeros((HALF_HEADS, LANES), F32)], axis=0).astype(BF16)
                got = jnp.dot(left, q, preferred_element_type=F32)
                got = got[:8] + got[8:16] + got[16:24]
                den = got if den is None else den + got
            inverse = 1.0 / den
            for head in range(HALF_HEADS):
                first = HD * head // 8 * 8
                shift = HD * head - first
                count = -(-(shift + HD) // 8) * 8
                rows = lax.broadcasted_iota(jnp.int32, (TROWS, LANES), 0)
                total = None
                for tile in tiles_of(head):
                    block = jnp.where(lane_mask((TROWS, LANES), tile, head) & (rows < HD), tiles[tile], 0.0)
                    block = jnp.concatenate([block, jnp.zeros((80 - TROWS, LANES), F32)], axis=0)
                    if shift:
                        block = jnp.concatenate([block[80 - shift :], block[: 80 - shift]], axis=0)
                    left = jnp.concatenate(split3(block), axis=0)
                    q = query[step, pl.ds(pl.multiple_of(base + TILE_BASE[tile], 16), LANES)]
                    got = jnp.dot(left, q, preferred_element_type=F32)
                    got = got[:80] + got[80:160] + got[160:]
                    total = got if total is None else total + got
                spot = pl.ds(pl.multiple_of(base + first, 8), count)
                acc[step, spot] = acc[step, spot] + total[:count] * inverse[head : head + 1]
    for step in range(2):
        mixed[:, step * TOK : (step + 1) * TOK] = acc[step].astype(BF16)
    loads[2].wait()
    stores = []
    for n, (start, size) in enumerate(chunks):
        prod = lax.dot_general(
            weight[:, start : start + size], mixed[...], (((0,), (0,)), ((), ())), preferred_element_type=F32
        )
        for step in range(2):
            result[step, start : start + size] = (
                prod[:, step * TOK : (step + 1) * TOK] * gates[start : start + size, step : step + 1]
            )
            stores.append(
                pltpu.make_async_copy(
                    result.at[step, start : start + size], out_hbm.at[step, start : start + size], sem_out.at[n, step]
                )
            )
            stores[-1].start()
    for store in stores:
        store.wait()


def mix(core, timesteps, queries, conv, weight, gate_table, own, other, keep0, send0, keep1, send1):
    width = weight.shape[1]
    chunks = [(s, min(256, width - s)) for s in range(0, width, 256)]
    smem = pl.BlockSpec(memory_space=pltpu.SMEM)
    anyspace = pl.BlockSpec(memory_space=pl.ANY)
    vmem = pl.BlockSpec(memory_space=pltpu.VMEM)
    return pl.pallas_call(
        functools.partial(mix_kernel, chunks),
        out_shape=jax.ShapeDtypeStruct((2, width, TOK), F32),
        in_specs=[smem, smem, anyspace, anyspace, anyspace] + [vmem] * 7,
        out_specs=anyspace,
        scratch_shapes=[
            pltpu.VMEM((2, 2 * HALF, TOK), BF16),
            pltpu.VMEM((2, 2 * HALF, TOK), F32),
            pltpu.VMEM((2 * HALF, width), BF16),
            pltpu.VMEM((2 * HALF, 2 * TOK), BF16),
            pltpu.VMEM((2, width, TOK), F32),
            pltpu.SemaphoreType.DMA((3,)),
            pltpu.SemaphoreType.DMA((len(chunks), 2)),
        ],
        compiler_params=pltpu.CompilerParams(vmem_limit_bytes=LIMIT),
        cost_estimate=pl.CostEstimate(flops=3_000_000_000, bytes_accessed=14_000_000, transcendentals=0),
        name="mix",
    )(core, timesteps, queries, conv, weight, gate_table, own, other, keep0, send0, keep1, send1)


def fresh_kernel(scale, core_ref, own_ref, other_ref, state_ref, total_ref):
    first = core_ref[0] == 0
    own, other = own_ref[...], other_ref[...]
    halves = (jnp.where(first, own, other), jnp.where(first, other, own))
    lanes = lax.broadcasted_iota(jnp.int32, (TROWS, LANES), 1)
    for half, packed in enumerate(halves):
        tiles = unpack_tiles(packed * scale)
        for head in range(HALF_HEADS):
            block = None
            for tile in tiles_of(head):
                low = max(HD * head, LANES * tile)
                turn = (HD * head - TILE_BASE[tile]) % LANES
                moved = pltpu.roll(tiles[tile], (LANES - turn) % LANES, 1) if turn else tiles[tile]
                block = moved if block is None else jnp.where(lanes >= low - HD * head, moved, block)
            at = half * HALF_HEADS + head
            total_ref[at : at + 1, :] = block[HD : HD + 1, :HD]
            state_ref[:, at, :] = block.T[:HD, :HD]


def fresh(core, own, other, tokens):
    return pl.pallas_call(
        functools.partial(fresh_kernel, 1.0 / tokens),
        out_shape=(jax.ShapeDtypeStruct((HD, NH, HD), F32), jax.ShapeDtypeStruct((NH, HD), F32)),
        in_specs=[pl.BlockSpec(memory_space=pltpu.SMEM)] + [pl.BlockSpec(memory_space=pltpu.VMEM)] * 2,
        out_specs=(pl.BlockSpec(memory_space=pltpu.VMEM),) * 2,
        compiler_params=pltpu.CompilerParams(vmem_limit_bytes=LIMIT),
        name="fresh",
    )(core, own, other)


def local(queries, keys, values, timesteps, gate_table, out_weight, conv_weight):
    count = lax.axis_size("tm")
    tokens = queries.shape[1] * count
    core = (lax.axis_index("tm") % 2).astype(jnp.int32).reshape(1)
    queries, keys, values = (x.transpose(0, 2, 1) for x in (queries, keys, values))

    def swap(x, pick):
        return lax.ppermute(x, "tm", [(i, i ^ pick(i % 2)) for i in range(count)])

    def partner(x):
        return swap(x, lambda c: 1)

    bits = [1 << b for b in range(1, count.bit_length() - 1)]
    turned = bits[-1:] + bits[:-1]
    rounds = [lambda c, b=b, t=t: t if c else b for b, t in zip(bits, turned)]

    send0 = local_states(core, keys, values, ((0, 0),))
    got0 = partner(send0)
    near, far = rims(core, values)
    near = partner(near)
    rest = local_states(core, keys, values, ((0, 1), (1, 0), (1, 1)))
    keep0, send1, keep1 = rest[0:1], rest[1:2], rest[2:3]
    links = [p for i in range(1, count - 1, 2) for p in ((i, i + 1), (i + 1, i))]
    far = lax.ppermute(far, "tm", links)
    conv = convolve(core, values, near, far, conv_weight.reshape(9, 2, HALF).transpose(1, 0, 2))
    whole = keep0[0] + got0[0]
    second = keep1[0] + partner(send1)[0]
    for pick in rounds:
        whole = whole + swap(whole, pick)
        second = second + swap(second, pick)
    other = partner(whole)
    update = mix(core, timesteps, queries, conv, out_weight, gate_table, whole, other, keep0, send0, keep1, send1)
    fresh_state, fresh_total = fresh(core, second, partner(second), tokens)
    return update.transpose(0, 2, 1), fresh_state.transpose(1, 0, 2), fresh_total


def solution(mesh):
    placed = (
        P(None, ("grp", "tm"), None),
        P(None, ("grp", "tm"), None),
        P(None, ("grp", "tm"), None),
        P("grp"),
        P(),
        P(),
        P(),
    )
    return jax.shard_map(
        local,
        mesh=mesh,
        in_specs=placed,
        out_specs=(P(None, ("grp", "tm"), None), P("grp", None, None), P("grp", None)),
        check_vma=False,
    )
```

time: 147 us -> 67.3 us (0.46); the launches traced: 145 us -> 66.9 us
  blocking collectives: 56.6 us -> 0 us
  Pallas kernels: 0 us -> 28.7 us
  matrix products: 16 us -> 0 us
  between operations: 14.3 us -> 0.74 us
  local copies, waits for them, and re-layouts: 15.6 us -> 4.96 us
  other arithmetic: 10.5 us -> 0.18 us
  starting transfers between devices: 6.59 us -> 13.1 us
  waiting for transfers between devices: 25 us -> 19.3 us
    psum x1 -> x0, blocking collectives: 56.6 us -> none  [local(): whole_state, whole_total = lax.psum((state_one, total_one), 'tm')]
    pallas_call x0 -> x6, Pallas kernels: none -> 28.7 us  [the longest x1 13.8 us: convolve(): pl.pallas_call(conv_kernel, out_shape=jax.ShapeDtypeStruct((2, 2 * HALF,...]
    psum x1 -> x0, waiting for transfers between devices: 25 us -> none  [local(): whole_state, whole_total = lax.psum((state_one, total_one), 'tm')]
    ppermute x2 -> x12, waiting for transfers between devices: 0.01 us -> 19.3 us  [the longest x11 17.8 us: swap(): return lax.ppermute(x, 'tm', [(i, i ^ pick(i % 2)) for i in range(count)])]
    dot_general x8 -> x0, matrix products: 16 us -> none  [the longest x1 5.41 us: local(): jnp.dot(mixed_one, out_weight, preferred_element_type=jnp.float32)]
    ppermute x2 -> x12, starting transfers between devices: 6.56 us -> 13.1 us  [the longest x11 8.84 us: swap(): return lax.ppermute(x, 'tm', [(i, i ^ pick(i % 2)) for i in range(count)])]
    slice x6 -> x1, local copies, waits for them, and re-layouts: 4.24 us -> 0.01 us  [local(): keep0, send1, keep1 = (rest[0:1], rest[1:2], rest[2:3])]
    another operation x4 -> x0, local copies, waits for them, and re-layouts: 2.48 us -> none  [the longest x2 1.36 us: key_value_state(): key_grid = key_rows.reshape(-1, NH, HD)]
  transfers between devices with their start and end apart: 3 -> 12, of which waited for: 1 -> 9; matrix products, arithmetic and copies ran while one was open for 14% -> 4% of each run, Pallas kernels for 0% -> 28%
where the time goes in v1:
time: 67.3 us; the launch traced here: 66.9 us
  Pallas kernels  28.7 us (43%)
  waiting for transfers between devices  19.3 us (29%)
  starting transfers between devices  13.1 us (19%)
  local copies, waits for them, and re-layouts  4.96 us (7%)
  between operations  0.74 us (1%)
    ppermute x11, waiting for transfers between devices, swap(): return lax.ppermute(x, 'tm', [(i, i ^ pick(i % 2)) for i in range(count)])  17.8 us
    pallas_call x1, Pallas kernels, convolve(): pl.pallas_call(conv_kernel, out_shape=jax.ShapeDtypeStruct((2, 2 * HALF,...  13.8 us
    ppermute x11, starting transfers between devices, swap(): return lax.ppermute(x, 'tm', [(i, i ^ pick(i % 2)) for i in range(count)])  8.84 us
    pallas_call x1, Pallas kernels, mix(): pl.pallas_call(functools.partial(mix_kernel, chunks), out_shape=jax.Shape...  8.39 us
    ppermute x1, starting transfers between devices, local(): far = lax.ppermute(far, 'tm', links)  4.27 us
    unnamed x12, local copies, waits for them, and re-layouts  2.53 us
    reshape x2, local copies, waits for them, and re-layouts, local(): conv_weight.reshape(9, 2, HALF).transpose(1, 0, 2)  2.41 us
    pallas_call x1, Pallas kernels, fresh(): pl.pallas_call(functools.partial(fresh_kernel, 1.0 / tokens), out_shape=(...  2.35 us
  transfers between devices with their start and end apart: 12, of which 9 were waited for; matrix products, arithmetic and copies ran while one was open for 4% of the time, Pallas kernels for 28%

profile of v1, /device:TPU:1, one launch (start us, length us, event | category | flops | bytes accessed | tf_op | source)
XLA Modules:
  0.0 66.9 jit_solution(7146200704655024653)
XLA Ops:
  0.6 0.0 copy-start
  0.7 1.2 %copy-done = bf16[2,256,1120]{1,2,0:T(8,128)(2,1)S(1)} copy-done((bf16[2,256,1120]{1,2,0:T(8,128)(2,1)S(1)}, bf16[2,256,1120]{1,2,0:T(8,128)(2,1)}, u32[]{:S(2)}) %copy-start) | copy-done | bytes 1146904
  1.9 0.0 copy-start.2
  1.9 1.3 %copy-done.2 = bf16[2,256,1120]{1,2,0:T(8,128)(2,1)S(1)} copy-done((bf16[2,256,1120]{1,2,0:T(8,128)(2,1)S(1)}, bf16[2,256,1120]{1,2,0:T(8,128)(2,1)}, u32[]{:S(2)}) %copy-start.2) | copy-done | bytes 1146904
  3.2 1.6 %local_states.2 = f32[3,328,128]{2,1,0:T(8,128)S(1)} custom-call(s32[1]{0:T(128)} %bitcast.core_ref.core, bf16[2,1120,256]{2,1,0:T(8,128)(2,1)S(1)} %bitcast.17, bf16[2,1120,256]{2,1,0:T(8,128)(2,1)S(1)} %bitcast.14), custom_call_target="tpu_custom_call" | custom-call | flops 10000000 | bytes 1800000 | tf_op jit(solution)/shard_map/local_states/pallas_call | solution.py:98
  4.8 0.1 collective-permute-start.7
  4.9 0.5 local_states.3.send0
  5.4 0.5 collective-permute-start.2
  5.9 0.3 collective-permute-done.7
  6.3 0.7 %collective-permute-done.2 = f32[1,328,128]{2,1,0:T(8,128)S(1)} collective-permute-done((f32[1,328,128]{2,1,0:T(8,128)S(1)}, f32[1,328,128]{2,1,0:T(8,128)S(1)}, u32[]{:S(2)}, u32[]{:S(2)}) %collective-permute-start.2) | collective-permute-done | bytes 167968 | tf_op jit(solution)/shard_map/ppermute | solution.py:363
  7.0 0.0 copy-start.1
  7.0 3.7 %collective-permute-start.8 = (f32[328,128]{1,0:T(8,128)S(1)}, f32[328,128]{1,0:T(8,128)S(1)}, u32[]{:S(2)}, u32[]{:S(2)}) collective-permute-start(f32[328,128]{1,0:T(8,128)S(1)} %get-tuple-element.11), channel_id=1, source_target_pairs={{0,2},{1,9},{2,0},{3,11},{4,6},{5,13},{6,4},{7,15},{8,10},{9,1},{1... | collective-permute-start | bytes 503816 | tf_op jit(solution)/shard_map/ppermute | solution.py:363
  10.7 0.1 collective-permute-start.3
  10.8 6.4 %collective-permute-done.8 = f32[328,128]{1,0:T(8,128)S(1)} collective-permute-done((f32[328,128]{1,0:T(8,128)S(1)}, f32[328,128]{1,0:T(8,128)S(1)}, u32[]{:S(2)}, u32[]{:S(2)}) %collective-permute-start.8) | collective-permute-done | bytes 167968 | tf_op jit(solution)/shard_map/ppermute | solution.py:363
  17.2 1.3 %collective-permute-start.9 = (f32[328,128]{1,0:T(8,128)S(1)}, f32[328,128]{1,0:T(8,128)S(1)}, u32[]{:S(2)}, u32[]{:S(2)}) collective-permute-start(f32[328,128]{1,0:T(8,128)S(1)} %add.42), channel_id=1, source_target_pairs={{0,4},{1,3},{2,6},{3,1},{4,0},{5,7},{6,2},{7,5},{8,12},{9,11},{10,... | collective-permute-start | bytes 503816 | tf_op jit(solution)/shard_map/ppermute | solution.py:363
  18.5 0.5 collective-permute-done.3
  19.0 1.4 %collective-permute-start.4 = (f32[328,128]{1,0:T(8,128)S(1)}, f32[328,128]{1,0:T(8,128)S(1)}, u32[]{:S(2)}, u32[]{:S(2)}) collective-permute-start(f32[328,128]{1,0:T(8,128)S(1)} %add.37), channel_id=1, source_target_pairs={{0,4},{1,3},{2,6},{3,1},{4,0},{5,7},{6,2},{7,5},{8,12},{9,11},{10,... | collective-permute-start | bytes 503816 | tf_op jit(solution)/shard_map/ppermute | solution.py:363
  20.4 1.4 %collective-permute-done.9 = f32[328,128]{1,0:T(8,128)S(1)} collective-permute-done((f32[328,128]{1,0:T(8,128)S(1)}, f32[328,128]{1,0:T(8,128)S(1)}, u32[]{:S(2)}, u32[]{:S(2)}) %collective-permute-start.9) | collective-permute-done | bytes 167968 | tf_op jit(solution)/shard_map/ppermute | solution.py:363
  21.8 0.4 collective-permute-start.10
  22.2 1.1 %collective-permute-done.4 = f32[328,128]{1,0:T(8,128)S(1)} collective-permute-done((f32[328,128]{1,0:T(8,128)S(1)}, f32[328,128]{1,0:T(8,128)S(1)}, u32[]{:S(2)}, u32[]{:S(2)}) %collective-permute-start.4) | collective-permute-done | bytes 167968 | tf_op jit(solution)/shard_map/ppermute | solution.py:363
  23.3 0.7 %collective-permute-start.5 = (f32[328,128]{1,0:T(8,128)S(1)}, f32[328,128]{1,0:T(8,128)S(1)}, u32[]{:S(2)}, u32[]{:S(2)}) collective-permute-start(f32[328,128]{1,0:T(8,128)S(1)} %add.38), channel_id=1, source_target_pairs={{0,8},{1,5},{2,10},{3,7},{4,12},{5,1},{6,14},{7,3},{8,0},{9,13},{1... | collective-permute-start | bytes 503816 | tf_op jit(solution)/shard_map/ppermute | solution.py:363
  24.0 4.4 %collective-permute-done.10 = f32[328,128]{1,0:T(8,128)S(1)} collective-permute-done((f32[328,128]{1,0:T(8,128)S(1)}, f32[328,128]{1,0:T(8,128)S(1)}, u32[]{:S(2)}, u32[]{:S(2)}) %collective-permute-start.10) | collective-permute-done | bytes 167968 | tf_op jit(solution)/shard_map/ppermute | solution.py:363
  28.5 0.1 collective-permute-start.11
  28.6 3.0 %collective-permute-done.5 = f32[328,128]{1,0:T(8,128)S(1)} collective-permute-done((f32[328,128]{1,0:T(8,128)S(1)}, f32[328,128]{1,0:T(8,128)S(1)}, u32[]{:S(2)}, u32[]{:S(2)}) %collective-permute-start.5) | collective-permute-done | bytes 167968 | tf_op jit(solution)/shard_map/ppermute | solution.py:363
  31.5 0.5 collective-permute-start.6
  32.0 1.9 %rims.1 = (bf16[560,128]{1,0:T(8,128)(2,1)}, bf16[560,128]{1,0:T(8,128)(2,1)}) custom-call(s32[1]{0:T(128)} %bitcast.core_ref.core, bf16[2,1120,256]{2,1,0:T(8,128)(2,1)} %bitcast.13), custom_call_target="tpu_custom_call" | custom-call | tf_op jit(solution)/shard_map/rims/pallas_call | solution.py:129
  33.9 0.0 copy-start.3
  33.9 0.0 copy-start.4
  33.9 0.0 copy-start.5
  33.9 0.2 collective-permute-start
  34.1 4.3 %collective-permute-start.1 = (bf16[560,128]{1,0:T(8,128)(2,1)}, bf16[560,128]{1,0:T(8,128)(2,1)}, u32[]{:S(2)}, u32[]{:S(2)}) collective-permute-start(bf16[560,128]{1,0:T(8,128)(2,1)} %get-tuple-element.8), channel_id=1, source_target_pairs={{1,2},{2,1},{3,4},{4,3},{5,6},{6,5},{7,8},{8,7},{9,10},{10,9},{11,... | collective-permute-start | bytes 430088 | tf_op jit(solution)/shard_map/ppermute | solution.py:379
  38.4 1.6 %reshape.15 = f32[9,2,560]{2,1,0:T(2,128)} reshape(f32[9,1120]{1,0:T(8,128)} %param.13) | data formatting | bytes 80640 | tf_op jit(solution)/shard_map/reshape | solution.py:380
  40.0 0.8 %copy.12 = f32[9,2,560]{2,0,1:T(8,128)S(1)} copy(f32[9,2,560]{2,1,0:T(2,128)} %reshape.15) | data formatting | bytes 80640 | tf_op jit(solution)/shard_map/reshape | solution.py:380
  40.8 0.0 collective-permute-done.near_ref
  40.8 1.5 %collective-permute-done.1.far_ref = bf16[560,128]{1,0:T(8,128)(2,1)} collective-permute-done((bf16[560,128]{1,0:T(8,128)(2,1)}, bf16[560,128]{1,0:T(8,128)(2,1)}, u32[]{:S(2)}, u32[]{:S(2)}) %collective-permute-start.1) | collective-permute-done | bytes 143392 | tf_op jit(solution)/shard_map/ppermute | solution.py:379
  42.3 0.0 copy-done.1
  42.3 13.8 %convolve.1.conv_hbm = f32[2,1120,256]{2,1,0:T(8,128)S(1)} custom-call(s32[1]{0:T(128)} %bitcast.core_ref.core, bf16[2,1120,256]{2,1,0:T(8,128)(2,1)S(1)} %bitcast.16, bf16[560,128]{1,0:T(8,128)(2,1)} %collective-permute-done.near_ref, bf16[560,128]{1,0:T(8,128)(2,1)} %collective-permute-done.1.far_ref, f32[2,9,560]{2,1,0:T(8,128)S(1)} %bitcast.20), custom_call_target="tpu_custom_call" | custom-call | flops 12000000 | bytes 3500000 | tf_op jit(solution)/shard_map/convolve/pallas_call | solution.py:201
  56.1 0.0 collective-permute-done.11.other_ref
  56.1 2.3 %fresh.1 = (f32[70,16,70]{2,1,0:T(8,128)}, f32[16,70]{1,0:T(8,128)}) custom-call(s32[1]{0:T(128)} %bitcast.core_ref.core, f32[328,128]{1,0:T(8,128)S(1)} %add.44.own_ref, f32[328,128]{1,0:T(8,128)} %collective-permute-done.11.other_ref), custom_call_target="tpu_custom_call" | custom-call | tf_op jit(solution)/shard_map/fresh/pallas_call | solution.py:346
  58.5 0.0 collective-permute-done.6.other_ref
  58.5 0.0 copy-done.3
  58.5 0.0 copy-done.4
  58.5 0.0 copy-done.5
  58.5 8.4 %mix.1 = f32[2,2240,256]{2,1,0:T(8,128)} custom-call(s32[1]{0:T(128)} %bitcast.core_ref.core, s32[2]{0:T(128)S(1)} %copy-done.5, bf16[2,1120,256]{2,1,0:T(8,128)(2,1)S(1)} %bitcast.19, f32[2,1120,256]{2,1,0:T(8,128)S(1)} %convolve.1.conv_hbm, bf16[1120,2240]{1,0:T(8,128)(2,1)} %weight_hbm.1, f32[20,2240]{1,0:T(8,128)S(1)} %copy-done.4, ...), custom_call_target="tpu_custom_call" | custom-call | flops 3000000000 | bytes 14000000 | tf_op jit(solution)/shard_map/mix/pallas_call | solution.py:306
  (8 shorter events, 0.2 us)
Async XLA Ops:
  0.6 1.3 %copy-start = (bf16[2,256,1120]{1,2,0:T(8,128)(2,1)S(1)}, bf16[2,256,1120]{1,2,0:T(8,128)(2,1)}, u32[]{:S(2)}) copy-start(bf16[2,256,1120]{1,2,0:T(8,128)(2,1)} %param.9) | copy-start | bytes 3440644
  1.9 1.3 %copy-start.2 = (bf16[2,256,1120]{1,2,0:T(8,128)(2,1)S(1)}, bf16[2,256,1120]{1,2,0:T(8,128)(2,1)}, u32[]{:S(2)}) copy-start(bf16[2,256,1120]{1,2,0:T(8,128)(2,1)} %param.8) | copy-start | bytes 3440644
  4.8 1.5 %collective-permute-start.7 = (f32[1,328,128]{2,1,0:T(8,128)S(1)}, f32[1,328,128]{2,1,0:T(8,128)S(1)}, u32[]{:S(2)}, u32[]{:S(2)}) collective-permute-start(f32[1,328,128]{2,1,0:T(8,128)S(1)} %slice.14.send1), channel_id=1, source_target_pairs={{0,1},{1,0},{2,3},{3,2},{4,5},{5,4},{6,7},{7,6},{8,9},{9,8},{10,11... | collective-permute-start | bytes 503816 | tf_op jit(solution)/shard_map/ppermute | solution.py:363
  5.4 1.5 %collective-permute-start.2 = (f32[1,328,128]{2,1,0:T(8,128)S(1)}, f32[1,328,128]{2,1,0:T(8,128)S(1)}, u32[]{:S(2)}, u32[]{:S(2)}) collective-permute-start(f32[1,328,128]{2,1,0:T(8,128)S(1)} %local_states.3.send0), channel_id=1, source_target_pairs={{0,1},{1,0},{2,3},{3,2},{4,5},{5,4},{6,7},{7,6},{8,9},{9,8},{10,11... | collective-permute-start | bytes 503816 | tf_op jit(solution)/shard_map/ppermute | solution.py:363
  7.0 35.3 %copy-start.1 = (bf16[2,256,1120]{1,2,0:T(8,128)(2,1)S(1)}, bf16[2,256,1120]{1,2,0:T(8,128)(2,1)}, u32[]{:S(2)}) copy-start(bf16[2,256,1120]{1,2,0:T(8,128)(2,1)} %param.9) | copy-start | bytes 3440644
  7.0 10.2 %collective-permute-start.8 = (f32[328,128]{1,0:T(8,128)S(1)}, f32[328,128]{1,0:T(8,128)S(1)}, u32[]{:S(2)}, u32[]{:S(2)}) collective-permute-start(f32[328,128]{1,0:T(8,128)S(1)} %get-tuple-element.11), channel_id=1, source_target_pairs={{0,2},{1,9},{2,0},{3,11},{4,6},{5,13},{6,4},{7,15},{8,10},{9,1},{1... | collective-permute-start | bytes 503816 | tf_op jit(solution)/shard_map/ppermute | solution.py:363
  10.7 8.3 %collective-permute-start.3 = (f32[328,128]{1,0:T(8,128)S(1)}, f32[328,128]{1,0:T(8,128)S(1)}, u32[]{:S(2)}, u32[]{:S(2)}) collective-permute-start(f32[328,128]{1,0:T(8,128)S(1)} %get-tuple-element.12), channel_id=1, source_target_pairs={{0,2},{1,9},{2,0},{3,11},{4,6},{5,13},{6,4},{7,15},{8,10},{9,1},{1... | collective-permute-start | bytes 503816 | tf_op jit(solution)/shard_map/ppermute | solution.py:363
  17.2 4.6 %collective-permute-start.9 = (f32[328,128]{1,0:T(8,128)S(1)}, f32[328,128]{1,0:T(8,128)S(1)}, u32[]{:S(2)}, u32[]{:S(2)}) collective-permute-start(f32[328,128]{1,0:T(8,128)S(1)} %add.42), channel_id=1, source_target_pairs={{0,4},{1,3},{2,6},{3,1},{4,0},{5,7},{6,2},{7,5},{8,12},{9,11},{10,... | collective-permute-start | bytes 503816 | tf_op jit(solution)/shard_map/ppermute | solution.py:363
  19.0 4.3 %collective-permute-start.4 = (f32[328,128]{1,0:T(8,128)S(1)}, f32[328,128]{1,0:T(8,128)S(1)}, u32[]{:S(2)}, u32[]{:S(2)}) collective-permute-start(f32[328,128]{1,0:T(8,128)S(1)} %add.37), channel_id=1, source_target_pairs={{0,4},{1,3},{2,6},{3,1},{4,0},{5,7},{6,2},{7,5},{8,12},{9,11},{10,... | collective-permute-start | bytes 503816 | tf_op jit(solution)/shard_map/ppermute | solution.py:363
  21.8 6.6 %collective-permute-start.10 = (f32[328,128]{1,0:T(8,128)S(1)}, f32[328,128]{1,0:T(8,128)S(1)}, u32[]{:S(2)}, u32[]{:S(2)}) collective-permute-start(f32[328,128]{1,0:T(8,128)S(1)} %add.43), channel_id=1, source_target_pairs={{0,8},{1,5},{2,10},{3,7},{4,12},{5,1},{6,14},{7,3},{8,0},{9,13},{1... | collective-permute-start | bytes 503816 | tf_op jit(solution)/shard_map/ppermute | solution.py:363
  23.3 8.2 %collective-permute-start.5 = (f32[328,128]{1,0:T(8,128)S(1)}, f32[328,128]{1,0:T(8,128)S(1)}, u32[]{:S(2)}, u32[]{:S(2)}) collective-permute-start(f32[328,128]{1,0:T(8,128)S(1)} %add.38), channel_id=1, source_target_pairs={{0,8},{1,5},{2,10},{3,7},{4,12},{5,1},{6,14},{7,3},{8,0},{9,13},{1... | collective-permute-start | bytes 503816 | tf_op jit(solution)/shard_map/ppermute | solution.py:363
  28.5 27.7 %collective-permute-start.11 = (f32[328,128]{1,0:T(8,128)S(1)}, f32[328,128]{1,0:T(8,128)}, u32[]{:S(2)}, u32[]{:S(2)}) collective-permute-start(f32[328,128]{1,0:T(8,128)S(1)} %add.44.own_ref), channel_id=1, source_target_pairs={{0,1},{1,0},{2,3},{3,2},{4,5},{5,4},{6,7},{7,6},{8,9},{9,8},{10,11... | collective-permute-start | bytes 503816 | tf_op jit(solution)/shard_map/ppermute | solution.py:363
  31.5 27.0 %collective-permute-start.6 = (f32[328,128]{1,0:T(8,128)S(1)}, f32[328,128]{1,0:T(8,128)}, u32[]{:S(2)}, u32[]{:S(2)}) collective-permute-start(f32[328,128]{1,0:T(8,128)S(1)} %add.39.own_ref), channel_id=1, source_target_pairs={{0,1},{1,0},{2,3},{3,2},{4,5},{5,4},{6,7},{7,6},{8,9},{9,8},{10,11... | collective-permute-start | bytes 503816 | tf_op jit(solution)/shard_map/ppermute | solution.py:363
  33.9 24.6 %copy-start.3 = (bf16[2,256,1120]{1,2,0:T(8,128)(2,1)S(1)}, bf16[2,256,1120]{1,2,0:T(8,128)(2,1)}, u32[]{:S(2)}) copy-start(bf16[2,256,1120]{1,2,0:T(8,128)(2,1)} %param.7) | copy-start | bytes 3440644
  33.9 24.6 %copy-start.4 = (f32[20,2240]{1,0:T(8,128)S(1)}, f32[20,2240]{1,0:T(8,128)}, u32[]{:S(2)}) copy-start(f32[20,2240]{1,0:T(8,128)} %gate_ref.1) | copy-start | bytes 537604
  33.9 24.6 %copy-start.5 = (s32[2]{0:T(128)S(1)}, s32[2]{0:T(128)}, u32[]{:S(2)}) copy-start(s32[2]{0:T(128)} %step_ref.1) | copy-start | bytes 28
  33.9 6.9 %collective-permute-start = (bf16[560,128]{1,0:T(8,128)(2,1)}, bf16[560,128]{1,0:T(8,128)(2,1)}, u32[]{:S(2)}, u32[]{:S(2)}) collective-permute-start(bf16[560,128]{1,0:T(8,128)(2,1)} %get-tuple-element.7), channel_id=1, source_target_pairs={{0,1},{1,0},{2,3},{3,2},{4,5},{5,4},{6,7},{7,6},{8,9},{9,8},{10,11... | collective-permute-start | bytes 430088 | tf_op jit(solution)/shard_map/ppermute | solution.py:363
  34.1 8.2 %collective-permute-start.1 = (bf16[560,128]{1,0:T(8,128)(2,1)}, bf16[560,128]{1,0:T(8,128)(2,1)}, u32[]{:S(2)}, u32[]{:S(2)}) collective-permute-start(bf16[560,128]{1,0:T(8,128)(2,1)} %get-tuple-element.8), channel_id=1, source_target_pairs={{1,2},{2,1},{3,4},{4,3},{5,6},{6,5},{7,8},{8,7},{9,10},{10,9},{11,... | collective-permute-start | bytes 430088 | tf_op jit(solution)/shard_map/ppermute | solution.py:379

commit v2 on v1

v2 whole, which is shorter than its diff:
```python
import functools

import jax
import jax.numpy as jnp
from jax import lax
from jax.experimental.layout import Layout, with_layout_constraint
from jax.experimental import pallas as pl
from jax.experimental.pallas import tpu as pltpu
from jax.sharding import PartitionSpec as P


NH = 16
HD = 70
COLS = 64
ROWS_DEV = 4

F32 = jnp.float32
BF16 = jnp.bfloat16
LANES = 128
HALF_HEADS = NH // 2
HALF = HALF_HEADS * HD
TOK = ROWS_DEV * COLS
FULL_TILES = HALF // LANES
TILE_BASE = [LANES * j for j in range(FULL_TILES)] + [HALF - LANES]
REST = HALF - LANES * FULL_TILES
TROWS = 72
FOLD = 40
SLAB = 80
PACKED = FULL_TILES * TROWS + FOLD
LIMIT = 48 << 20


def tiles_of(head):
    first, last = HD * head, HD * head + HD
    return [j for j in range(FULL_TILES + 1) if first < min(LANES * j + LANES, HALF) and last > LANES * j]


def lane_mask(shape, tile, head):
    chan = TILE_BASE[tile] + lax.broadcasted_iota(jnp.int32, shape, 1)
    low = max(HD * head, LANES * tile)
    return (chan >= low) & (chan < HD * head + HD)


def nt_dot(a, b):
    return lax.dot_general(a, b, (((1,), (1,)), ((), ())), preferred_element_type=F32)


def pack_states(keys, values, out_ref):
    acc = [jnp.zeros((TROWS, LANES), F32) for _ in TILE_BASE]
    rows = lax.broadcasted_iota(jnp.int32, (TROWS, LANES), 0)
    for head in range(HALF_HEADS):
        start = HD * head // 16 * 16
        stop = min(HALF, -(-(HD * head + HD) // 16) * 16)
        shift = HD * head - start
        for tile in tiles_of(head):
            base = TILE_BASE[tile]
            prod = nt_dot(values[start:stop], keys[base : base + LANES])
            part = jnp.concatenate([prod[shift : shift + HD], jnp.zeros((TROWS - HD, LANES), F32)], axis=0)
            acc[tile] = jnp.where(lane_mask((TROWS, LANES), tile, head), part, acc[tile])
    ones = jnp.ones((16, TOK), BF16)
    for tile, base in enumerate(TILE_BASE):
        total = nt_dot(ones, keys[base : base + LANES])[:1]
        acc[tile] = jnp.where(rows == HD, jnp.broadcast_to(total, (TROWS, LANES)), acc[tile])
    for tile in range(FULL_TILES):
        out_ref[tile * TROWS : (tile + 1) * TROWS] = acc[tile]
    last = acc[FULL_TILES]
    low = jnp.concatenate([last[FOLD:], jnp.zeros((2 * FOLD - TROWS, LANES), F32)], axis=0)
    lanes = lax.broadcasted_iota(jnp.int32, (FOLD, LANES), 1)
    out_ref[FULL_TILES * TROWS :] = jnp.where(lanes >= LANES - REST, last[:FOLD], pltpu.roll(low, LANES // 2, 1))


def unpack_tiles(packed):
    tiles = [packed[j * TROWS : (j + 1) * TROWS] for j in range(FULL_TILES)]
    fold = packed[FULL_TILES * TROWS :]
    tiles.append(jnp.concatenate([fold, pltpu.roll(fold, LANES // 2, 1)[: TROWS - FOLD]], axis=0))
    return tiles


def split2(x):
    one = x.astype(BF16)
    return one, (x - one.astype(F32)).astype(BF16)


def state_kernel(picks, core_ref, key_hbm, value_hbm, *refs):
    out_refs, (key, value, sems) = refs[: len(picks)], refs[len(picks) :]
    loads = []
    for n, (step, own) in enumerate(picks):
        half = core_ref[0] if own else 1 - core_ref[0]
        spot = pl.ds(pl.multiple_of(half * HALF, HALF), HALF)
        loads.append(
            (
                pltpu.make_async_copy(key_hbm.at[step, spot], key.at[n], sems.at[n, 0]),
                pltpu.make_async_copy(value_hbm.at[step, spot], value.at[n], sems.at[n, 1]),
            )
        )
    for pair in loads:
        for load in pair:
            load.start()
    for n, pair in enumerate(loads):
        for load in pair:
            load.wait()
        pack_states(key[n], value[n], out_refs[n])


def local_states(core, keys, values, picks):
    n = len(picks)
    hbm = pl.BlockSpec(memory_space=pltpu.HBM)
    return pl.pallas_call(
        functools.partial(state_kernel, picks),
        out_shape=(jax.ShapeDtypeStruct((PACKED, LANES), F32),) * n,
        in_specs=[pl.BlockSpec(memory_space=pltpu.SMEM), hbm, hbm],
        out_specs=(pl.BlockSpec(memory_space=pltpu.VMEM),) * n,
        scratch_shapes=[
            pltpu.VMEM((n, HALF, TOK), BF16),
            pltpu.VMEM((n, HALF, TOK), BF16),
            pltpu.SemaphoreType.DMA((n, 2)),
        ],
        compiler_params=pltpu.CompilerParams(vmem_limit_bytes=16 << 20),
        cost_estimate=pl.CostEstimate(flops=300_000_000 * n, bytes_accessed=800_000 * n, transcendentals=0),
        name="local_states",
    )(core, keys, values)


def convolve(padded, conv_weight):
    widened = jnp.pad(padded.astype(F32), ((0, 0), (1, 1), (0, 0)))
    summed = jnp.zeros((ROWS_DEV, COLS, padded.shape[-1]), F32)
    for tap_row in range(3):
        for tap_col in range(3):
            summed = (
                summed
                + widened[tap_row : tap_row + ROWS_DEV, tap_col : tap_col + COLS]
                * conv_weight[3 * tap_row + tap_col]
            )
    return summed.reshape(TOK, padded.shape[-1])


def mix_kernel(chunks, core_ref, step_ref, query_hbm, conv0_hbm, conv1_hbm, weight_hbm, gate_ref,
               own_ref, other_ref, keep0, send0, keep1, send1, out_hbm,
               query, acc, weight, mixed, result, sem_in, sem_out):
    loads = [
        pltpu.make_async_copy(query_hbm, query, sem_in.at[0]),
        pltpu.make_async_copy(conv0_hbm, acc.at[0], sem_in.at[1]),
        pltpu.make_async_copy(conv1_hbm, acc.at[1], sem_in.at[2]),
        pltpu.make_async_copy(weight_hbm, weight, sem_in.at[3]),
    ]
    for load in loads:
        load.start()
    gate_rows = [gate_ref[pl.ds(step_ref[s], 1), :] for s in range(2)]
    gates = jnp.concatenate(gate_rows + [gate_rows[0]] * 6, axis=0).T
    waited = False
    for part, (whole_ref, zero_ref, one_ref) in enumerate(((own_ref, keep0, keep1), (other_ref, send0, send1))):
        half = core_ref[0] if part == 0 else 1 - core_ref[0]
        base = half * HALF
        whole = whole_ref[...]
        states = (whole, whole - zero_ref[...] + one_ref[...])
        for step in range(2):
            tiles = unpack_tiles(states[step])
            if not waited:
                for load in loads[:3]:
                    load.wait()
                waited = True
            rows8 = lax.broadcasted_iota(jnp.int32, (HALF_HEADS, LANES), 0)
            rows = lax.broadcasted_iota(jnp.int32, (TROWS, LANES), 0)
            den = None
            sums = [None] * HALF_HEADS
            for tile, packed in enumerate(tiles):
                heads = [h for h in range(HALF_HEADS) if tile in tiles_of(h)]
                blocks = []
                for head in heads:
                    shift = HD * head % 8
                    block = jnp.where(lane_mask((TROWS, LANES), tile, head) & (rows < HD), packed, 0.0)
                    block = jnp.concatenate([block, jnp.zeros((SLAB - TROWS, LANES), F32)], axis=0)
                    if shift:
                        block = jnp.concatenate([block[SLAB - shift :], block[: SLAB - shift]], axis=0)
                    blocks.append(block)
                owner = jnp.zeros((HALF_HEADS, LANES), jnp.int32)
                for head in heads:
                    owner = jnp.where(lane_mask((HALF_HEADS, LANES), tile, head) & (rows8 == head), 1, owner)
                row = jnp.where(owner == 1, jnp.broadcast_to(packed[HD : HD + 1], (HALF_HEADS, LANES)), 0.0)
                blocks += [row, jnp.zeros((HALF_HEADS, LANES), F32)]
                left = jnp.concatenate(split2(jnp.concatenate(blocks, axis=0)), axis=1)
                q = query[step, pl.ds(pl.multiple_of(base + TILE_BASE[tile], 16), LANES)]
                got = jnp.dot(left, jnp.concatenate([q, q], axis=0), preferred_element_type=F32)
                for n, head in enumerate(heads):
                    part_sum = got[n * SLAB : (n + 1) * SLAB]
                    sums[head] = part_sum if sums[head] is None else sums[head] + part_sum
                part_den = got[len(heads) * SLAB : len(heads) * SLAB + HALF_HEADS]
                den = part_den if den is None else den + part_den
            inverse = 1.0 / den
            for head in range(HALF_HEADS):
                first = HD * head // 8 * 8
                count = -(-(HD * head - first + HD) // 8) * 8
                spot = pl.ds(pl.multiple_of(base + first, 8), count)
                acc[step, spot] = acc[step, spot] + sums[head][:count] * inverse[head : head + 1]
    for step in range(2):
        mixed[:, step * TOK : (step + 1) * TOK] = acc[step].astype(BF16)
    loads[3].wait()
    stores = []
    for n, (start, size) in enumerate(chunks):
        prod = lax.dot_general(
            weight[:, start : start + size], mixed[...], (((0,), (0,)), ((), ())), preferred_element_type=F32
        )
        for step in range(2):
            result[step, start : start + size] = (
                prod[:, step * TOK : (step + 1) * TOK] * gates[start : start + size, step : step + 1]
            )
            stores.append(
                pltpu.make_async_copy(
                    result.at[step, start : start + size], out_hbm.at[step, start : start + size], sem_out.at[n, step]
                )
            )
            stores[-1].start()
    for store in stores:
        store.wait()


def mix(core, timesteps, queries, conv, weight, gate_table, own, other, keep0, send0, keep1, send1):
    width = weight.shape[1]
    chunks = [(s, min(256, width - s)) for s in range(0, width, 256)]
    smem = pl.BlockSpec(memory_space=pltpu.SMEM)
    anyspace = pl.BlockSpec(memory_space=pl.ANY)
    vmem = pl.BlockSpec(memory_space=pltpu.VMEM)
    return pl.pallas_call(
        functools.partial(mix_kernel, chunks),
        out_shape=jax.ShapeDtypeStruct((2, width, TOK), F32),
        in_specs=[smem, smem, anyspace, anyspace, anyspace, anyspace] + [vmem] * 7,
        out_specs=anyspace,
        scratch_shapes=[
            pltpu.VMEM((2, 2 * HALF, TOK), BF16),
            pltpu.VMEM((2, 2 * HALF, TOK), F32),
            pltpu.VMEM((2 * HALF, width), BF16),
            pltpu.VMEM((2 * HALF, 2 * TOK), BF16),
            pltpu.VMEM((2, width, TOK), F32),
            pltpu.SemaphoreType.DMA((4,)),
            pltpu.SemaphoreType.DMA((len(chunks), 2)),
        ],
        compiler_params=pltpu.CompilerParams(vmem_limit_bytes=LIMIT),
        cost_estimate=pl.CostEstimate(flops=3_000_000_000, bytes_accessed=14_000_000, transcendentals=0),
        name="mix",
    )(core, timesteps, queries, *conv, weight, gate_table, own, other, keep0, send0, keep1, send1)


def fresh_kernel(scale, core_ref, own_ref, other_ref, state_ref, total_ref):
    first = core_ref[0] == 0
    own, other = own_ref[...], other_ref[...]
    halves = (jnp.where(first, own, other), jnp.where(first, other, own))
    lanes = lax.broadcasted_iota(jnp.int32, (TROWS, LANES), 1)
    for half, packed in enumerate(halves):
        tiles = unpack_tiles(packed * scale)
        for head in range(HALF_HEADS):
            block = None
            for tile in tiles_of(head):
                low = max(HD * head, LANES * tile)
                turn = (HD * head - TILE_BASE[tile]) % LANES
                moved = pltpu.roll(tiles[tile], (LANES - turn) % LANES, 1) if turn else tiles[tile]
                block = moved if block is None else jnp.where(lanes >= low - HD * head, moved, block)
            at = half * HALF_HEADS + head
            total_ref[at : at + 1, :] = block[HD : HD + 1, :HD]
            state_ref[:, at, :] = block.T[:HD, :HD]


def fresh(core, own, other, tokens):
    return pl.pallas_call(
        functools.partial(fresh_kernel, 1.0 / tokens),
        out_shape=(jax.ShapeDtypeStruct((HD, NH, HD), F32), jax.ShapeDtypeStruct((NH, HD), F32)),
        in_specs=[pl.BlockSpec(memory_space=pltpu.SMEM)] + [pl.BlockSpec(memory_space=pltpu.VMEM)] * 2,
        out_specs=(pl.BlockSpec(memory_space=pltpu.VMEM),) * 2,
        compiler_params=pltpu.CompilerParams(vmem_limit_bytes=LIMIT),
        name="fresh",
    )(core, own, other)


def local(queries, keys, values, timesteps, gate_table, out_weight, conv_weight):
    count = lax.axis_size("tm")
    tokens = queries.shape[1] * count
    core = (lax.axis_index("tm") % 2).astype(jnp.int32).reshape(1)
    plain = with_layout_constraint(values, Layout((0, 1, 2)))
    grid = plain.reshape(2, ROWS_DEV, COLS, values.shape[-1])
    queries, keys, values = (
        pltpu.with_memory_space_constraint(x.transpose(0, 2, 1), pltpu.HBM) for x in (queries, keys, values)
    )

    def swap(x, pick):
        return lax.ppermute(x, "tm", [(i, i ^ pick(i % 2)) for i in range(count)])

    def partner(x):
        return swap(x, lambda c: 1)

    bits = [1 << b for b in range(1, count.bit_length() - 1)]
    turned = bits[-1:] + bits[:-1]
    rounds = [lambda c, b=b, t=t: t if c else b for b, t in zip(bits, turned)]

    first = core[0] == 0
    (send0,) = local_states(core, keys, values, ((0, 0),))
    (keep0,) = local_states(core, keys, values, ((0, 1),))
    send1, keep1 = local_states(core, keys, values, ((1, 0), (1, 1)))
    near = jnp.where(first, grid[0, -1], grid[0, 0])
    far = jnp.where(first, grid[0, 0], grid[0, -1])
    near = partner(near)
    links = [p for i in range(1, count - 1, 2) for p in ((i, i + 1), (i + 1, i))]
    far = lax.ppermute(far, "tm", links)
    above, below = jnp.where(first, far, near), jnp.where(first, near, far)
    conv = [
        convolve(jnp.concatenate([above[None], grid[s], below[None]], axis=0), conv_weight).T for s in range(2)
    ]
    got0 = partner(send0)
    got1 = partner(send1)
    whole, second = keep0 + got0, keep1 + got1
    for pick in rounds:
        got = swap(whole, pick)
        whole = whole + got
    for pick in rounds[1:] + rounds[:1]:
        got = swap(second, pick)
        second = second + got
    other = partner(whole)
    update = mix(core, timesteps, queries, conv, out_weight, gate_table, whole, other, keep0, send0, keep1, send1)
    other1 = partner(second)
    fresh_state, fresh_total = fresh(core, second, other1, tokens)
    return update.transpose(0, 2, 1), fresh_state.transpose(1, 0, 2), fresh_total


def solution(mesh):
    placed = (
        P(None, ("grp", "tm"), None),
        P(None, ("grp", "tm"), None),
        P(None, ("grp", "tm"), None),
        P("grp"),
        P(),
        P(),
        P(),
    )

    return jax.shard_map(
        local,
        mesh=mesh,
        in_specs=placed,
        out_specs=(P(None, ("grp", "tm"), None), P("grp", None, None), P("grp", None)),
        check_vma=False,
    )
```

time: 67.3 us -> 55.4 us (0.82)
  Pallas kernels: 28.7 us -> 16.1 us
  waiting for transfers between devices: 19.3 us -> 8.13 us
  starting transfers between devices: 13.1 us -> 22.8 us
  other arithmetic: 0.18 us -> 3.72 us
  local copies, waits for them, and re-layouts: 4.96 us -> 2.97 us
    pallas_call x4 -> x3, Pallas kernels: 17.9 us -> 5.55 us  [local_states(): pl.pallas_call(functools.partial(state_kernel, picks), out_shape=(jax.Sha...]
    ppermute x11, waiting for transfers between devices: 17.8 us -> 8.13 us  [swap(): return lax.ppermute(x, 'tm', [(i, i ^ pick(i % 2)) for i in range(count)])]
    ppermute x11, starting transfers between devices: 8.84 us -> 18.3 us  [swap(): return lax.ppermute(x, 'tm', [(i, i ^ pick(i % 2)) for i in range(count)])]
    add x7 -> x9, other arithmetic: 0.18 us -> 3.37 us  [the longest x1 3.18 us: convolve(): summed + widened[tap_row:tap_row + ROWS_DEV, tap_col:tap_col + COLS] * co...]
    unnamed x12 -> x13, local copies, waits for them, and re-layouts: 2.53 us -> 0.74 us
    ppermute x1, waiting for transfers between devices: 1.49 us -> 0.01 us  [local(): far = lax.ppermute(far, 'tm', links)]
  transfers between devices with their start and end apart: 12 -> 12, of which waited for: 9 -> 3; matrix products, arithmetic and copies ran while one was open for 4% -> 12% of each run, Pallas kernels for 28% -> 12%
where the time goes in v2:
time: 55.4 us; the launch traced here: 54.6 us
  starting transfers between devices  22.8 us (41%)
  Pallas kernels  16.1 us (29%)
  waiting for transfers between devices  8.13 us (15%)
  other arithmetic  3.72 us (7%)
  local copies, waits for them, and re-layouts  2.97 us (5%)
  between operations  0.85 us (2%)
    ppermute x11, starting transfers between devices, swap(): return lax.ppermute(x, 'tm', [(i, i ^ pick(i % 2)) for i in range(count)])  18.3 us
    pallas_call x1, Pallas kernels, mix(): pl.pallas_call(functools.partial(mix_kernel, chunks), out_shape=jax.Shape...  8.25 us
    ppermute x11, waiting for transfers between devices, swap(): return lax.ppermute(x, 'tm', [(i, i ^ pick(i % 2)) for i in range(count)])  8.13 us
    pallas_call x3, Pallas kernels, local_states(): pl.pallas_call(functools.partial(state_kernel, picks), out_shape=(jax.Sha...  5.55 us
    ppermute x1, starting transfers between devices, local(): far = lax.ppermute(far, 'tm', links)  4.52 us
    add x1, other arithmetic, convolve(): summed + widened[tap_row:tap_row + ROWS_DEV, tap_col:tap_col + COLS] * co...  3.18 us
    pallas_call x1, Pallas kernels, fresh(): pl.pallas_call(functools.partial(fresh_kernel, 1.0 / tokens), out_shape=(...  2.35 us
    reshape x2, local copies, waits for them, and re-layouts, convolve(): return summed.reshape(TOK, padded.shape[-1])  2.02 us
  transfers between devices with their start and end apart: 12, of which 3 were waited for; matrix products, arithmetic and copies ran while one was open for 12% of the time, Pallas kernels for 12%

profile of v2, /device:TPU:1, one launch (start us, length us, event | category | flops | bytes accessed | tf_op | source)
XLA Modules:
  0.0 54.6 jit_solution(279547478469471433)
XLA Ops:
  0.6 1.6 %local_states.4.send0 = f32[328,128]{1,0:T(8,128)S(1)} custom-call(s32[1]{0:T(128)} %bitcast.core_ref, bf16[2,1120,256]{2,1,0:T(8,128)(2,1)} %bitcast.26, bf16[2,1120,256]{2,1,0:T(8,128)(2,1)} %bitcast.23), custom_call_target="tpu_custom_call" | custom-call | flops 300000000 | bytes 800000 | tf_op jit(solution)/shard_map/local_states/pallas_call | solution.py:108
  2.3 0.0 copy-start.2
  2.3 0.1 collective-permute-start.2
  2.3 2.2 %local_states.5 = (f32[328,128]{1,0:T(8,128)S(1)}, f32[328,128]{1,0:T(8,128)S(1)}) custom-call(s32[1]{0:T(128)} %bitcast.core_ref, bf16[2,1120,256]{2,1,0:T(8,128)(2,1)} %bitcast.27, bf16[2,1120,256]{2,1,0:T(8,128)(2,1)} %bitcast.24), custom_call_target="tpu_custom_call" | custom-call | flops 600000000 | bytes 1600000 | tf_op jit(solution)/shard_map/local_states/pallas_call | solution.py:108
  4.6 0.5 collective-permute-start.7
  5.1 0.0 copy-done.2
  5.1 0.7 %copy.17 = bf16[2,256,1120]{2,1,0:T(8,128)(2,1)S(1)} copy(bf16[2,256,1120]{1,2,0:T(8,128)(2,1)S(1)} %copy-done.2) | data formatting | bytes 2293760 | tf_op args[2]
  5.8 0.0 copy-start.3
  5.8 4.5 %collective-permute-start = (bf16[64,1120]{1,0:T(8,128)(2,1)S(1)}, bf16[64,1120]{1,0:T(8,128)(2,1)S(1)}, u32[]{:S(2)}, u32[]{:S(2)}) collective-permute-start(bf16[64,1120]{1,0:T(8,128)(2,1)S(1)} %get-tuple-element.22), channel_id=1, source_target_pairs={{1,2},{2,1},{3,4},{4,3},{5,6},{6,5},{7,8},{8,7},{9,10},{10,9},{11,... | collective-permute-start | bytes 430088 | tf_op jit(solution)/shard_map/ppermute | solution.py:301
  10.4 0.0 copy-done.3
  10.4 0.1 collective-permute-start.1
  10.5 0.0 copy-start.4
  10.5 1.7 %local_states.3.keep0 = f32[328,128]{1,0:T(8,128)S(1)} custom-call(s32[1]{0:T(128)} %bitcast.core_ref, bf16[2,1120,256]{2,1,0:T(8,128)(2,1)} %bitcast.28, bf16[2,1120,256]{2,1,0:T(8,128)(2,1)} %bitcast.25), custom_call_target="tpu_custom_call" | custom-call | flops 300000000 | bytes 800000 | tf_op jit(solution)/shard_map/local_states/pallas_call | solution.py:108
  12.2 0.0 collective-permute-done.2
  12.2 2.4 %collective-permute-start.3 = (f32[328,128]{1,0:T(8,128)S(1)}, f32[328,128]{1,0:T(8,128)S(1)}, u32[]{:S(2)}, u32[]{:S(2)}) collective-permute-start(f32[328,128]{1,0:T(8,128)S(1)} %add.97), channel_id=1, source_target_pairs={{0,2},{1,9},{2,0},{3,11},{4,6},{5,13},{6,4},{7,15},{8,10},{9,1},{1... | collective-permute-start | bytes 503816 | tf_op jit(solution)/shard_map/ppermute | solution.py:284
  14.6 0.0 collective-permute-done.7
  14.6 0.0 copy-start.5
  14.6 1.3 %collective-permute-start.8 = (f32[328,128]{1,0:T(8,128)S(1)}, f32[328,128]{1,0:T(8,128)S(1)}, u32[]{:S(2)}, u32[]{:S(2)}) collective-permute-start(f32[328,128]{1,0:T(8,128)S(1)} %add.101), channel_id=1, source_target_pairs={{0,4},{1,3},{2,6},{3,1},{4,0},{5,7},{6,2},{7,5},{8,12},{9,11},{10,... | collective-permute-start | bytes 503816 | tf_op jit(solution)/shard_map/ppermute | solution.py:284
  15.9 0.0 copy-done.4
  15.9 0.1 fusion.30
  16.0 0.0 copy-done.5
  16.0 0.1 slice_reduce_fusion.8
  16.2 3.1 %collective-permute-done.3 = f32[328,128]{1,0:T(8,128)S(1)} collective-permute-done((f32[328,128]{1,0:T(8,128)S(1)}, f32[328,128]{1,0:T(8,128)S(1)}, u32[]{:S(2)}, u32[]{:S(2)}) %collective-permute-start.3) | collective-permute-done | bytes 167968 | tf_op jit(solution)/shard_map/ppermute | solution.py:284
  19.3 1.2 %collective-permute-start.4 = (f32[328,128]{1,0:T(8,128)S(1)}, f32[328,128]{1,0:T(8,128)S(1)}, u32[]{:S(2)}, u32[]{:S(2)}) collective-permute-start(f32[328,128]{1,0:T(8,128)S(1)} %add.98), channel_id=1, source_target_pairs={{0,4},{1,3},{2,6},{3,1},{4,0},{5,7},{6,2},{7,5},{8,12},{9,11},{10,... | collective-permute-start | bytes 503816 | tf_op jit(solution)/shard_map/ppermute | solution.py:284
  20.5 0.0 collective-permute-done.8
  20.6 0.4 collective-permute-start.9
  20.9 0.0 collective-permute-done
  20.9 0.0 collective-permute-done.1
  21.0 2.8 %collective-permute-done.4 = f32[328,128]{1,0:T(8,128)S(1)} collective-permute-done((f32[328,128]{1,0:T(8,128)S(1)}, f32[328,128]{1,0:T(8,128)S(1)}, u32[]{:S(2)}, u32[]{:S(2)}) %collective-permute-start.4) | collective-permute-done | bytes 167968 | tf_op jit(solution)/shard_map/ppermute | solution.py:284
  23.8 0.9 %collective-permute-start.5 = (f32[328,128]{1,0:T(8,128)S(1)}, f32[328,128]{1,0:T(8,128)S(1)}, u32[]{:S(2)}, u32[]{:S(2)}) collective-permute-start(f32[328,128]{1,0:T(8,128)S(1)} %add.99), channel_id=1, source_target_pairs={{0,8},{1,5},{2,10},{3,7},{4,12},{5,1},{6,14},{7,3},{8,0},{9,13},{1... | collective-permute-start | bytes 503816 | tf_op jit(solution)/shard_map/ppermute | solution.py:284
  24.6 2.2 %collective-permute-done.9 = f32[328,128]{1,0:T(8,128)S(1)} collective-permute-done((f32[328,128]{1,0:T(8,128)S(1)}, f32[328,128]{1,0:T(8,128)S(1)}, u32[]{:S(2)}, u32[]{:S(2)}) %collective-permute-start.9) | collective-permute-done | bytes 167968 | tf_op jit(solution)/shard_map/ppermute | solution.py:284
  26.9 1.9 %collective-permute-start.10 = (f32[328,128]{1,0:T(8,128)S(1)}, f32[328,128]{1,0:T(8,128)S(1)}, u32[]{:S(2)}, u32[]{:S(2)}) collective-permute-start(f32[328,128]{1,0:T(8,128)S(1)} %add.103), channel_id=1, source_target_pairs={{0,2},{1,9},{2,0},{3,11},{4,6},{5,13},{6,4},{7,15},{8,10},{9,1},{1... | collective-permute-start | bytes 503816 | tf_op jit(solution)/shard_map/ppermute | solution.py:284
  28.8 0.3 fusion.29
  29.1 0.0 collective-permute-done.5
  29.1 9.6 %collective-permute-start.6 = (f32[328,128]{1,0:T(8,128)S(1)}, f32[328,128]{1,0:T(8,128)}, u32[]{:S(2)}, u32[]{:S(2)}) collective-permute-start(f32[328,128]{1,0:T(8,128)S(1)} %add.100.own_ref), channel_id=1, source_target_pairs={{0,1},{1,0},{2,3},{3,2},{4,5},{5,4},{6,7},{7,6},{8,9},{9,8},{10,11... | collective-permute-start | bytes 503816 | tf_op jit(solution)/shard_map/ppermute | solution.py:284
  38.7 0.0 collective-permute-done.10
  38.7 0.1 collective-permute-start.11
  38.8 3.2 %fusion.22 = (f32[4,64,1120]{2,1,0:T(8,128)}, f32[4,64,1120]{2,1,0:T(8,128)S(1)}) fusion(f32[6,64,1120]{2,1,0:T(8,128)S(1)} %get-tuple-element.24, f32[1120]{0:T(1024)S(1)} %get-tuple-element.18, f32[1120]{0:T(1024)S(1)} %get-tuple-element.19, f32[1120]{0:T(1024)S(1)} %get-tuple-element.12, f32[1120]{0:T(1024)S(1)} %get-tuple-element.13, ...), kind=kLoop, calls=%fused_computation.34 | loop fusion | flops 9748480 | bytes 12984320 | tf_op jit(solution)/shard_map/add | solution.py:130
  42.0 0.4 copy.18
  42.3 0.0 copy-start
  42.3 0.0 copy-start.1
  42.4 1.7 %copy.19 = f32[256,1120]{0,1:T(8,128)S(1)} copy(f32[256,1120]{1,0:T(8,128)} %bitcast.30) | data formatting | bytes 2293760 | tf_op jit(solution)/shard_map/reshape | solution.py:134
  44.0 0.0 collective-permute-done.11.other_ref
  44.0 2.3 %fresh.1 = (f32[70,16,70]{2,1,0:T(8,128)}, f32[16,70]{1,0:T(8,128)}) custom-call(s32[1]{0:T(128)} %bitcast.core_ref, f32[328,128]{1,0:T(8,128)S(1)} %add.104.own_ref, f32[328,128]{1,0:T(8,128)} %collective-permute-done.11.other_ref), custom_call_target="tpu_custom_call" | custom-call | tf_op jit(solution)/shard_map/fresh/pallas_call | solution.py:263
  46.4 0.0 collective-permute-done.6.other_ref
  46.4 0.0 copy-done
  46.4 0.0 copy-done.1
  46.4 8.2 %mix.1 = f32[2,2240,256]{2,1,0:T(8,128)} custom-call(s32[1]{0:T(128)} %bitcast.core_ref, s32[2]{0:T(128)S(1)} %copy-done.1, bf16[2,1120,256]{2,1,0:T(8,128)(2,1)} %bitcast.35, f32[1120,256]{1,0:T(8,128)S(1)} %bitcast.21, f32[1120,256]{1,0:T(8,128)S(1)} %bitcast.22, bf16[1120,2240]{1,0:T(8,128)(2,1)} %weight_hbm.1, f32[20,2240]{1,0:T(8,128)S(1)} %copy-done, ...), custom_call_target="tpu_custom_call" | custom-call | flops 3000000000 | bytes 14000000 | tf_op jit(solution)/shard_map/mix/pallas_call | solution.py:223
  (10 shorter events, 0.3 us)
Async XLA Ops:
  2.3 2.8 %copy-start.2 = (bf16[2,256,1120]{1,2,0:T(8,128)(2,1)S(1)}, bf16[2,256,1120]{1,2,0:T(8,128)(2,1)}, u32[]{:S(2)}) copy-start(bf16[2,256,1120]{1,2,0:T(8,128)(2,1)} %param.9) | copy-start | bytes 3440644
  2.3 9.9 %collective-permute-start.2 = (f32[328,128]{1,0:T(8,128)S(1)}, f32[328,128]{1,0:T(8,128)S(1)}, u32[]{:S(2)}, u32[]{:S(2)}) collective-permute-start(f32[328,128]{1,0:T(8,128)S(1)} %local_states.4.send0), channel_id=1, source_target_pairs={{0,1},{1,0},{2,3},{3,2},{4,5},{5,4},{6,7},{7,6},{8,9},{9,8},{10,11... | collective-permute-start | bytes 503816 | tf_op jit(solution)/shard_map/ppermute | solution.py:284
  4.6 10.0 %collective-permute-start.7 = (f32[328,128]{1,0:T(8,128)S(1)}, f32[328,128]{1,0:T(8,128)S(1)}, u32[]{:S(2)}, u32[]{:S(2)}) collective-permute-start(f32[328,128]{1,0:T(8,128)S(1)} %get-tuple-element.8.send1), channel_id=1, source_target_pairs={{0,1},{1,0},{2,3},{3,2},{4,5},{5,4},{6,7},{7,6},{8,9},{9,8},{10,11... | collective-permute-start | bytes 503816 | tf_op jit(solution)/shard_map/ppermute | solution.py:284
  5.8 4.6 %copy-start.3 = (bf16[2,256,1120]{2,1,0:T(8,128)(2,1)}, bf16[2,256,1120]{2,1,0:T(8,128)(2,1)S(1)}, u32[]{:S(2)}) copy-start(bf16[2,256,1120]{2,1,0:T(8,128)(2,1)S(1)} %copy.17) | copy-start | bytes 3440644
  5.8 15.1 %collective-permute-start = (bf16[64,1120]{1,0:T(8,128)(2,1)S(1)}, bf16[64,1120]{1,0:T(8,128)(2,1)S(1)}, u32[]{:S(2)}, u32[]{:S(2)}) collective-permute-start(bf16[64,1120]{1,0:T(8,128)(2,1)S(1)} %get-tuple-element.22), channel_id=1, source_target_pairs={{1,2},{2,1},{3,4},{4,3},{5,6},{6,5},{7,8},{8,7},{9,10},{10,9},{11,... | collective-permute-start | bytes 430088 | tf_op jit(solution)/shard_map/ppermute | solution.py:301
  10.4 10.5 %collective-permute-start.1 = (bf16[64,1120]{1,0:T(8,128)(2,1)S(1)}, bf16[64,1120]{1,0:T(8,128)(2,1)S(1)}, u32[]{:S(2)}, u32[]{:S(2)}) collective-permute-start(bf16[64,1120]{1,0:T(8,128)(2,1)S(1)} %get-tuple-element.23), channel_id=1, source_target_pairs={{0,1},{1,0},{2,3},{3,2},{4,5},{5,4},{6,7},{7,6},{8,9},{9,8},{10,11... | collective-permute-start | bytes 430088 | tf_op jit(solution)/shard_map/ppermute | solution.py:284
  10.5 5.5 %copy-start.4 = (bf16[2,256,1120]{2,1,0:T(8,128)(2,1)S(1)}, bf16[2,256,1120]{2,1,0:T(8,128)(2,1)}, u32[]{:S(2)}) copy-start(bf16[2,256,1120]{2,1,0:T(8,128)(2,1)} %copy-done.3) | copy-start | bytes 3440644
  12.2 7.1 %collective-permute-start.3 = (f32[328,128]{1,0:T(8,128)S(1)}, f32[328,128]{1,0:T(8,128)S(1)}, u32[]{:S(2)}, u32[]{:S(2)}) collective-permute-start(f32[328,128]{1,0:T(8,128)S(1)} %add.97), channel_id=1, source_target_pairs={{0,2},{1,9},{2,0},{3,11},{4,6},{5,13},{6,4},{7,15},{8,10},{9,1},{1... | collective-permute-start | bytes 503816 | tf_op jit(solution)/shard_map/ppermute | solution.py:284
  14.6 1.4 %copy-start.5 = (f32[9,1120]{1,0:T(8,128)S(1)}, f32[9,1120]{1,0:T(8,128)}, u32[]{:S(2)}) copy-start(f32[9,1120]{1,0:T(8,128)} %param.13) | copy-start | bytes 120964
  14.6 5.9 %collective-permute-start.8 = (f32[328,128]{1,0:T(8,128)S(1)}, f32[328,128]{1,0:T(8,128)S(1)}, u32[]{:S(2)}, u32[]{:S(2)}) collective-permute-start(f32[328,128]{1,0:T(8,128)S(1)} %add.101), channel_id=1, source_target_pairs={{0,4},{1,3},{2,6},{3,1},{4,0},{5,7},{6,2},{7,5},{8,12},{9,11},{10,... | collective-permute-start | bytes 503816 | tf_op jit(solution)/shard_map/ppermute | solution.py:284
  19.3 4.4 %collective-permute-start.4 = (f32[328,128]{1,0:T(8,128)S(1)}, f32[328,128]{1,0:T(8,128)S(1)}, u32[]{:S(2)}, u32[]{:S(2)}) collective-permute-start(f32[328,128]{1,0:T(8,128)S(1)} %add.98), channel_id=1, source_target_pairs={{0,4},{1,3},{2,6},{3,1},{4,0},{5,7},{6,2},{7,5},{8,12},{9,11},{10,... | collective-permute-start | bytes 503816 | tf_op jit(solution)/shard_map/ppermute | solution.py:284
  20.6 6.3 %collective-permute-start.9 = (f32[328,128]{1,0:T(8,128)S(1)}, f32[328,128]{1,0:T(8,128)S(1)}, u32[]{:S(2)}, u32[]{:S(2)}) collective-permute-start(f32[328,128]{1,0:T(8,128)S(1)} %add.102), channel_id=1, source_target_pairs={{0,8},{1,5},{2,10},{3,7},{4,12},{5,1},{6,14},{7,3},{8,0},{9,13},{1... | collective-permute-start | bytes 503816 | tf_op jit(solution)/shard_map/ppermute | solution.py:284
  23.8 5.3 %collective-permute-start.5 = (f32[328,128]{1,0:T(8,128)S(1)}, f32[328,128]{1,0:T(8,128)S(1)}, u32[]{:S(2)}, u32[]{:S(2)}) collective-permute-start(f32[328,128]{1,0:T(8,128)S(1)} %add.99), channel_id=1, source_target_pairs={{0,8},{1,5},{2,10},{3,7},{4,12},{5,1},{6,14},{7,3},{8,0},{9,13},{1... | collective-permute-start | bytes 503816 | tf_op jit(solution)/shard_map/ppermute | solution.py:284
  26.9 11.8 %collective-permute-start.10 = (f32[328,128]{1,0:T(8,128)S(1)}, f32[328,128]{1,0:T(8,128)S(1)}, u32[]{:S(2)}, u32[]{:S(2)}) collective-permute-start(f32[328,128]{1,0:T(8,128)S(1)} %add.103), channel_id=1, source_target_pairs={{0,2},{1,9},{2,0},{3,11},{4,6},{5,13},{6,4},{7,15},{8,10},{9,1},{1... | collective-permute-start | bytes 503816 | tf_op jit(solution)/shard_map/ppermute | solution.py:284
  29.1 17.3 %collective-permute-start.6 = (f32[328,128]{1,0:T(8,128)S(1)}, f32[328,128]{1,0:T(8,128)}, u32[]{:S(2)}, u32[]{:S(2)}) collective-permute-start(f32[328,128]{1,0:T(8,128)S(1)} %add.100.own_ref), channel_id=1, source_target_pairs={{0,1},{1,0},{2,3},{3,2},{4,5},{5,4},{6,7},{7,6},{8,9},{9,8},{10,11... | collective-permute-start | bytes 503816 | tf_op jit(solution)/shard_map/ppermute | solution.py:284
  38.7 5.3 %collective-permute-start.11 = (f32[328,128]{1,0:T(8,128)S(1)}, f32[328,128]{1,0:T(8,128)}, u32[]{:S(2)}, u32[]{:S(2)}) collective-permute-start(f32[328,128]{1,0:T(8,128)S(1)} %add.104.own_ref), channel_id=1, source_target_pairs={{0,1},{1,0},{2,3},{3,2},{4,5},{5,4},{6,7},{7,6},{8,9},{9,8},{10,11... | collective-permute-start | bytes 503816 | tf_op jit(solution)/shard_map/ppermute | solution.py:284
  42.3 4.1 %copy-start = (f32[20,2240]{1,0:T(8,128)S(1)}, f32[20,2240]{1,0:T(8,128)}, u32[]{:S(2)}) copy-start(f32[20,2240]{1,0:T(8,128)} %gate_ref.1) | copy-start | bytes 537604
  42.3 4.1 %copy-start.1 = (s32[2]{0:T(128)S(1)}, s32[2]{0:T(128)}, u32[]{:S(2)}) copy-start(s32[2]{0:T(128)} %step_ref.1) | copy-start | bytes 28

commit v3 on v2

v3 whole, which is shorter than its diff:
```python
import functools

import jax
import jax.numpy as jnp
from jax import lax
from jax.experimental import pallas as pl
from jax.experimental.pallas import tpu as pltpu
from jax.sharding import PartitionSpec as P


NH = 16
HD = 70
COLS = 64
ROWS_DEV = 4

F32 = jnp.float32
BF16 = jnp.bfloat16
LANES = 128
HALF_HEADS = NH // 2
HALF = HALF_HEADS * HD
TOK = ROWS_DEV * COLS
FULL_TILES = HALF // LANES
TILE_BASE = [LANES * j for j in range(FULL_TILES)] + [HALF - LANES]
REST = HALF - LANES * FULL_TILES
TROWS = 72
FOLD = 40
SLAB = 80
PACKED = FULL_TILES * TROWS + FOLD
LIMIT = 24 << 20


def core_of():
    return lax.rem(lax.axis_index("tm"), 2)


def tiles_of(head):
    first, last = HD * head, HD * head + HD
    return [j for j in range(FULL_TILES + 1) if first < min(LANES * j + LANES, HALF) and last > LANES * j]


def lane_mask(shape, tile, head):
    chan = TILE_BASE[tile] + lax.broadcasted_iota(jnp.int32, shape, 1)
    low = max(HD * head, LANES * tile)
    return (chan >= low) & (chan < HD * head + HD)


def nt_dot(a, b):
    return lax.dot_general(a, b, (((1,), (1,)), ((), ())), preferred_element_type=F32)


def pack_states(keys, values, out_ref):
    acc = [jnp.zeros((TROWS, LANES), F32) for _ in TILE_BASE]
    rows = lax.broadcasted_iota(jnp.int32, (TROWS, LANES), 0)
    for head in range(HALF_HEADS):
        start = HD * head // 16 * 16
        stop = min(HALF, -(-(HD * head + HD) // 16) * 16)
        shift = HD * head - start
        for tile in tiles_of(head):
            base = TILE_BASE[tile]
            prod = nt_dot(values[start:stop], keys[base : base + LANES])
            part = jnp.concatenate([prod[shift : shift + HD], jnp.zeros((TROWS - HD, LANES), F32)], axis=0)
            acc[tile] = jnp.where(lane_mask((TROWS, LANES), tile, head), part, acc[tile])
    ones = jnp.ones((16, TOK), BF16)
    for tile, base in enumerate(TILE_BASE):
        total = nt_dot(ones, keys[base : base + LANES])[:1]
        acc[tile] = jnp.where(rows == HD, jnp.broadcast_to(total, (TROWS, LANES)), acc[tile])
    for tile in range(FULL_TILES):
        out_ref[tile * TROWS : (tile + 1) * TROWS] = acc[tile]
    last = acc[FULL_TILES]
    low = jnp.concatenate([last[FOLD:], jnp.zeros((2 * FOLD - TROWS, LANES), F32)], axis=0)
    lanes = lax.broadcasted_iota(jnp.int32, (FOLD, LANES), 1)
    out_ref[FULL_TILES * TROWS :] = jnp.where(lanes >= LANES - REST, last[:FOLD], pltpu.roll(low, LANES // 2, 1))


def unpack_tiles(packed):
    tiles = [packed[j * TROWS : (j + 1) * TROWS] for j in range(FULL_TILES)]
    fold = packed[FULL_TILES * TROWS :]
    tiles.append(jnp.concatenate([fold, pltpu.roll(fold, LANES // 2, 1)[: TROWS - FOLD]], axis=0))
    return tiles


def split2(x):
    one = x.astype(BF16)
    return one, (x - one.astype(F32)).astype(BF16)


def state_kernel(picks, key_hbm, value_hbm, *refs):
    out_refs, (key, value, sems) = refs[: len(picks)], refs[len(picks) :]
    loads = []
    for n, (step, own) in enumerate(picks):
        half = core_of() if own else 1 - core_of()
        spot = pl.ds(pl.multiple_of(half * HALF, HALF), HALF)
        loads.append(
            (
                pltpu.make_async_copy(key_hbm.at[step, spot], key.at[n], sems.at[n, 0]),
                pltpu.make_async_copy(value_hbm.at[step, spot], value.at[n], sems.at[n, 1]),
            )
        )
    for pair in loads:
        for load in pair:
            load.start()
    for n, pair in enumerate(loads):
        for load in pair:
            load.wait()
        pack_states(key[n], value[n], out_refs[n])


def held_kernel(picks, key_ref, value_ref, *out_refs):
    for (step, own), out_ref in zip(picks, out_refs):
        half = core_of() if own else 1 - core_of()
        spot = pl.ds(pl.multiple_of(half * HALF, HALF), HALF)
        pack_states(key_ref[step, spot], value_ref[step, spot], out_ref)


def held_states(keys, values, picks):
    n = len(picks)
    vmem = pl.BlockSpec(memory_space=pltpu.VMEM)
    return pl.pallas_call(
        functools.partial(held_kernel, picks),
        out_shape=(jax.ShapeDtypeStruct((PACKED, LANES), F32),) * n,
        in_specs=[vmem, vmem],
        out_specs=(vmem,) * n,
        compiler_params=pltpu.CompilerParams(vmem_limit_bytes=8 << 20),
        cost_estimate=pl.CostEstimate(flops=300_000_000 * n, bytes_accessed=800_000 * n, transcendentals=0),
        name="held_states",
    )(keys, values)


def local_states(keys, values, picks):
    n = len(picks)
    hbm = pl.BlockSpec(memory_space=pltpu.HBM)
    return pl.pallas_call(
        functools.partial(state_kernel, picks),
        out_shape=(jax.ShapeDtypeStruct((PACKED, LANES), F32),) * n,
        in_specs=[hbm, hbm],
        out_specs=(pl.BlockSpec(memory_space=pltpu.VMEM),) * n,
        scratch_shapes=[
            pltpu.VMEM((n, HALF, TOK), BF16),
            pltpu.VMEM((n, HALF, TOK), BF16),
            pltpu.SemaphoreType.DMA((n, 2)),
        ],
        compiler_params=pltpu.CompilerParams(vmem_limit_bytes=4 << 20),
        cost_estimate=pl.CostEstimate(flops=300_000_000 * n, bytes_accessed=800_000 * n, transcendentals=0),
        name="local_states",
    )(keys, values)


def plain_kernel(value_ref, plain_ref, near_ref, far_ref):
    first = core_of() == 0
    for step in range(2):
        plain_ref[step] = value_ref[step].T
    head, tail = plain_ref[0, :COLS], plain_ref[0, TOK - COLS :]
    near_ref[...] = jnp.where(first, tail, head)
    far_ref[...] = jnp.where(first, head, tail)


def plain_values(values):
    vmem = pl.BlockSpec(memory_space=pltpu.VMEM)
    width = values.shape[1]
    row = jax.ShapeDtypeStruct((COLS, width), BF16)
    return pl.pallas_call(
        plain_kernel,
        out_shape=(jax.ShapeDtypeStruct((2, TOK, width), BF16), row, row),
        in_specs=[vmem],
        out_specs=(vmem,) * 3,
        compiler_params=pltpu.CompilerParams(vmem_limit_bytes=8 << 20),
        cost_estimate=pl.CostEstimate(flops=1_000_000, bytes_accessed=2_400_000, transcendentals=0),
        name="plain_values",
    )(values)


def convolve(padded, conv_weight):
    widened = jnp.pad(padded.astype(F32), ((0, 0), (1, 1), (0, 0)))
    summed = jnp.zeros((ROWS_DEV, COLS, padded.shape[-1]), F32)
    for tap_row in range(3):
        for tap_col in range(3):
            summed = (
                summed
                + widened[tap_row : tap_row + ROWS_DEV, tap_col : tap_col + COLS]
                * conv_weight[3 * tap_row + tap_col]
            )
    return summed.reshape(TOK, padded.shape[-1])


def spread_kernel(own, query, whole_ref, zero_ref, one_ref, out_ref):
    half = core_of() if own else 1 - core_of()
    base = half * HALF
    whole = whole_ref[...]
    states = (whole, whole - zero_ref[...] + one_ref[...])
    rows8 = lax.broadcasted_iota(jnp.int32, (HALF_HEADS, LANES), 0)
    rows = lax.broadcasted_iota(jnp.int32, (TROWS, LANES), 0)
    for step in range(2):
        tiles = unpack_tiles(states[step])
        den = None
        sums = [None] * HALF_HEADS
        for tile, packed in enumerate(tiles):
            heads = [h for h in range(HALF_HEADS) if tile in tiles_of(h)]
            blocks = []
            for head in heads:
                shift = HD * head % 8
                block = jnp.where(lane_mask((TROWS, LANES), tile, head) & (rows < HD), packed, 0.0)
                block = jnp.concatenate([block, jnp.zeros((SLAB - TROWS, LANES), F32)], axis=0)
                if shift:
                    block = jnp.concatenate([block[SLAB - shift :], block[: SLAB - shift]], axis=0)
                blocks.append(block)
            owner = jnp.zeros((HALF_HEADS, LANES), jnp.int32)
            for head in heads:
                owner = jnp.where(lane_mask((HALF_HEADS, LANES), tile, head) & (rows8 == head), 1, owner)
            row = jnp.where(owner == 1, jnp.broadcast_to(packed[HD : HD + 1], (HALF_HEADS, LANES)), 0.0)
            blocks += [row, jnp.zeros((HALF_HEADS, LANES), F32)]
            left = jnp.concatenate(split2(jnp.concatenate(blocks, axis=0)), axis=1)
            q = query[step, pl.ds(pl.multiple_of(base + TILE_BASE[tile], 16), LANES)]
            got = jnp.dot(left, jnp.concatenate([q, q], axis=0), preferred_element_type=F32)
            for n, head in enumerate(heads):
                part_sum = got[n * SLAB : (n + 1) * SLAB]
                sums[head] = part_sum if sums[head] is None else sums[head] + part_sum
            part_den = got[len(heads) * SLAB : len(heads) * SLAB + HALF_HEADS]
            den = part_den if den is None else den + part_den
        inverse = 1.0 / den
        out_ref[step] = jnp.zeros((HALF, TOK), F32)
        for head in range(HALF_HEADS):
            first = HD * head // 8 * 8
            count = -(-(HD * head - first + HD) // 8) * 8
            spot = slice(first, first + count)
            out_ref[step, spot] = out_ref[step, spot] + sums[head][:count] * inverse[head : head + 1]


def spread(own, queries, whole, zero, one):
    vmem = pl.BlockSpec(memory_space=pltpu.VMEM)
    return pl.pallas_call(
        functools.partial(spread_kernel, own),
        out_shape=jax.ShapeDtypeStruct((2, HALF, TOK), F32),
        in_specs=[vmem] * 4,
        out_specs=vmem,
        compiler_params=pltpu.CompilerParams(vmem_limit_bytes=8 << 20),
        cost_estimate=pl.CostEstimate(flops=800_000_000, bytes_accessed=2_000_000, transcendentals=0),
        name="spread",
    )(queries, whole, zero, one)


def project_kernel(chunks, step_ref, conv0, conv1, weight_hbm, gate_ref, own_ref, other_ref, out_hbm,
                   weight, turned, mixed, result, sem_in, sem_out):
    load = pltpu.make_async_copy(weight_hbm, weight, sem_in)
    load.start()
    half = core_of()
    for step in range(2):
        turned[...] = (conv0, conv1)[step][...].T
        for at, part in ((half, own_ref), (1 - half, other_ref)):
            spot = pl.ds(pl.multiple_of(at * HALF, HALF), HALF)
            mixed[spot, step * TOK : (step + 1) * TOK] = (part[step] + turned[spot]).astype(BF16)
    gate_rows = [gate_ref[pl.ds(step_ref[s], 1), :] for s in range(2)]
    gates = jnp.concatenate(gate_rows + [gate_rows[0]] * 6, axis=0).T
    load.wait()
    stores = []
    for n, (start, size) in enumerate(chunks):
        prod = lax.dot_general(
            weight[:, start : start + size], mixed[...], (((0,), (0,)), ((), ())), preferred_element_type=F32
        )
        for step in range(2):
            result[step, start : start + size] = (
                prod[:, step * TOK : (step + 1) * TOK] * gates[start : start + size, step : step + 1]
            )
            stores.append(
                pltpu.make_async_copy(
                    result.at[step, start : start + size], out_hbm.at[step, start : start + size], sem_out.at[n, step]
                )
            )
            stores[-1].start()
    for store in stores:
        store.wait()


def project(timesteps, conv, weight, gate_table, own, other):
    width = weight.shape[1]
    chunks = [(s, min(256, width - s)) for s in range(0, width, 256)]
    vmem = pl.BlockSpec(memory_space=pltpu.VMEM)
    anyspace = pl.BlockSpec(memory_space=pl.ANY)
    return pl.pallas_call(
        functools.partial(project_kernel, chunks),
        out_shape=jax.ShapeDtypeStruct((2, width, TOK), F32),
        in_specs=[pl.BlockSpec(memory_space=pltpu.SMEM), vmem, vmem, anyspace, vmem, vmem, vmem],
        out_specs=anyspace,
        scratch_shapes=[
            pltpu.VMEM((2 * HALF, width), BF16),
            pltpu.VMEM((2 * HALF, TOK), F32),
            pltpu.VMEM((2 * HALF, 2 * TOK), BF16),
            pltpu.VMEM((2, width, TOK), F32),
            pltpu.SemaphoreType.DMA,
            pltpu.SemaphoreType.DMA((len(chunks), 2)),
        ],
        compiler_params=pltpu.CompilerParams(vmem_limit_bytes=LIMIT),
        cost_estimate=pl.CostEstimate(flops=3_000_000_000, bytes_accessed=14_000_000, transcendentals=0),
        name="project",
    )(timesteps, *conv, weight, gate_table, own, other)


def fresh_kernel(scale, own_ref, other_ref, state_ref, total_ref):
    first = core_of() == 0
    own, other = own_ref[...], other_ref[...]
    halves = (jnp.where(first, own, other), jnp.where(first, other, own))
    lanes = lax.broadcasted_iota(jnp.int32, (TROWS, LANES), 1)
    for half, packed in enumerate(halves):
        tiles = unpack_tiles(packed * scale)
        for head in range(HALF_HEADS):
            block = None
            for tile in tiles_of(head):
                low = max(HD * head, LANES * tile)
                turn = (HD * head - TILE_BASE[tile]) % LANES
                moved = pltpu.roll(tiles[tile], (LANES - turn) % LANES, 1) if turn else tiles[tile]
                block = moved if block is None else jnp.where(lanes >= low - HD * head, moved, block)
            at = half * HALF_HEADS + head
            total_ref[at : at + 1, :] = block[HD : HD + 1, :HD]
            state_ref[:, at, :] = block.T[:HD, :HD]


def fresh(own, other, tokens):
    return pl.pallas_call(
        functools.partial(fresh_kernel, 1.0 / tokens),
        out_shape=(jax.ShapeDtypeStruct((HD, NH, HD), F32), jax.ShapeDtypeStruct((NH, HD), F32)),
        in_specs=[pl.BlockSpec(memory_space=pltpu.VMEM)] * 2,
        out_specs=(pl.BlockSpec(memory_space=pltpu.VMEM),) * 2,
        compiler_params=pltpu.CompilerParams(vmem_limit_bytes=LIMIT),
        name="fresh",
    )(own, other)


def local(queries, keys, values, timesteps, gate_table, out_weight, conv_weight):
    count = lax.axis_size("tm")
    tokens = queries.shape[1] * count
    queries, keys, values = (x.transpose(0, 2, 1) for x in (queries, keys, values))
    far_keys, far_values = (pltpu.with_memory_space_constraint(x, pltpu.HBM) for x in (keys, values))

    def swap(x, pick):
        return lax.ppermute(x, "tm", [(i, i ^ pick(i % 2)) for i in range(count)])

    def partner(x):
        return swap(x, lambda c: 1)

    bits = [1 << b for b in range(1, count.bit_length() - 1)]
    turned = bits[-1:] + bits[:-1]
    rounds = [lambda c, b=b, t=t: t if c else b for b, t in zip(bits, turned)]

    first = core_of() == 0
    (send0,) = local_states(far_keys, far_values, ((0, 0),))
    (keep0,) = held_states(keys, values, ((0, 1),))
    send1, keep1 = held_states(keys, values, ((1, 0), (1, 1)))
    plain, near, far = plain_values(values)
    near = partner(near)
    links = [p for i in range(1, count - 1, 2) for p in ((i, i + 1), (i + 1, i))]
    far = lax.ppermute(far, "tm", links)
    above, below = jnp.where(first, far, near), jnp.where(first, near, far)
    grid = plain.reshape(2, ROWS_DEV, COLS, plain.shape[-1])
    conv0 = convolve(jnp.concatenate([above[None], grid[0], below[None]], axis=0), conv_weight)
    again, above, below, weights, conv0 = lax.optimization_barrier((grid[1], above, below, conv_weight, conv0))
    conv1 = convolve(jnp.concatenate([above[None], again, below[None]], axis=0), weights)
    conv = conv0, conv1
    got0 = partner(send0)
    got1 = partner(send1)
    whole, second = keep0 + got0, keep1 + got1
    for pick in rounds:
        got = swap(whole, pick)
        whole = whole + got
    for pick in rounds[1:] + rounds[:1]:
        got = swap(second, pick)
        second = second + got
    other = partner(whole)
    own = spread(True, queries, whole, keep0, keep1)
    rest = spread(False, queries, other, send0, send1)
    update = project(timesteps, conv, out_weight, gate_table, own, rest)
    other1 = partner(second)
    fresh_state, fresh_total = fresh(second, other1, tokens)
    return update.transpose(0, 2, 1), fresh_state.transpose(1, 0, 2), fresh_total


def solution(mesh):
    placed = (
        P(None, ("grp", "tm"), None),
        P(None, ("grp", "tm"), None),
        P(None, ("grp", "tm"), None),
        P("grp"),
        P(),
        P(),
        P(),
    )

    return jax.shard_map(
        local,
        mesh=mesh,
        in_specs=placed,
        out_specs=(P(None, ("grp", "tm"), None), P("grp", None, None), P("grp", None)),
        check_vma=False,
    )
```

time: 55.4 us -> 49.9 us (0.901)
  Pallas kernels: 16.1 us -> 12.7 us
  starting transfers between devices: 22.8 us -> 20.8 us
    pallas_call x3 -> x1, Pallas kernels: 5.55 us -> 1.76 us  [local_states(): pl.pallas_call(functools.partial(state_kernel, picks), out_shape=(jax.Sha...]
    ppermute x11, starting transfers between devices: 18.3 us -> 16.2 us  [swap(): return lax.ppermute(x, 'tm', [(i, i ^ pick(i % 2)) for i in range(count)])]
    reshape x2 -> x0, local copies, waits for them, and re-layouts: 2.02 us -> none  [convolve(): return summed.reshape(TOK, padded.shape[-1])]
    unnamed x13 -> x22, local copies, waits for them, and re-layouts: 0.74 us -> 2.17 us
    add x1 -> x2, other arithmetic: 3.18 us -> 1.78 us  [convolve(): summed + widened[tap_row:tap_row + ROWS_DEV, tap_col:tap_col + COLS] * co...]
    pallas_call x1 -> x6, Pallas kernels: 8.25 us -> 9.5 us  [the longest x1 6.59 us: project(): pl.pallas_call(functools.partial(project_kernel, chunks), out_shape=jax.S...]
    select_n x1, other arithmetic: 0.03 us -> 1.05 us  [local(): above, below = (jnp.where(first, far, near), jnp.where(first, near, far))]
    slice x1, local copies, waits for them, and re-layouts: 0.09 us -> 1.09 us  [local(): grid[0]]
  transfers between devices with their start and end apart: 12 -> 12, of which waited for: 3 -> 3; matrix products, arithmetic and copies ran while one was open for 12% -> 9% of each run, Pallas kernels for 12% -> 22%
where the time goes in v3:
time: 49.9 us; the launch traced here: 49.2 us
  starting transfers between devices  20.8 us (42%)
  Pallas kernels  12.7 us (25%)
  waiting for transfers between devices  8.03 us (16%)
  local copies, waits for them, and re-layouts  3.49 us (7%)
  other arithmetic  3.32 us (7%)
  between operations  0.89 us (2%)
    ppermute x11, starting transfers between devices, swap(): return lax.ppermute(x, 'tm', [(i, i ^ pick(i % 2)) for i in range(count)])  16.2 us
    ppermute x11, waiting for transfers between devices, swap(): return lax.ppermute(x, 'tm', [(i, i ^ pick(i % 2)) for i in range(count)])  8.03 us
    pallas_call x1, Pallas kernels, project(): pl.pallas_call(functools.partial(project_kernel, chunks), out_shape=jax.S...  6.59 us
    ppermute x1, starting transfers between devices, local(): far = lax.ppermute(far, 'tm', links)  4.52 us
    unnamed x22, local copies, waits for them, and re-layouts  2.17 us
    add x2, other arithmetic, convolve(): summed + widened[tap_row:tap_row + ROWS_DEV, tap_col:tap_col + COLS] * co...  1.78 us
    pallas_call x1, Pallas kernels, local_states(): pl.pallas_call(functools.partial(state_kernel, picks), out_shape=(jax.Sha...  1.76 us
    pallas_call x1, Pallas kernels, fresh(): pl.pallas_call(functools.partial(fresh_kernel, 1.0 / tokens), out_shape=(...  1.44 us
  transfers between devices with their start and end apart: 12, of which 3 were waited for; matrix products, arithmetic and copies ran while one was open for 9% of the time, Pallas kernels for 22%

profile of v3, /device:TPU:1, one launch (start us, length us, event | category | flops | bytes accessed | tf_op | source)
XLA Modules:
  0.0 49.2 jit_solution(15043033489031314146)
XLA Ops:
  0.6 0.0 copy-start
  0.6 1.2 %copy-done = bf16[2,256,1120]{1,2,0:T(8,128)(2,1)S(1)} copy-done((bf16[2,256,1120]{1,2,0:T(8,128)(2,1)S(1)}, bf16[2,256,1120]{1,2,0:T(8,128)(2,1)}, u32[]{:S(2)}) %copy-start) | copy-done | bytes 1146904
  1.9 0.4 plain_values.1
  2.3 0.1 collective-permute-start.1
  2.3 4.5 %collective-permute-start = (bf16[64,1120]{1,0:T(8,128)(2,1)S(1)}, bf16[64,1120]{1,0:T(8,128)(2,1)}, u32[]{:S(2)}, u32[]{:S(2)}) collective-permute-start(bf16[64,1120]{1,0:T(8,128)(2,1)S(1)} %get-tuple-element.16), channel_id=1, source_target_pairs={{1,2},{2,1},{3,4},{4,3},{5,6},{6,5},{7,8},{8,7},{9,10},{10,9},{11,... | collective-permute-start | bytes 430088 | tf_op jit(solution)/shard_map/ppermute | solution.py:350
  6.9 0.0 copy-start.1
  6.9 0.0 copy-start.2
  6.9 1.8 %local_states.1.zero_ref = f32[328,128]{1,0:T(8,128)S(1)} custom-call(bf16[2,1120,256]{2,1,0:T(8,128)(2,1)} %bitcast.17, bf16[2,1120,256]{2,1,0:T(8,128)(2,1)} %bitcast.13), custom_call_target="tpu_custom_call" | custom-call | flops 300000000 | bytes 800000 | tf_op jit(solution)/shard_map/local_states/pallas_call | solution.py:132
  8.7 0.1 collective-permute-start.2
  8.8 0.9 %held_states.3 = (f32[328,128]{1,0:T(8,128)S(1)}, f32[328,128]{1,0:T(8,128)S(1)}) custom-call(bf16[2,1120,256]{2,1,0:T(8,128)(2,1)S(1)} %bitcast.18, bf16[2,1120,256]{2,1,0:T(8,128)(2,1)S(1)} %bitcast.15), custom_call_target="tpu_custom_call" | custom-call | flops 600000000 | bytes 1600000 | tf_op jit(solution)/shard_map/held_states/pallas_call | solution.py:118
  9.6 0.5 collective-permute-start.7
  10.1 1.1 %fusion.28 = (bf16[1,256,1120]{2,1,0:T(8,128)(2,1)}, bf16[1,256,1120]{2,1,0:T(8,128)(2,1)}) fusion(bf16[2,256,1120]{2,1,0:T(8,128)(2,1)S(1)} %get-tuple-element.15), kind=kLoop, calls=%fused_computation.68 | loop fusion | bytes 2293760 | tf_op jit(solution)/shard_map/slice | solution.py:353
  11.2 0.5 %held_states.2.zero_ref = f32[328,128]{1,0:T(8,128)S(1)} custom-call(bf16[2,1120,256]{2,1,0:T(8,128)(2,1)S(1)} %bitcast.19, bf16[2,1120,256]{2,1,0:T(8,128)(2,1)S(1)} %bitcast.16), custom_call_target="tpu_custom_call" | custom-call | flops 300000000 | bytes 800000 | tf_op jit(solution)/shard_map/held_states/pallas_call | solution.py:118
  11.8 0.4 copy-done.8
  12.1 0.1 slice_reduce_fusion.17
  12.2 0.0 collective-permute-done.1
  12.2 0.0 collective-permute-done
  12.2 1.1 %broadcast_select_fusion = (bf16[64,1120]{1,0:T(8,128)(2,1)S(1)}, bf16[64,1120]{1,0:T(8,128)(2,1)S(1)}) fusion(bf16[64,1120]{1,0:T(8,128)(2,1)} %collective-permute-done.1, bf16[64,1120]{1,0:T(8,128)(2,1)} %collective-permute-done, pred[]{:T(512)S(6)} %eq.3), kind=kLoop, calls=%fused_computation.48 | loop fusion | flops 143360 | bytes 573441 | tf_op jit(solution)/shard_map/jit(_where)/select_n | solution.py:351
  13.3 0.0 collective-permute-done.2
  13.3 2.4 %collective-permute-start.3 = (f32[328,128]{1,0:T(8,128)S(1)}, f32[328,128]{1,0:T(8,128)S(1)}, u32[]{:S(2)}, u32[]{:S(2)}) collective-permute-start(f32[328,128]{1,0:T(8,128)S(1)} %add.92), channel_id=1, source_target_pairs={{0,2},{1,9},{2,0},{3,11},{4,6},{5,13},{6,4},{7,15},{8,10},{9,1},{1... | collective-permute-start | bytes 503816 | tf_op jit(solution)/shard_map/ppermute | solution.py:334
  15.7 0.1 maximum_convert_fusion
  15.9 0.0 collective-permute-done.7
  15.9 1.3 %collective-permute-start.8 = (f32[328,128]{1,0:T(8,128)S(1)}, f32[328,128]{1,0:T(8,128)S(1)}, u32[]{:S(2)}, u32[]{:S(2)}) collective-permute-start(f32[328,128]{1,0:T(8,128)S(1)} %add.96), channel_id=1, source_target_pairs={{0,4},{1,3},{2,6},{3,1},{4,0},{5,7},{6,2},{7,5},{8,12},{9,11},{10,... | collective-permute-start | bytes 503816 | tf_op jit(solution)/shard_map/ppermute | solution.py:334
  17.2 3.2 %collective-permute-done.3 = f32[328,128]{1,0:T(8,128)S(1)} collective-permute-done((f32[328,128]{1,0:T(8,128)S(1)}, f32[328,128]{1,0:T(8,128)S(1)}, u32[]{:S(2)}, u32[]{:S(2)}) %collective-permute-start.3) | collective-permute-done | bytes 167968 | tf_op jit(solution)/shard_map/ppermute | solution.py:334
  20.4 1.2 %collective-permute-start.4 = (f32[328,128]{1,0:T(8,128)S(1)}, f32[328,128]{1,0:T(8,128)S(1)}, u32[]{:S(2)}, u32[]{:S(2)}) collective-permute-start(f32[328,128]{1,0:T(8,128)S(1)} %add.93), channel_id=1, source_target_pairs={{0,4},{1,3},{2,6},{3,1},{4,0},{5,7},{6,2},{7,5},{8,12},{9,11},{10,... | collective-permute-start | bytes 503816 | tf_op jit(solution)/shard_map/ppermute | solution.py:334
  21.6 0.9 %fusion.8 = f32[4,64,1120]{2,1,0:T(8,128)S(1)} fusion(f32[6,64,1120]{2,1,0:T(8,128)S(1)} %maximum_convert_fusion, f32[1120]{0:T(1024)S(1)} %get-tuple-element.44, f32[1120]{0:T(1024)S(1)} %get-tuple-element.37, f32[1120]{0:T(1024)S(1)} %get-tuple-element.38, f32[1120]{0:T(1024)S(1)} %get-tuple-element.39, f32[1120]{0:T(1024)S(1)} %get-tuple-element.40, ...), kind=kLoop, calls=%fused_computation.20 | loop fusion | flops 4874240 | bytes 6529024 | tf_op jit(solution)/shard_map/add | solution.py:178
  22.5 0.0 collective-permute-done.8
  22.6 0.1 collective-permute-start.9
  22.7 2.1 %collective-permute-done.4 = f32[328,128]{1,0:T(8,128)S(1)} collective-permute-done((f32[328,128]{1,0:T(8,128)S(1)}, f32[328,128]{1,0:T(8,128)S(1)}, u32[]{:S(2)}, u32[]{:S(2)}) %collective-permute-start.4) | collective-permute-done | bytes 167968 | tf_op jit(solution)/shard_map/ppermute | solution.py:334
  24.7 1.0 %collective-permute-start.5 = (f32[328,128]{1,0:T(8,128)S(1)}, f32[328,128]{1,0:T(8,128)S(1)}, u32[]{:S(2)}, u32[]{:S(2)}) collective-permute-start(f32[328,128]{1,0:T(8,128)S(1)} %add.94), channel_id=1, source_target_pairs={{0,8},{1,5},{2,10},{3,7},{4,12},{5,1},{6,14},{7,3},{8,0},{9,13},{1... | collective-permute-start | bytes 503816 | tf_op jit(solution)/shard_map/ppermute | solution.py:334
  25.7 0.1 maximum_convert_fusion.1
  25.9 0.1 slice_reduce_fusion.8
  26.0 2.7 %collective-permute-done.9 = f32[328,128]{1,0:T(8,128)S(1)} collective-permute-done((f32[328,128]{1,0:T(8,128)S(1)}, f32[328,128]{1,0:T(8,128)S(1)}, u32[]{:S(2)}, u32[]{:S(2)}) %collective-permute-start.9) | collective-permute-done | bytes 167968 | tf_op jit(solution)/shard_map/ppermute | solution.py:334
  28.8 2.0 %collective-permute-start.10 = (f32[328,128]{1,0:T(8,128)S(1)}, f32[328,128]{1,0:T(8,128)S(1)}, u32[]{:S(2)}, u32[]{:S(2)}) collective-permute-start(f32[328,128]{1,0:T(8,128)S(1)} %add.98), channel_id=1, source_target_pairs={{0,2},{1,9},{2,0},{3,11},{4,6},{5,13},{6,4},{7,15},{8,10},{9,1},{1... | collective-permute-start | bytes 503816 | tf_op jit(solution)/shard_map/ppermute | solution.py:334
  30.8 7.6 %collective-permute-start.6 = (f32[328,128]{1,0:T(8,128)S(1)}, f32[328,128]{1,0:T(8,128)S(1)}, u32[]{:S(2)}, u32[]{:S(2)}) collective-permute-start(f32[328,128]{1,0:T(8,128)S(1)} %add.95.whole_ref), channel_id=1, source_target_pairs={{0,1},{1,0},{2,3},{3,2},{4,5},{5,4},{6,7},{7,6},{8,9},{9,8},{10,11... | collective-permute-start | bytes 503816 | tf_op jit(solution)/shard_map/ppermute | solution.py:334
  38.4 0.9 %fusion.22 = f32[4,64,1120]{2,1,0:T(8,128)S(1)} fusion(f32[6,64,1120]{2,1,0:T(8,128)S(1)} %maximum_convert_fusion.1, f32[1120]{0:T(1024)S(1)} %get-tuple-element.28, f32[1120]{0:T(1024)S(1)} %get-tuple-element.29, f32[1120]{0:T(1024)S(1)} %get-tuple-element.30, f32[1120]{0:T(1024)S(1)} %get-tuple-element.31, f32[1120]{0:T(1024)S(1)} %get-tuple-element.32, ...), kind=kLoop, calls=%fused_computation.34 | loop fusion | flops 4874240 | bytes 6529024 | tf_op jit(solution)/shard_map/add | solution.py:178
  39.3 0.0 collective-permute-done.10
  39.3 0.1 collective-permute-start.11
  39.4 0.2 copy-done.5
  39.6 0.6 %spread.2.own_ref = f32[2,560,256]{2,1,0:T(8,128)S(1)} custom-call(bf16[2,1120,256]{2,1,0:T(8,128)(2,1)S(1)} %bitcast.24, f32[328,128]{1,0:T(8,128)S(1)} %add.95.whole_ref, f32[328,128]{1,0:T(8,128)S(1)} %held_states.2.zero_ref, f32[328,128]{1,0:T(8,128)S(1)} %get-tuple-element.23.one_ref), custom_call_target="tpu_custom_call" | custom-call | flops 800000000 | bytes 2000000 | tf_op jit(solution)/shard_map/spread/pallas_call | solution.py:230
  40.2 0.0 copy-start.3
  40.2 0.0 copy-start.4
  40.2 0.0 collective-permute-done.6.whole_ref
  40.2 0.6 %spread.3.other_ref = f32[2,560,256]{2,1,0:T(8,128)S(1)} custom-call(bf16[2,1120,256]{2,1,0:T(8,128)(2,1)S(1)} %bitcast.25, f32[328,128]{1,0:T(8,128)S(1)} %collective-permute-done.6.whole_ref, f32[328,128]{1,0:T(8,128)S(1)} %local_states.1.zero_ref, f32[328,128]{1,0:T(8,128)S(1)} %get-tuple-element.24.one_ref), custom_call_target="tpu_custom_call" | custom-call | flops 800000000 | bytes 2000000 | tf_op jit(solution)/shard_map/spread/pallas_call | solution.py:230
  40.8 0.3 copy-done.3
  41.1 6.6 %project.1 = f32[2,2240,256]{2,1,0:T(8,128)} custom-call(s32[2]{0:T(128)S(1)} %copy-done.4, f32[256,1120]{1,0:T(8,128)S(1)} %bitcast.22, f32[256,1120]{1,0:T(8,128)S(1)} %bitcast.23, bf16[1120,2240]{1,0:T(8,128)(2,1)S(1)} %bitcast.21, f32[20,2240]{1,0:T(8,128)S(1)} %copy-done.3, f32[2,560,256]{2,1,0:T(8,128)S(1)} %spread.2.own_ref, ...), custom_call_target="tpu_custom_call" | custom-call | flops 3000000000 | bytes 14000000 | tf_op jit(solution)/shard_map/project/pallas_call | solution.py:278
  47.7 0.0 collective-permute-done.11.other_ref
  47.8 1.4 %fresh.1 = (f32[70,16,70]{2,1,0:T(8,128)}, f32[16,70]{1,0:T(8,128)}) custom-call(f32[328,128]{1,0:T(8,128)S(1)} %add.99.own_ref, f32[328,128]{1,0:T(8,128)S(1)} %collective-permute-done.11.other_ref), custom_call_target="tpu_custom_call" | custom-call | tf_op jit(solution)/shard_map/fresh/pallas_call | solution.py:317
  (23 shorter events, 0.2 us)
Async XLA Ops:
  0.6 1.3 %copy-start = (bf16[2,256,1120]{1,2,0:T(8,128)(2,1)S(1)}, bf16[2,256,1120]{1,2,0:T(8,128)(2,1)}, u32[]{:S(2)}) copy-start(bf16[2,256,1120]{1,2,0:T(8,128)(2,1)} %param.9) | copy-start | bytes 3440644
  2.3 10.0 %collective-permute-start.1 = (bf16[64,1120]{1,0:T(8,128)(2,1)S(1)}, bf16[64,1120]{1,0:T(8,128)(2,1)}, u32[]{:S(2)}, u32[]{:S(2)}) collective-permute-start(bf16[64,1120]{1,0:T(8,128)(2,1)S(1)} %get-tuple-element.17), channel_id=1, source_target_pairs={{0,1},{1,0},{2,3},{3,2},{4,5},{5,4},{6,7},{7,6},{8,9},{9,8},{10,11... | collective-permute-start | bytes 430088 | tf_op jit(solution)/shard_map/ppermute | solution.py:334
  2.3 9.9 %collective-permute-start = (bf16[64,1120]{1,0:T(8,128)(2,1)S(1)}, bf16[64,1120]{1,0:T(8,128)(2,1)}, u32[]{:S(2)}, u32[]{:S(2)}) collective-permute-start(bf16[64,1120]{1,0:T(8,128)(2,1)S(1)} %get-tuple-element.16), channel_id=1, source_target_pairs={{1,2},{2,1},{3,4},{4,3},{5,6},{6,5},{7,8},{8,7},{9,10},{10,9},{11,... | collective-permute-start | bytes 430088 | tf_op jit(solution)/shard_map/ppermute | solution.py:350
  6.9 1.9 %copy-start.1 = (bf16[2,256,1120]{1,2,0:T(8,128)(2,1)S(1)}, bf16[2,256,1120]{1,2,0:T(8,128)(2,1)}, u32[]{:S(2)}) copy-start(bf16[2,256,1120]{1,2,0:T(8,128)(2,1)} %param.9) | copy-start | bytes 3440644
  6.9 1.9 %copy-start.2 = (bf16[2,256,1120]{1,2,0:T(8,128)(2,1)S(1)}, bf16[2,256,1120]{1,2,0:T(8,128)(2,1)}, u32[]{:S(2)}) copy-start(bf16[2,256,1120]{1,2,0:T(8,128)(2,1)} %param.8) | copy-start | bytes 3440644
  8.7 4.6 %collective-permute-start.2 = (f32[328,128]{1,0:T(8,128)S(1)}, f32[328,128]{1,0:T(8,128)S(1)}, u32[]{:S(2)}, u32[]{:S(2)}) collective-permute-start(f32[328,128]{1,0:T(8,128)S(1)} %local_states.1.zero_ref), channel_id=1, source_target_pairs={{0,1},{1,0},{2,3},{3,2},{4,5},{5,4},{6,7},{7,6},{8,9},{9,8},{10,11... | collective-permute-start | bytes 503816 | tf_op jit(solution)/shard_map/ppermute | solution.py:334
  9.6 6.2 %collective-permute-start.7 = (f32[328,128]{1,0:T(8,128)S(1)}, f32[328,128]{1,0:T(8,128)S(1)}, u32[]{:S(2)}, u32[]{:S(2)}) collective-permute-start(f32[328,128]{1,0:T(8,128)S(1)} %get-tuple-element.24.one_ref), channel_id=1, source_target_pairs={{0,1},{1,0},{2,3},{3,2},{4,5},{5,4},{6,7},{7,6},{8,9},{9,8},{10,11... | collective-permute-start | bytes 503816 | tf_op jit(solution)/shard_map/ppermute | solution.py:334
  11.2 0.9 %copy-start.8 = (f32[9,1120]{1,0:T(8,128)S(1)}, f32[9,1120]{1,0:T(8,128)}, u32[]{:S(2)}) copy-start(f32[9,1120]{1,0:T(8,128)} %param.13) | copy-start | bytes 120964
  12.1 3.6 %copy-start.7 = (bf16[1,256,1120]{2,1,0:T(8,128)(2,1)S(1)}, bf16[1,256,1120]{2,1,0:T(8,128)(2,1)}, u32[]{:S(2)}) copy-start(bf16[1,256,1120]{2,1,0:T(8,128)(2,1)} %get-tuple-element.45) | copy-start | bytes 1720324
  13.3 7.1 %collective-permute-start.3 = (f32[328,128]{1,0:T(8,128)S(1)}, f32[328,128]{1,0:T(8,128)S(1)}, u32[]{:S(2)}, u32[]{:S(2)}) collective-permute-start(f32[328,128]{1,0:T(8,128)S(1)} %add.92), channel_id=1, source_target_pairs={{0,2},{1,9},{2,0},{3,11},{4,6},{5,13},{6,4},{7,15},{8,10},{9,1},{1... | collective-permute-start | bytes 503816 | tf_op jit(solution)/shard_map/ppermute | solution.py:334
  15.9 6.6 %collective-permute-start.8 = (f32[328,128]{1,0:T(8,128)S(1)}, f32[328,128]{1,0:T(8,128)S(1)}, u32[]{:S(2)}, u32[]{:S(2)}) collective-permute-start(f32[328,128]{1,0:T(8,128)S(1)} %add.96), channel_id=1, source_target_pairs={{0,4},{1,3},{2,6},{3,1},{4,0},{5,7},{6,2},{7,5},{8,12},{9,11},{10,... | collective-permute-start | bytes 503816 | tf_op jit(solution)/shard_map/ppermute | solution.py:334
  20.4 4.3 %collective-permute-start.4 = (f32[328,128]{1,0:T(8,128)S(1)}, f32[328,128]{1,0:T(8,128)S(1)}, u32[]{:S(2)}, u32[]{:S(2)}) collective-permute-start(f32[328,128]{1,0:T(8,128)S(1)} %add.93), channel_id=1, source_target_pairs={{0,4},{1,3},{2,6},{3,1},{4,0},{5,7},{6,2},{7,5},{8,12},{9,11},{10,... | collective-permute-start | bytes 503816 | tf_op jit(solution)/shard_map/ppermute | solution.py:334
  22.5 3.2 %copy-start.6 = (bf16[1,256,1120]{2,1,0:T(8,128)(2,1)S(1)}, bf16[1,256,1120]{2,1,0:T(8,128)(2,1)}, u32[]{:S(2)}) copy-start(bf16[1,256,1120]{2,1,0:T(8,128)(2,1)} %get-tuple-element.46) | copy-start | bytes 1720324
  22.6 6.2 %collective-permute-start.9 = (f32[328,128]{1,0:T(8,128)S(1)}, f32[328,128]{1,0:T(8,128)S(1)}, u32[]{:S(2)}, u32[]{:S(2)}) collective-permute-start(f32[328,128]{1,0:T(8,128)S(1)} %add.97), channel_id=1, source_target_pairs={{0,8},{1,5},{2,10},{3,7},{4,12},{5,1},{6,14},{7,3},{8,0},{9,13},{1... | collective-permute-start | bytes 503816 | tf_op jit(solution)/shard_map/ppermute | solution.py:334
  24.7 6.0 %collective-permute-start.5 = (f32[328,128]{1,0:T(8,128)S(1)}, f32[328,128]{1,0:T(8,128)S(1)}, u32[]{:S(2)}, u32[]{:S(2)}) collective-permute-start(f32[328,128]{1,0:T(8,128)S(1)} %add.94), channel_id=1, source_target_pairs={{0,8},{1,5},{2,10},{3,7},{4,12},{5,1},{6,14},{7,3},{8,0},{9,13},{1... | collective-permute-start | bytes 503816 | tf_op jit(solution)/shard_map/ppermute | solution.py:334
  28.8 10.5 %collective-permute-start.10 = (f32[328,128]{1,0:T(8,128)S(1)}, f32[328,128]{1,0:T(8,128)S(1)}, u32[]{:S(2)}, u32[]{:S(2)}) collective-permute-start(f32[328,128]{1,0:T(8,128)S(1)} %add.98), channel_id=1, source_target_pairs={{0,2},{1,9},{2,0},{3,11},{4,6},{5,13},{6,4},{7,15},{8,10},{9,1},{1... | collective-permute-start | bytes 503816 | tf_op jit(solution)/shard_map/ppermute | solution.py:334
  30.8 10.0 %slice-start = ((s8[5160960]{0:T(1024)(128)(4,1)}), s8[4194304]{0:T(1024)(128)(4,1)S(1)}, s32[]{:S(2)}) async-start(s8[5160960]{0:T(1024)(128)(4,1)} %bitcast.20), calls=%async_computation | async-start | bytes 8388608
  30.8 9.4 %collective-permute-start.6 = (f32[328,128]{1,0:T(8,128)S(1)}, f32[328,128]{1,0:T(8,128)S(1)}, u32[]{:S(2)}, u32[]{:S(2)}) collective-permute-start(f32[328,128]{1,0:T(8,128)S(1)} %add.95.whole_ref), channel_id=1, source_target_pairs={{0,1},{1,0},{2,3},{3,2},{4,5},{5,4},{6,7},{7,6},{8,9},{9,8},{10,11... | collective-permute-start | bytes 503816 | tf_op jit(solution)/shard_map/ppermute | solution.py:334
  38.4 1.3 %copy-start.5 = (bf16[2,256,1120]{1,2,0:T(8,128)(2,1)S(1)}, bf16[2,256,1120]{1,2,0:T(8,128)(2,1)}, u32[]{:S(2)}) copy-start(bf16[2,256,1120]{1,2,0:T(8,128)(2,1)} %param.7) | copy-start | bytes 3440644
  38.4 2.5 %slice-start.1 = ((s8[5160960]{0:T(1024)(128)(4,1)}), s8[966656]{0:T(1024)(128)(4,1)S(1)}, s32[]{:S(2)}) async-start(s8[5160960]{0:T(1024)(128)(4,1)} %bitcast.20), calls=%async_computation.1 | async-start | bytes 1933312
  39.3 8.4 %collective-permute-start.11 = (f32[328,128]{1,0:T(8,128)S(1)}, f32[328,128]{1,0:T(8,128)S(1)}, u32[]{:S(2)}, u32[]{:S(2)}) collective-permute-start(f32[328,128]{1,0:T(8,128)S(1)} %add.99.own_ref), channel_id=1, source_target_pairs={{0,1},{1,0},{2,3},{3,2},{4,5},{5,4},{6,7},{7,6},{8,9},{9,8},{10,11... | collective-permute-start | bytes 503816 | tf_op jit(solution)/shard_map/ppermute | solution.py:334
  40.2 0.9 %copy-start.3 = (f32[20,2240]{1,0:T(8,128)S(1)}, f32[20,2240]{1,0:T(8,128)}, u32[]{:S(2)}) copy-start(f32[20,2240]{1,0:T(8,128)} %gate_ref.1) | copy-start | bytes 537604
  40.2 0.9 %copy-start.4 = (s32[2]{0:T(128)S(1)}, s32[2]{0:T(128)}, u32[]{:S(2)}) copy-start(s32[2]{0:T(128)} %step_ref.1) | copy-start | bytes 28

commit v4 on v3

--- a/solution.py
+++ b/solution.py
@@ -25,8 +25,10 @@
 TROWS = 72
 FOLD = 40
 SLAB = 80
+FIRST_ORDERS = (0, 1, 2), (1, 2, 0)
+SECOND_ORDERS = (2, 0, 1), (0, 1, 2)
 PACKED = FULL_TILES * TROWS + FOLD
-LIMIT = 24 << 20
+LIMIT = 16 << 20
 
 
 def core_of():
@@ -145,7 +147,8 @@
     )(keys, values)
 
 
-def plain_kernel(value_ref, plain_ref, near_ref, far_ref):
+def plain_kernel(value_ref, weight_ref, plain_ref, near_ref, far_ref, taps_ref):
+    taps_ref[...] = weight_ref[...]
     first = core_of() == 0
     for step in range(2):
         plain_ref[step] = value_ref[step].T
@@ -154,19 +157,19 @@
     far_ref[...] = jnp.where(first, head, tail)
 
 
-def plain_values(values):
+def plain_values(values, weights):
     vmem = pl.BlockSpec(memory_space=pltpu.VMEM)
     width = values.shape[1]
     row = jax.ShapeDtypeStruct((COLS, width), BF16)
     return pl.pallas_call(
         plain_kernel,
-        out_shape=(jax.ShapeDtypeStruct((2, TOK, width), BF16), row, row),
-        in_specs=[vmem],
-        out_specs=(vmem,) * 3,
+        out_shape=(jax.ShapeDtypeStruct((2, TOK, width), BF16), row, row, jax.ShapeDtypeStruct(weights.shape, F32)),
+        in_specs=[vmem] * 2,
+        out_specs=(vmem,) * 4,
         compiler_params=pltpu.CompilerParams(vmem_limit_bytes=8 << 20),
         cost_estimate=pl.CostEstimate(flops=1_000_000, bytes_accessed=2_400_000, transcendentals=0),
         name="plain_values",
-    )(values)
+    )(values, weights)
 
 
 def convolve(padded, conv_weight):
@@ -182,7 +185,7 @@
     return summed.reshape(TOK, padded.shape[-1])
 
 
-def spread_kernel(own, query, whole_ref, zero_ref, one_ref, out_ref):
+def spread_kernel(own, query, conv_ref, whole_ref, zero_ref, one_ref, out_ref, acc):
     half = core_of() if own else 1 - core_of()
     base = half * HALF
     whole = whole_ref[...]
@@ -217,40 +220,55 @@
             part_den = got[len(heads) * SLAB : len(heads) * SLAB + HALF_HEADS]
             den = part_den if den is None else den + part_den
         inverse = 1.0 / den
-        out_ref[step] = jnp.zeros((HALF, TOK), F32)
+        acc[...] = jnp.zeros((HALF, TOK), F32)
         for head in range(HALF_HEADS):
             first = HD * head // 8 * 8
             count = -(-(HD * head - first + HD) // 8) * 8
             spot = slice(first, first + count)
-            out_ref[step, spot] = out_ref[step, spot] + sums[head][:count] * inverse[head : head + 1]
-
-
-def spread(own, queries, whole, zero, one):
+            acc[spot] = acc[spot] + sums[head][:count] * inverse[head : head + 1]
+        conv = conv_ref[step, pl.ds(pl.multiple_of(base, HALF), HALF)]
+        out_ref[:, step * TOK : (step + 1) * TOK] = (acc[...] + conv).astype(BF16)
+
+
+def spread(own, queries, conv, whole, zero, one):
     vmem = pl.BlockSpec(memory_space=pltpu.VMEM)
     return pl.pallas_call(
         functools.partial(spread_kernel, own),
-        out_shape=jax.ShapeDtypeStruct((2, HALF, TOK), F32),
-        in_specs=[vmem] * 4,
+        out_shape=jax.ShapeDtypeStruct((HALF, 2 * TOK), BF16),
+        in_specs=[vmem] * 5,
         out_specs=vmem,
+        scratch_shapes=[pltpu.VMEM((HALF, TOK), F32)],
         compiler_params=pltpu.CompilerParams(vmem_limit_bytes=8 << 20),
         cost_estimate=pl.CostEstimate(flops=800_000_000, bytes_accessed=2_000_000, transcendentals=0),
         name="spread",
-    )(queries, whole, zero, one)
-
-
-def project_kernel(chunks, step_ref, conv0, conv1, weight_hbm, gate_ref, own_ref, other_ref, out_hbm,
-                   weight, turned, mixed, result, sem_in, sem_out):
-    load = pltpu.make_async_copy(weight_hbm, weight, sem_in)
-    load.start()
+    )(queries, conv, whole, zero, one)
+
+
+def turn_kernel(conv0, conv1, out_ref):
+    for step, conv in enumerate((conv0, conv1)):
+        out_ref[step] = conv[...].T
+
+
+def turn(conv0, conv1):
+    tokens, width = conv0.shape
+    vmem = pl.BlockSpec(memory_space=pltpu.VMEM)
+    return pl.pallas_call(
+        turn_kernel,
+        out_shape=jax.ShapeDtypeStruct((2, width, tokens), F32),
+        in_specs=[vmem] * 2,
+        out_specs=vmem,
+        compiler_params=pltpu.CompilerParams(vmem_limit_bytes=8 << 20),
+        cost_estimate=pl.CostEstimate(flops=1_000_000, bytes_accessed=4_600_000, transcendentals=0),
+        name="turn",
+    )(conv0, conv1)
+
+
+def project_kernel(chunks, step_ref, weight, gate_ref, own_ref, other_ref, out_hbm, mixed, result, sem_out):
     half = core_of()
-    for step in range(2):
-        turned[...] = (conv0, conv1)[step][...].T
-        for at, part in ((half, own_ref), (1 - half, other_ref)):
-            spot = pl.ds(pl.multiple_of(at * HALF, HALF), HALF)
-            mixed[spot, step * TOK : (step + 1) * TOK] = (part[step] + turned[spot]).astype(BF16)
+    for at, part in ((half, own_ref), (1 - half, other_ref)):
+        mixed[pl.ds(pl.multiple_of(at * HALF, HALF), HALF)] = part[...]
     gate_rows = [gate_ref[pl.ds(step_ref[s], 1), :] for s in range(2)]
     gates = jnp.concatenate(gate_rows + [gate_rows[0]] * 6, axis=0).T
-    load.wait()
     stores = []
     for n, (start, size) in enumerate(chunks):
         prod = lax.dot_general(
@@ -270,7 +288,26 @@
         store.wait()
 
 
-def project(timesteps, conv, weight, gate_table, own, other):
+def stage_kernel(weight_hbm, out_ref, sem):
+    load = pltpu.make_async_copy(weight_hbm, out_ref, sem)
+    load.start()
+    load.wait()
+
+
+def stage(weight):
+    return pl.pallas_call(
+        stage_kernel,
+        out_shape=jax.ShapeDtypeStruct(weight.shape, weight.dtype),
+        in_specs=[pl.BlockSpec(memory_space=pltpu.HBM)],
+        out_specs=pl.BlockSpec(memory_space=pltpu.VMEM),
+        scratch_shapes=[pltpu.SemaphoreType.DMA],
+        compiler_params=pltpu.CompilerParams(vmem_limit_bytes=8 << 20),
+        cost_estimate=pl.CostEstimate(flops=0, bytes_accessed=5_000_000, transcendentals=0),
+        name="stage",
+    )(weight)
+
+
+def project(timesteps, weight, gate_table, own, other):
     width = weight.shape[1]
     chunks = [(s, min(256, width - s)) for s in range(0, width, 256)]
     vmem = pl.BlockSpec(memory_space=pltpu.VMEM)
@@ -278,50 +315,88 @@
     return pl.pallas_call(
         functools.partial(project_kernel, chunks),
         out_shape=jax.ShapeDtypeStruct((2, width, TOK), F32),
-        in_specs=[pl.BlockSpec(memory_space=pltpu.SMEM), vmem, vmem, anyspace, vmem, vmem, vmem],
+        in_specs=[pl.BlockSpec(memory_space=pltpu.SMEM)] + [vmem] * 4,
         out_specs=anyspace,
         scratch_shapes=[
-            pltpu.VMEM((2 * HALF, width), BF16),
-            pltpu.VMEM((2 * HALF, TOK), F32),
             pltpu.VMEM((2 * HALF, 2 * TOK), BF16),
             pltpu.VMEM((2, width, TOK), F32),
-            pltpu.SemaphoreType.DMA,
             pltpu.SemaphoreType.DMA((len(chunks), 2)),
         ],
         compiler_params=pltpu.CompilerParams(vmem_limit_bytes=LIMIT),
         cost_estimate=pl.CostEstimate(flops=3_000_000_000, bytes_accessed=14_000_000, transcendentals=0),
         name="project",
-    )(timesteps, *conv, weight, gate_table, own, other)
-
-
-def fresh_kernel(scale, own_ref, other_ref, state_ref, total_ref):
-    first = core_of() == 0
-    own, other = own_ref[...], other_ref[...]
-    halves = (jnp.where(first, own, other), jnp.where(first, other, own))
+    )(timesteps, weight, gate_table, own, other)
+
+
+def unpack_half(scale, packed, state_ref, total_ref):
     lanes = lax.broadcasted_iota(jnp.int32, (TROWS, LANES), 1)
-    for half, packed in enumerate(halves):
-        tiles = unpack_tiles(packed * scale)
-        for head in range(HALF_HEADS):
-            block = None
-            for tile in tiles_of(head):
-                low = max(HD * head, LANES * tile)
-                turn = (HD * head - TILE_BASE[tile]) % LANES
-                moved = pltpu.roll(tiles[tile], (LANES - turn) % LANES, 1) if turn else tiles[tile]
-                block = moved if block is None else jnp.where(lanes >= low - HD * head, moved, block)
-            at = half * HALF_HEADS + head
-            total_ref[at : at + 1, :] = block[HD : HD + 1, :HD]
-            state_ref[:, at, :] = block.T[:HD, :HD]
-
-
-def fresh(own, other, tokens):
-    return pl.pallas_call(
-        functools.partial(fresh_kernel, 1.0 / tokens),
+    tiles = unpack_tiles(packed * scale)
+    for head in range(HALF_HEADS):
+        block = None
+        for tile in tiles_of(head):
+            low = max(HD * head, LANES * tile)
+            turn = (HD * head - TILE_BASE[tile]) % LANES
+            moved = pltpu.roll(tiles[tile], (LANES - turn) % LANES, 1) if turn else tiles[tile]
+            block = moved if block is None else jnp.where(lanes >= low - HD * head, moved, block)
+        total_ref[head : head + 1, :] = block[HD : HD + 1, :HD]
+        state_ref[:, head, :] = block.T[:HD, :HD]
+
+
+def own_kernel(scale, packed_ref, state_ref, total_ref):
+    unpack_half(scale, packed_ref[...], state_ref, total_ref)
+
+
+def rest_kernel(scale, packed_ref, own_state, own_total, state_out, total_out, state, total, sems):
+    def stores(half, pair, n):
+        spot = pl.ds(pl.multiple_of(half * HALF_HEADS, HALF_HEADS), HALF_HEADS)
+        moves = [
+            pltpu.make_async_copy(pair[0], state_out.at[:, spot], sems.at[n]),
+            pltpu.make_async_copy(pair[1], total_out.at[spot], sems.at[n + 1]),
+        ]
+        for move in moves:
+            move.start()
+        return moves
+
+    moves = stores(core_of(), (own_state, own_total), 0)
+    unpack_half(scale, packed_ref[...], state, total)
+    moves += stores(1 - core_of(), (state, total), 2)
+    for move in moves:
+        move.wait()
+
+
+FRESH_COST = pl.CostEstimate(flops=1_000_000, bytes_accessed=600_000, transcendentals=0)
+
+
+def fresh_own(packed, tokens):
+    vmem = pl.BlockSpec(memory_space=pltpu.VMEM)
+    return pl.pallas_call(
+        functools.partial(own_kernel, 1.0 / tokens),
+        out_shape=(jax.ShapeDtypeStruct((HD, HALF_HEADS, HD), F32), jax.ShapeDtypeStruct((HALF_HEADS, HD), F32)),
+        in_specs=[vmem],
+        out_specs=(vmem,) * 2,
+        compiler_params=pltpu.CompilerParams(vmem_limit_bytes=4 << 20),
+        cost_estimate=FRESH_COST,
+        name="fresh_own",
+    )(packed)
+
+
+def fresh_rest(packed, own, tokens):
+    vmem = pl.BlockSpec(memory_space=pltpu.VMEM)
+    anyspace = pl.BlockSpec(memory_space=pl.ANY)
+    return pl.pallas_call(
+        functools.partial(rest_kernel, 1.0 / tokens),
         out_shape=(jax.ShapeDtypeStruct((HD, NH, HD), F32), jax.ShapeDtypeStruct((NH, HD), F32)),
-        in_specs=[pl.BlockSpec(memory_space=pltpu.VMEM)] * 2,
-        out_specs=(pl.BlockSpec(memory_space=pltpu.VMEM),) * 2,
-        compiler_params=pltpu.CompilerParams(vmem_limit_bytes=LIMIT),
-        name="fresh",
-    )(own, other)
+        in_specs=[vmem] * 3,
+        out_specs=(anyspace,) * 2,
+        scratch_shapes=[
+            pltpu.VMEM((HD, HALF_HEADS, HD), F32),
+            pltpu.VMEM((HALF_HEADS, HD), F32),
+            pltpu.SemaphoreType.DMA((4,)),
+        ],
+        compiler_params=pltpu.CompilerParams(vmem_limit_bytes=4 << 20),
+        cost_estimate=FRESH_COST,
+        name="fresh_rest",
+    )(packed, *own)
 
 
 def local(queries, keys, values, timesteps, gate_table, out_weight, conv_weight):
@@ -337,14 +412,18 @@
         return swap(x, lambda c: 1)
 
     bits = [1 << b for b in range(1, count.bit_length() - 1)]
-    turned = bits[-1:] + bits[:-1]
-    rounds = [lambda c, b=b, t=t: t if c else b for b, t in zip(bits, turned)]
+
+    parts = [bits[len(bits) * i // 3 : len(bits) * (i + 1) // 3] for i in range(3)]
+
+    def rounds(even, odd):
+        pairs = zip(*([b for i in order for b in parts[i]] for order in (even, odd)))
+        return [lambda c, b=b, t=t: t if c else b for b, t in pairs]
 
     first = core_of() == 0
     (send0,) = local_states(far_keys, far_values, ((0, 0),))
     (keep0,) = held_states(keys, values, ((0, 1),))
     send1, keep1 = held_states(keys, values, ((1, 0), (1, 1)))
-    plain, near, far = plain_values(values)
+    plain, near, far, conv_weight = plain_values(values, conv_weight)
     near = partner(near)
     links = [p for i in range(1, count - 1, 2) for p in ((i, i + 1), (i + 1, i))]
     far = lax.ppermute(far, "tm", links)
@@ -353,22 +432,24 @@
     conv0 = convolve(jnp.concatenate([above[None], grid[0], below[None]], axis=0), conv_weight)
     again, above, below, weights, conv0 = lax.optimization_barrier((grid[1], above, below, conv_weight, conv0))
     conv1 = convolve(jnp.concatenate([above[None], again, below[None]], axis=0), weights)
-    conv = conv0, conv1
+    conv = turn(conv0, conv1)
     got0 = partner(send0)
     got1 = partner(send1)
     whole, second = keep0 + got0, keep1 + got1
-    for pick in rounds:
+    for pick in rounds(*FIRST_ORDERS):
         got = swap(whole, pick)
         whole = whole + got
-    for pick in rounds[1:] + rounds[:1]:
+    for pick in rounds(*SECOND_ORDERS):
         got = swap(second, pick)
         second = second + got
     other = partner(whole)
-    own = spread(True, queries, whole, keep0, keep1)
-    rest = spread(False, queries, other, send0, send1)
-    update = project(timesteps, conv, out_weight, gate_table, own, rest)
+    staged = stage(pltpu.with_memory_space_constraint(out_weight, pltpu.HBM))
+    own = spread(True, queries, conv, whole, keep0, keep1)
+    rest = spread(False, queries, conv, other, send0, send1)
+    update = project(timesteps, staged, gate_table, own, rest)
     other1 = partner(second)
-    fresh_state, fresh_total = fresh(second, other1, tokens)
+    outs = fresh_own(second, tokens)
+    fresh_state, fresh_total = fresh_rest(other1, outs, tokens)
     return update.transpose(0, 2, 1), fresh_state.transpose(1, 0, 2), fresh_total
 
 

time: 49.9 us -> 56.5 us (1.13)
  local copies, waits for them, and re-layouts: 3.49 us -> 6.52 us
  waiting for transfers between devices: 8.03 us -> 10.5 us
  Pallas kernels: 12.7 us -> 14.7 us
  starting transfers between devices: 20.8 us -> 20.1 us
    pallas_call x1 -> x4, Pallas kernels: 1.44 us -> 4.58 us  [the longest x1 2.47 us: stage(): pl.pallas_call(stage_kernel, out_shape=jax.ShapeDtypeStruct(weight.shape,...]
    unnamed x22 -> x24, local copies, waits for them, and re-layouts: 2.17 us -> 5.17 us
    ppermute x11, waiting for transfers between devices: 8.03 us -> 10.5 us  [swap(): return lax.ppermute(x, 'tm', [(i, i ^ pick(i % 2)) for i in range(count)])]
    pallas_call x1, Pallas kernels: 6.59 us -> 5.14 us  [project(): pl.pallas_call(functools.partial(project_kernel, chunks), out_shape=jax.S...]
    ppermute x11, starting transfers between devices: 16.2 us -> 15.6 us  [swap(): return lax.ppermute(x, 'tm', [(i, i ^ pick(i % 2)) for i in range(count)])]
  transfers between devices with their start and end apart: 12 -> 12, of which waited for: 3 -> 4; matrix products, arithmetic and copies ran while one was open for 9% -> 8% of each run, Pallas kernels for 22% -> 24%
where the time goes in v4:
time: 56.5 us; the launch traced here: 56 us
  starting transfers between devices  20.1 us (36%)
  Pallas kernels  14.7 us (26%)
  waiting for transfers between devices  10.5 us (19%)
  local copies, waits for them, and re-layouts  6.52 us (12%)
  other arithmetic  3.32 us (6%)
  between operations  0.92 us (2%)
    ppermute x11, starting transfers between devices, swap(): return lax.ppermute(x, 'tm', [(i, i ^ pick(i % 2)) for i in range(count)])  15.6 us
    ppermute x11, waiting for transfers between devices, swap(): return lax.ppermute(x, 'tm', [(i, i ^ pick(i % 2)) for i in range(count)])  10.5 us
    unnamed x24, local copies, waits for them, and re-layouts  5.17 us
    pallas_call x1, Pallas kernels, project(): pl.pallas_call(functools.partial(project_kernel, chunks), out_shape=jax.S...  5.14 us
    ppermute x1, starting transfers between devices, local(): far = lax.ppermute(far, 'tm', links)  4.52 us
    pallas_call x1, Pallas kernels, stage(): pl.pallas_call(stage_kernel, out_shape=jax.ShapeDtypeStruct(weight.shape,...  2.47 us
    add x2, other arithmetic, convolve(): summed + widened[tap_row:tap_row + ROWS_DEV, tap_col:tap_col + COLS] * co...  1.78 us
    pallas_call x1, Pallas kernels, local_states(): pl.pallas_call(functools.partial(state_kernel, picks), out_shape=(jax.Sha...  1.76 us
  transfers between devices with their start and end apart: 12, of which 4 were waited for; matrix products, arithmetic and copies ran while one was open for 8% of the time, Pallas kernels for 24%

profile of v4, /device:TPU:1, one launch (start us, length us, event | category | flops | bytes accessed | tf_op | source)
XLA Modules:
  0.0 56.0 jit_solution(13576691232671038172)
XLA Ops:
  0.6 0.0 copy-start.1
  0.6 1.2 %copy-done.1 = bf16[2,256,1120]{1,2,0:T(8,128)(2,1)S(1)} copy-done((bf16[2,256,1120]{1,2,0:T(8,128)(2,1)S(1)}, bf16[2,256,1120]{1,2,0:T(8,128)(2,1)}, u32[]{:S(2)}) %copy-start.1) | copy-done | bytes 1146904
  1.9 0.9 %copy-done.6 = f32[9,1120]{1,0:T(8,128)S(1)} copy-done((f32[9,1120]{1,0:T(8,128)S(1)}, f32[9,1120]{1,0:T(8,128)}, u32[]{:S(2)}) %copy-start.6) | copy-done | bytes 40344
  2.8 0.4 plain_values.1
  3.1 0.1 collective-permute-start.1
  3.2 4.5 %collective-permute-start = (bf16[64,1120]{1,0:T(8,128)(2,1)S(1)}, bf16[64,1120]{1,0:T(8,128)(2,1)}, u32[]{:S(2)}, u32[]{:S(2)}) collective-permute-start(bf16[64,1120]{1,0:T(8,128)(2,1)S(1)} %get-tuple-element.19), channel_id=1, source_target_pairs={{1,2},{2,1},{3,4},{4,3},{5,6},{6,5},{7,8},{8,7},{9,10},{10,9},{11,... | collective-permute-start | bytes 430088 | tf_op jit(solution)/shard_map/ppermute | solution.py:429
  7.8 0.0 copy-start.2
  7.8 0.0 copy-start.3
  7.8 1.8 %local_states.1.zero_ref = f32[328,128]{1,0:T(8,128)S(1)} custom-call(bf16[2,1120,256]{2,1,0:T(8,128)(2,1)} %bitcast.19, bf16[2,1120,256]{2,1,0:T(8,128)(2,1)} %bitcast.15), custom_call_target="tpu_custom_call" | custom-call | flops 300000000 | bytes 800000 | tf_op jit(solution)/shard_map/local_states/pallas_call | solution.py:134
  9.6 0.1 collective-permute-start.2
  9.7 0.9 %held_states.3 = (f32[328,128]{1,0:T(8,128)S(1)}, f32[328,128]{1,0:T(8,128)S(1)}) custom-call(bf16[2,1120,256]{2,1,0:T(8,128)(2,1)S(1)} %bitcast.20, bf16[2,1120,256]{2,1,0:T(8,128)(2,1)S(1)} %bitcast.17), custom_call_target="tpu_custom_call" | custom-call | flops 600000000 | bytes 1600000 | tf_op jit(solution)/shard_map/held_states/pallas_call | solution.py:120
  10.5 0.5 collective-permute-start.7
  11.0 2.5 %stage.1.weight = bf16[1120,2240]{1,0:T(8,128)(2,1)S(1)} custom-call(bf16[1120,2240]{1,0:T(8,128)(2,1)} %weight_hbm.1), custom_call_target="tpu_custom_call" | custom-call | bytes 5000000 | tf_op jit(solution)/shard_map/stage/pallas_call | solution.py:298
  13.5 2.3 %copy-done = bf16[1120,2240]{1,0:T(8,128)(2,1)} copy-done((bf16[1120,2240]{1,0:T(8,128)(2,1)}, bf16[1120,2240]{1,0:T(8,128)(2,1)S(1)}, u32[]{:S(2)}) %copy-start) | copy-done | bytes 5017624
  15.8 1.1 %fusion.28 = (bf16[1,256,1120]{2,1,0:T(8,128)(2,1)}, bf16[1,256,1120]{2,1,0:T(8,128)(2,1)}) fusion(bf16[2,256,1120]{2,1,0:T(8,128)(2,1)S(1)} %get-tuple-element.18), kind=kLoop, calls=%fused_computation.68 | loop fusion | bytes 2293760 | tf_op jit(solution)/shard_map/slice | solution.py:432
  16.9 0.5 held_states.2.zero_ref
  17.4 0.1 slice_reduce_fusion.17
  17.6 1.1 %broadcast_select_fusion = (bf16[64,1120]{1,0:T(8,128)(2,1)S(1)}, bf16[64,1120]{1,0:T(8,128)(2,1)S(1)}) fusion(bf16[64,1120]{1,0:T(8,128)(2,1)} %collective-permute-done.1, bf16[64,1120]{1,0:T(8,128)(2,1)} %collective-permute-done, pred[]{:T(512)S(6)} %eq.3), kind=kLoop, calls=%fused_computation.48 | loop fusion | flops 143360 | bytes 573441 | tf_op jit(solution)/shard_map/jit(_where)/select_n | solution.py:430
  18.7 1.4 %collective-permute-start.3 = (f32[328,128]{1,0:T(8,128)S(1)}, f32[328,128]{1,0:T(8,128)S(1)}, u32[]{:S(2)}, u32[]{:S(2)}) collective-permute-start(f32[328,128]{1,0:T(8,128)S(1)} %add.92), channel_id=1, source_target_pairs={{0,2},{1,5},{2,0},{3,7},{4,6},{5,1},{6,4},{7,3},{8,10},{9,13},{10,... | collective-permute-start | bytes 503816 | tf_op jit(solution)/shard_map/ppermute | solution.py:409
  20.0 0.1 maximum_convert_fusion
  20.2 1.3 %collective-permute-start.8 = (f32[328,128]{1,0:T(8,128)S(1)}, f32[328,128]{1,0:T(8,128)S(1)}, u32[]{:S(2)}, u32[]{:S(2)}) collective-permute-start(f32[328,128]{1,0:T(8,128)S(1)} %add.96), channel_id=1, source_target_pairs={{0,8},{1,3},{2,10},{3,1},{4,12},{5,7},{6,14},{7,5},{8,0},{9,11},{1... | collective-permute-start | bytes 503816 | tf_op jit(solution)/shard_map/ppermute | solution.py:409
  21.5 1.7 %collective-permute-done.3 = f32[328,128]{1,0:T(8,128)S(1)} collective-permute-done((f32[328,128]{1,0:T(8,128)S(1)}, f32[328,128]{1,0:T(8,128)S(1)}, u32[]{:S(2)}, u32[]{:S(2)}) %collective-permute-start.3) | collective-permute-done | bytes 167968 | tf_op jit(solution)/shard_map/ppermute | solution.py:409
  23.3 2.4 %collective-permute-start.4 = (f32[328,128]{1,0:T(8,128)S(1)}, f32[328,128]{1,0:T(8,128)S(1)}, u32[]{:S(2)}, u32[]{:S(2)}) collective-permute-start(f32[328,128]{1,0:T(8,128)S(1)} %add.93), channel_id=1, source_target_pairs={{0,4},{1,9},{2,6},{3,11},{4,0},{5,13},{6,2},{7,15},{8,12},{9,1},{1... | collective-permute-start | bytes 503816 | tf_op jit(solution)/shard_map/ppermute | solution.py:409
  25.6 0.9 %fusion.8 = f32[4,64,1120]{2,1,0:T(8,128)S(1)} fusion(f32[6,64,1120]{2,1,0:T(8,128)S(1)} %maximum_convert_fusion, f32[1120]{0:T(1024)S(1)} %get-tuple-element.43, f32[1120]{0:T(1024)S(1)} %get-tuple-element.44, f32[1120]{0:T(1024)S(1)} %get-tuple-element.45, f32[1120]{0:T(1024)S(1)} %get-tuple-element.46, f32[1120]{0:T(1024)S(1)} %get-tuple-element.47, ...), kind=kLoop, calls=%fused_computation.20 | loop fusion | flops 4874240 | bytes 6529024 | tf_op jit(solution)/shard_map/add | solution.py:181
  26.6 1.4 %collective-permute-start.9 = (f32[328,128]{1,0:T(8,128)S(1)}, f32[328,128]{1,0:T(8,128)S(1)}, u32[]{:S(2)}, u32[]{:S(2)}) collective-permute-start(f32[328,128]{1,0:T(8,128)S(1)} %add.97), channel_id=1, source_target_pairs={{0,2},{1,5},{2,0},{3,7},{4,6},{5,1},{6,4},{7,3},{8,10},{9,13},{10,... | collective-permute-start | bytes 503816 | tf_op jit(solution)/shard_map/ppermute | solution.py:409
  27.9 3.7 %collective-permute-done.4 = f32[328,128]{1,0:T(8,128)S(1)} collective-permute-done((f32[328,128]{1,0:T(8,128)S(1)}, f32[328,128]{1,0:T(8,128)S(1)}, u32[]{:S(2)}, u32[]{:S(2)}) %collective-permute-start.4) | collective-permute-done | bytes 167968 | tf_op jit(solution)/shard_map/ppermute | solution.py:409
  31.6 0.3 collective-permute-start.5
  31.9 0.1 maximum_convert_fusion.1
  32.1 0.1 slice_reduce_fusion.8
  32.2 1.8 %collective-permute-done.9 = f32[328,128]{1,0:T(8,128)S(1)} collective-permute-done((f32[328,128]{1,0:T(8,128)S(1)}, f32[328,128]{1,0:T(8,128)S(1)}, u32[]{:S(2)}, u32[]{:S(2)}) %collective-permute-start.9) | collective-permute-done | bytes 167968 | tf_op jit(solution)/shard_map/ppermute | solution.py:409
  34.1 0.7 %collective-permute-start.10 = (f32[328,128]{1,0:T(8,128)S(1)}, f32[328,128]{1,0:T(8,128)S(1)}, u32[]{:S(2)}, u32[]{:S(2)}) collective-permute-start(f32[328,128]{1,0:T(8,128)S(1)} %add.98), channel_id=1, source_target_pairs={{0,4},{1,9},{2,6},{3,11},{4,0},{5,13},{6,2},{7,15},{8,12},{9,1},{1... | collective-permute-start | bytes 503816 | tf_op jit(solution)/shard_map/ppermute | solution.py:409
  34.7 3.3 %collective-permute-done.5 = f32[328,128]{1,0:T(8,128)S(1)} collective-permute-done((f32[328,128]{1,0:T(8,128)S(1)}, f32[328,128]{1,0:T(8,128)S(1)}, u32[]{:S(2)}, u32[]{:S(2)}) %collective-permute-start.5) | collective-permute-done | bytes 167968 | tf_op jit(solution)/shard_map/ppermute | solution.py:409
  38.0 7.5 %collective-permute-start.6 = (f32[328,128]{1,0:T(8,128)S(1)}, f32[328,128]{1,0:T(8,128)S(1)}, u32[]{:S(2)}, u32[]{:S(2)}) collective-permute-start(f32[328,128]{1,0:T(8,128)S(1)} %add.95.whole_ref), channel_id=1, source_target_pairs={{0,1},{1,0},{2,3},{3,2},{4,5},{5,4},{6,7},{7,6},{8,9},{9,8},{10,11... | collective-permute-start | bytes 503816 | tf_op jit(solution)/shard_map/ppermute | solution.py:409
  45.5 0.9 %fusion.22 = f32[4,64,1120]{2,1,0:T(8,128)S(1)} fusion(f32[6,64,1120]{2,1,0:T(8,128)S(1)} %maximum_convert_fusion.1, f32[1120]{0:T(1024)S(1)} %get-tuple-element.34, f32[1120]{0:T(1024)S(1)} %get-tuple-element.35, f32[1120]{0:T(1024)S(1)} %get-tuple-element.36, f32[1120]{0:T(1024)S(1)} %get-tuple-element.37, f32[1120]{0:T(1024)S(1)} %get-tuple-element.38, ...), kind=kLoop, calls=%fused_computation.34 | loop fusion | flops 4874240 | bytes 6529024 | tf_op jit(solution)/shard_map/add | solution.py:181
  46.4 0.0 copy-start.4
  46.4 0.7 %turn.1.conv_ref = f32[2,1120,256]{2,1,0:T(8,128)S(1)} custom-call(f32[256,1120]{1,0:T(8,128)S(1)} %bitcast.22, f32[256,1120]{1,0:T(8,128)S(1)} %bitcast.23), custom_call_target="tpu_custom_call" | custom-call | flops 1000000 | bytes 4600000 | tf_op jit(solution)/shard_map/turn/pallas_call | solution.py:255
  47.1 0.1 collective-permute-start.11
  47.2 0.3 fresh_own.1
  47.6 0.1 copy-done.4
  47.7 0.7 %spread.2.own_ref = bf16[560,512]{1,0:T(8,128)(2,1)S(1)} custom-call(bf16[2,1120,256]{2,1,0:T(8,128)(2,1)S(1)} %bitcast.24, f32[2,1120,256]{2,1,0:T(8,128)S(1)} %turn.1.conv_ref, f32[328,128]{1,0:T(8,128)S(1)} %add.95.whole_ref, f32[328,128]{1,0:T(8,128)S(1)} %held_states.2.zero_ref, f32[328,128]{1,0:T(8,128)S(1)} %get-tuple-element.27.one_ref), custom_call_target="tpu_custom_call" | custom-call | flops 800000000 | bytes 2000000 | tf_op jit(solution)/shard_map/spread/pallas_call | solution.py:235
  48.4 0.0 copy-start.5
  48.4 0.0 copy-start.7
  48.4 0.7 %spread.3.other_ref = bf16[560,512]{1,0:T(8,128)(2,1)S(1)} custom-call(bf16[2,1120,256]{2,1,0:T(8,128)(2,1)S(1)} %bitcast.25, f32[2,1120,256]{2,1,0:T(8,128)S(1)} %turn.1.conv_ref, f32[328,128]{1,0:T(8,128)S(1)} %collective-permute-done.6.whole_ref, f32[328,128]{1,0:T(8,128)S(1)} %local_states.1.zero_ref, f32[328,128]{1,0:T(8,128)S(1)} %get-tuple-element.28.one_ref), custom_call_target="tpu_custom_call" | custom-call | flops 800000000 | bytes 2000000 | tf_op jit(solution)/shard_map/spread/pallas_call | solution.py:235
  49.2 0.2 slice-done
  49.4 0.3 slice-done.1
  49.6 0.1 copy-done.5
  49.8 5.1 %project.1 = f32[2,2240,256]{2,1,0:T(8,128)} custom-call(s32[2]{0:T(128)S(1)} %copy-done.7, bf16[1120,2240]{1,0:T(8,128)(2,1)S(1)} %bitcast.14, f32[20,2240]{1,0:T(8,128)S(1)} %copy-done.5, bf16[560,512]{1,0:T(8,128)(2,1)S(1)} %spread.2.own_ref, bf16[560,512]{1,0:T(8,128)(2,1)S(1)} %spread.3.other_ref), custom_call_target="tpu_custom_call" | custom-call | flops 3000000000 | bytes 14000000 | tf_op jit(solution)/shard_map/project/pallas_call | solution.py:315
  54.9 1.1 %fresh_rest.1 = (f32[70,16,70]{2,1,0:T(8,128)}, f32[16,70]{1,0:T(8,128)}) custom-call(f32[328,128]{1,0:T(8,128)S(1)} %collective-permute-done.11.packed_ref, f32[70,8,70]{2,1,0:T(8,128)S(1)} %get-tuple-element.29.own_state, f32[8,70]{1,0:T(8,128)S(1)} %get-tuple-element.30.own_total), custom_call_target="tpu_custom_call" | custom-call | flops 1000000 | bytes 600000 | tf_op jit(solution)/shard_map/fresh_rest/pallas_call | solution.py:386
  (28 shorter events, 0.2 us)
Async XLA Ops:
  0.6 1.3 %copy-start.1 = (bf16[2,256,1120]{1,2,0:T(8,128)(2,1)S(1)}, bf16[2,256,1120]{1,2,0:T(8,128)(2,1)}, u32[]{:S(2)}) copy-start(bf16[2,256,1120]{1,2,0:T(8,128)(2,1)} %param.9) | copy-start | bytes 3440644
  1.9 0.9 %copy-start.6 = (f32[9,1120]{1,0:T(8,128)S(1)}, f32[9,1120]{1,0:T(8,128)}, u32[]{:S(2)}) copy-start(f32[9,1120]{1,0:T(8,128)} %weight_ref.1) | copy-start | bytes 120964
  3.1 14.4 %collective-permute-start.1 = (bf16[64,1120]{1,0:T(8,128)(2,1)S(1)}, bf16[64,1120]{1,0:T(8,128)(2,1)}, u32[]{:S(2)}, u32[]{:S(2)}) collective-permute-start(bf16[64,1120]{1,0:T(8,128)(2,1)S(1)} %get-tuple-element.20), channel_id=1, source_target_pairs={{0,1},{1,0},{2,3},{3,2},{4,5},{5,4},{6,7},{7,6},{8,9},{9,8},{10,11... | collective-permute-start | bytes 430088 | tf_op jit(solution)/shard_map/ppermute | solution.py:409
  3.2 14.3 %collective-permute-start = (bf16[64,1120]{1,0:T(8,128)(2,1)S(1)}, bf16[64,1120]{1,0:T(8,128)(2,1)}, u32[]{:S(2)}, u32[]{:S(2)}) collective-permute-start(bf16[64,1120]{1,0:T(8,128)(2,1)S(1)} %get-tuple-element.19), channel_id=1, source_target_pairs={{1,2},{2,1},{3,4},{4,3},{5,6},{6,5},{7,8},{8,7},{9,10},{10,9},{11,... | collective-permute-start | bytes 430088 | tf_op jit(solution)/shard_map/ppermute | solution.py:429
  7.8 1.9 %copy-start.2 = (bf16[2,256,1120]{1,2,0:T(8,128)(2,1)S(1)}, bf16[2,256,1120]{1,2,0:T(8,128)(2,1)}, u32[]{:S(2)}) copy-start(bf16[2,256,1120]{1,2,0:T(8,128)(2,1)} %param.9) | copy-start | bytes 3440644
  7.8 1.9 %copy-start.3 = (bf16[2,256,1120]{1,2,0:T(8,128)(2,1)S(1)}, bf16[2,256,1120]{1,2,0:T(8,128)(2,1)}, u32[]{:S(2)}) copy-start(bf16[2,256,1120]{1,2,0:T(8,128)(2,1)} %param.8) | copy-start | bytes 3440644
  9.6 9.1 %collective-permute-start.2 = (f32[328,128]{1,0:T(8,128)S(1)}, f32[328,128]{1,0:T(8,128)S(1)}, u32[]{:S(2)}, u32[]{:S(2)}) collective-permute-start(f32[328,128]{1,0:T(8,128)S(1)} %local_states.1.zero_ref), channel_id=1, source_target_pairs={{0,1},{1,0},{2,3},{3,2},{4,5},{5,4},{6,7},{7,6},{8,9},{9,8},{10,11... | collective-permute-start | bytes 503816 | tf_op jit(solution)/shard_map/ppermute | solution.py:409
  10.5 9.7 %collective-permute-start.7 = (f32[328,128]{1,0:T(8,128)S(1)}, f32[328,128]{1,0:T(8,128)S(1)}, u32[]{:S(2)}, u32[]{:S(2)}) collective-permute-start(f32[328,128]{1,0:T(8,128)S(1)} %get-tuple-element.28.one_ref), channel_id=1, source_target_pairs={{0,1},{1,0},{2,3},{3,2},{4,5},{5,4},{6,7},{7,6},{8,9},{9,8},{10,11... | collective-permute-start | bytes 503816 | tf_op jit(solution)/shard_map/ppermute | solution.py:409
  13.5 2.3 %copy-start = (bf16[1120,2240]{1,0:T(8,128)(2,1)}, bf16[1120,2240]{1,0:T(8,128)(2,1)S(1)}, u32[]{:S(2)}) copy-start(bf16[1120,2240]{1,0:T(8,128)(2,1)S(1)} %stage.1.weight) | copy-start | bytes 15052804
  17.4 2.6 %copy-start.9 = (bf16[1,256,1120]{2,1,0:T(8,128)(2,1)S(1)}, bf16[1,256,1120]{2,1,0:T(8,128)(2,1)}, u32[]{:S(2)}) copy-start(bf16[1,256,1120]{2,1,0:T(8,128)(2,1)} %get-tuple-element.51) | copy-start | bytes 1720324
  18.7 4.6 %collective-permute-start.3 = (f32[328,128]{1,0:T(8,128)S(1)}, f32[328,128]{1,0:T(8,128)S(1)}, u32[]{:S(2)}, u32[]{:S(2)}) collective-permute-start(f32[328,128]{1,0:T(8,128)S(1)} %add.92), channel_id=1, source_target_pairs={{0,2},{1,5},{2,0},{3,7},{4,6},{5,1},{6,4},{7,3},{8,10},{9,13},{10,... | collective-permute-start | bytes 503816 | tf_op jit(solution)/shard_map/ppermute | solution.py:409
  20.2 6.3 %collective-permute-start.8 = (f32[328,128]{1,0:T(8,128)S(1)}, f32[328,128]{1,0:T(8,128)S(1)}, u32[]{:S(2)}, u32[]{:S(2)}) collective-permute-start(f32[328,128]{1,0:T(8,128)S(1)} %add.96), channel_id=1, source_target_pairs={{0,8},{1,3},{2,10},{3,1},{4,12},{5,7},{6,14},{7,5},{8,0},{9,11},{1... | collective-permute-start | bytes 503816 | tf_op jit(solution)/shard_map/ppermute | solution.py:409
  23.3 8.4 %collective-permute-start.4 = (f32[328,128]{1,0:T(8,128)S(1)}, f32[328,128]{1,0:T(8,128)S(1)}, u32[]{:S(2)}, u32[]{:S(2)}) collective-permute-start(f32[328,128]{1,0:T(8,128)S(1)} %add.93), channel_id=1, source_target_pairs={{0,4},{1,9},{2,6},{3,11},{4,0},{5,13},{6,2},{7,15},{8,12},{9,1},{1... | collective-permute-start | bytes 503816 | tf_op jit(solution)/shard_map/ppermute | solution.py:409
  26.5 5.4 %copy-start.8 = (bf16[1,256,1120]{2,1,0:T(8,128)(2,1)S(1)}, bf16[1,256,1120]{2,1,0:T(8,128)(2,1)}, u32[]{:S(2)}) copy-start(bf16[1,256,1120]{2,1,0:T(8,128)(2,1)} %get-tuple-element.52) | copy-start | bytes 1720324
  26.6 7.5 %collective-permute-start.9 = (f32[328,128]{1,0:T(8,128)S(1)}, f32[328,128]{1,0:T(8,128)S(1)}, u32[]{:S(2)}, u32[]{:S(2)}) collective-permute-start(f32[328,128]{1,0:T(8,128)S(1)} %add.97), channel_id=1, source_target_pairs={{0,2},{1,5},{2,0},{3,7},{4,6},{5,1},{6,4},{7,3},{8,10},{9,13},{10,... | collective-permute-start | bytes 503816 | tf_op jit(solution)/shard_map/ppermute | solution.py:409
  31.6 6.3 %collective-permute-start.5 = (f32[328,128]{1,0:T(8,128)S(1)}, f32[328,128]{1,0:T(8,128)S(1)}, u32[]{:S(2)}, u32[]{:S(2)}) collective-permute-start(f32[328,128]{1,0:T(8,128)S(1)} %add.94), channel_id=1, source_target_pairs={{0,8},{1,3},{2,10},{3,1},{4,12},{5,7},{6,14},{7,5},{8,0},{9,11},{1... | collective-permute-start | bytes 503816 | tf_op jit(solution)/shard_map/ppermute | solution.py:409
  34.1 13.0 %collective-permute-start.10 = (f32[328,128]{1,0:T(8,128)S(1)}, f32[328,128]{1,0:T(8,128)S(1)}, u32[]{:S(2)}, u32[]{:S(2)}) collective-permute-start(f32[328,128]{1,0:T(8,128)S(1)} %add.98), channel_id=1, source_target_pairs={{0,4},{1,9},{2,6},{3,11},{4,0},{5,13},{6,2},{7,15},{8,12},{9,1},{1... | collective-permute-start | bytes 503816 | tf_op jit(solution)/shard_map/ppermute | solution.py:409
  38.0 10.4 %collective-permute-start.6 = (f32[328,128]{1,0:T(8,128)S(1)}, f32[328,128]{1,0:T(8,128)S(1)}, u32[]{:S(2)}, u32[]{:S(2)}) collective-permute-start(f32[328,128]{1,0:T(8,128)S(1)} %add.95.whole_ref), channel_id=1, source_target_pairs={{0,1},{1,0},{2,3},{3,2},{4,5},{5,4},{6,7},{7,6},{8,9},{9,8},{10,11... | collective-permute-start | bytes 503816 | tf_op jit(solution)/shard_map/ppermute | solution.py:409
  46.4 1.3 %copy-start.4 = (bf16[2,256,1120]{1,2,0:T(8,128)(2,1)S(1)}, bf16[2,256,1120]{1,2,0:T(8,128)(2,1)}, u32[]{:S(2)}) copy-start(bf16[2,256,1120]{1,2,0:T(8,128)(2,1)} %param.7) | copy-start | bytes 3440644
  47.1 2.3 %slice-start = ((s8[5160960]{0:T(1024)(128)(4,1)}), s8[4194304]{0:T(1024)(128)(4,1)S(1)}, s32[]{:S(2)}) async-start(s8[5160960]{0:T(1024)(128)(4,1)} %bitcast.13), calls=%async_computation | async-start | bytes 8388608
  47.1 7.8 %collective-permute-start.11 = (f32[328,128]{1,0:T(8,128)S(1)}, f32[328,128]{1,0:T(8,128)S(1)}, u32[]{:S(2)}, u32[]{:S(2)}) collective-permute-start(f32[328,128]{1,0:T(8,128)S(1)} %add.99.packed_ref), channel_id=1, source_target_pairs={{0,1},{1,0},{2,3},{3,2},{4,5},{5,4},{6,7},{7,6},{8,9},{9,8},{10,11... | collective-permute-start | bytes 503816 | tf_op jit(solution)/shard_map/ppermute | solution.py:409
  47.7 2.0 %slice-start.1 = ((s8[5160960]{0:T(1024)(128)(4,1)}), s8[966656]{0:T(1024)(128)(4,1)S(1)}, s32[]{:S(2)}) async-start(s8[5160960]{0:T(1024)(128)(4,1)} %bitcast.13), calls=%async_computation.1 | async-start | bytes 1933312
  48.4 1.4 %copy-start.5 = (f32[20,2240]{1,0:T(8,128)S(1)}, f32[20,2240]{1,0:T(8,128)}, u32[]{:S(2)}) copy-start(f32[20,2240]{1,0:T(8,128)} %gate_ref.1) | copy-start | bytes 537604
  48.4 1.4 %copy-start.7 = (s32[2]{0:T(128)S(1)}, s32[2]{0:T(128)}, u32[]{:S(2)}) copy-start(s32[2]{0:T(128)} %step_ref.1) | copy-start | bytes 28

commit v5 on v4

--- a/solution.py
+++ b/solution.py
@@ -53,18 +53,17 @@
 def pack_states(keys, values, out_ref):
     acc = [jnp.zeros((TROWS, LANES), F32) for _ in TILE_BASE]
     rows = lax.broadcasted_iota(jnp.int32, (TROWS, LANES), 0)
-    for head in range(HALF_HEADS):
-        start = HD * head // 16 * 16
-        stop = min(HALF, -(-(HD * head + HD) // 16) * 16)
-        shift = HD * head - start
-        for tile in tiles_of(head):
-            base = TILE_BASE[tile]
-            prod = nt_dot(values[start:stop], keys[base : base + LANES])
+    ones = jnp.ones((16, TOK), BF16)
+    for tile, base in enumerate(TILE_BASE):
+        heads = [h for h in range(HALF_HEADS) if tile in tiles_of(h)]
+        start = HD * heads[0] // 16 * 16
+        stop = min(HALF, -(-(HD * heads[-1] + HD) // 16) * 16)
+        prod = nt_dot(jnp.concatenate([values[start:stop], ones], axis=0), keys[base : base + LANES])
+        for head in heads:
+            shift = HD * head - start
             part = jnp.concatenate([prod[shift : shift + HD], jnp.zeros((TROWS - HD, LANES), F32)], axis=0)
             acc[tile] = jnp.where(lane_mask((TROWS, LANES), tile, head), part, acc[tile])
-    ones = jnp.ones((16, TOK), BF16)
-    for tile, base in enumerate(TILE_BASE):
-        total = nt_dot(ones, keys[base : base + LANES])[:1]
+        total = prod[stop - start : stop - start + 1]
         acc[tile] = jnp.where(rows == HD, jnp.broadcast_to(total, (TROWS, LANES)), acc[tile])
     for tile in range(FULL_TILES):
         out_ref[tile * TROWS : (tile + 1) * TROWS] = acc[tile]
@@ -86,72 +85,61 @@
     return one, (x - one.astype(F32)).astype(BF16)
 
 
-def state_kernel(picks, key_hbm, value_hbm, *refs):
-    out_refs, (key, value, sems) = refs[: len(picks)], refs[len(picks) :]
+def state_kernel(key_hbm, value_hbm, out_ref, key, value, sems):
+    half = core_of()
+    first = pl.ds(pl.multiple_of((1 - half) * HALF, HALF), HALF)
+    later = pl.ds(pl.multiple_of(half * HALF, HALF), HALF)
     loads = []
-    for n, (step, own) in enumerate(picks):
-        half = core_of() if own else 1 - core_of()
+    for n, spot in enumerate((first, later)):
+        for m, (source, held) in enumerate(((key_hbm, key), (value_hbm, value))):
+            loads.append(pltpu.make_async_copy(source.at[0, spot], held.at[spot], sems.at[n, m]))
+            loads[-1].start()
+    for load in loads[:2]:
+        load.wait()
+    pack_states(key[first], value[first], out_ref)
+    for load in loads[2:]:
+        load.wait()
+
+
+def keep_kernel(key_hbm, value_hbm, key0, value0, out_ref, key, value, sems):
+    loads = [
+        pltpu.make_async_copy(key_hbm.at[1], key, sems.at[0]),
+        pltpu.make_async_copy(value_hbm.at[1], value, sems.at[1]),
+    ]
+    for load in loads:
+        load.start()
+    own = pl.ds(pl.multiple_of(core_of() * HALF, HALF), HALF)
+    pack_states(key0[own], value0[own], out_ref)
+    for load in loads:
+        load.wait()
+
+
+def both_kernel(key, value, send_ref, keep_ref):
+    for half, out_ref in ((1 - core_of(), send_ref), (core_of(), keep_ref)):
         spot = pl.ds(pl.multiple_of(half * HALF, HALF), HALF)
-        loads.append(
-            (
-                pltpu.make_async_copy(key_hbm.at[step, spot], key.at[n], sems.at[n, 0]),
-                pltpu.make_async_copy(value_hbm.at[step, spot], value.at[n], sems.at[n, 1]),
-            )
-        )
-    for pair in loads:
-        for load in pair:
-            load.start()
-    for n, pair in enumerate(loads):
-        for load in pair:
-            load.wait()
-        pack_states(key[n], value[n], out_refs[n])
-
-
-def held_kernel(picks, key_ref, value_ref, *out_refs):
-    for (step, own), out_ref in zip(picks, out_refs):
-        half = core_of() if own else 1 - core_of()
-        spot = pl.ds(pl.multiple_of(half * HALF, HALF), HALF)
-        pack_states(key_ref[step, spot], value_ref[step, spot], out_ref)
-
-
-def held_states(keys, values, picks):
-    n = len(picks)
-    vmem = pl.BlockSpec(memory_space=pltpu.VMEM)
-    return pl.pallas_call(
-        functools.partial(held_kernel, picks),
-        out_shape=(jax.ShapeDtypeStruct((PACKED, LANES), F32),) * n,
-        in_specs=[vmem, vmem],
-        out_specs=(vmem,) * n,
+        pack_states(key[spot], value[spot], out_ref)
+
+
+def local_states(kernel, sources, held, outs, sems):
+    vmem = pl.BlockSpec(memory_space=pltpu.VMEM)
+    packed = jax.ShapeDtypeStruct((PACKED, LANES), F32)
+    copies = (jax.ShapeDtypeStruct(sources[0].shape[1:], BF16),) * 2 if sources else ()
+    return pl.pallas_call(
+        kernel,
+        out_shape=(packed,) * outs + copies,
+        in_specs=[pl.BlockSpec(memory_space=pltpu.HBM)] * len(sources) + [vmem] * len(held),
+        out_specs=(vmem,) * (outs + len(copies)),
+        scratch_shapes=[pltpu.SemaphoreType.DMA(sems)] if sems else [],
         compiler_params=pltpu.CompilerParams(vmem_limit_bytes=8 << 20),
-        cost_estimate=pl.CostEstimate(flops=300_000_000 * n, bytes_accessed=800_000 * n, transcendentals=0),
-        name="held_states",
-    )(keys, values)
-
-
-def local_states(keys, values, picks):
-    n = len(picks)
-    hbm = pl.BlockSpec(memory_space=pltpu.HBM)
-    return pl.pallas_call(
-        functools.partial(state_kernel, picks),
-        out_shape=(jax.ShapeDtypeStruct((PACKED, LANES), F32),) * n,
-        in_specs=[hbm, hbm],
-        out_specs=(pl.BlockSpec(memory_space=pltpu.VMEM),) * n,
-        scratch_shapes=[
-            pltpu.VMEM((n, HALF, TOK), BF16),
-            pltpu.VMEM((n, HALF, TOK), BF16),
-            pltpu.SemaphoreType.DMA((n, 2)),
-        ],
-        compiler_params=pltpu.CompilerParams(vmem_limit_bytes=4 << 20),
-        cost_estimate=pl.CostEstimate(flops=300_000_000 * n, bytes_accessed=800_000 * n, transcendentals=0),
-        name="local_states",
-    )(keys, values)
-
-
-def plain_kernel(value_ref, weight_ref, plain_ref, near_ref, far_ref, taps_ref):
+        cost_estimate=pl.CostEstimate(flops=300_000_000 * outs, bytes_accessed=1_200_000, transcendentals=0),
+    )(*sources, *held)
+
+
+def plain_kernel(value0, value1, weight_ref, plain_ref, near_ref, far_ref, taps_ref):
     taps_ref[...] = weight_ref[...]
     first = core_of() == 0
     for step in range(2):
-        plain_ref[step] = value_ref[step].T
+        plain_ref[step] = (value0, value1)[step][...].T
     head, tail = plain_ref[0, :COLS], plain_ref[0, TOK - COLS :]
     near_ref[...] = jnp.where(first, tail, head)
     far_ref[...] = jnp.where(first, head, tail)
@@ -159,17 +147,17 @@
 
 def plain_values(values, weights):
     vmem = pl.BlockSpec(memory_space=pltpu.VMEM)
-    width = values.shape[1]
+    width = values[0].shape[0]
     row = jax.ShapeDtypeStruct((COLS, width), BF16)
     return pl.pallas_call(
         plain_kernel,
         out_shape=(jax.ShapeDtypeStruct((2, TOK, width), BF16), row, row, jax.ShapeDtypeStruct(weights.shape, F32)),
-        in_specs=[vmem] * 2,
+        in_specs=[vmem] * 3,
         out_specs=(vmem,) * 4,
         compiler_params=pltpu.CompilerParams(vmem_limit_bytes=8 << 20),
         cost_estimate=pl.CostEstimate(flops=1_000_000, bytes_accessed=2_400_000, transcendentals=0),
         name="plain_values",
-    )(values, weights)
+    )(*values, weights)
 
 
 def convolve(padded, conv_weight):
@@ -420,10 +408,11 @@
         return [lambda c, b=b, t=t: t if c else b for b, t in pairs]
 
     first = core_of() == 0
-    (send0,) = local_states(far_keys, far_values, ((0, 0),))
-    (keep0,) = held_states(keys, values, ((0, 1),))
-    send1, keep1 = held_states(keys, values, ((1, 0), (1, 1)))
-    plain, near, far, conv_weight = plain_values(values, conv_weight)
+    sources = far_keys, far_values
+    send0, *held0 = local_states(state_kernel, sources, (), 1, (2, 2))
+    keep0, *held1 = local_states(keep_kernel, sources, held0, 1, (2,))
+    send1, keep1 = local_states(both_kernel, (), held1, 2, None)
+    plain, near, far, conv_weight = plain_values((held0[1], held1[1]), conv_weight)
     near = partner(near)
     links = [p for i in range(1, count - 1, 2) for p in ((i, i + 1), (i + 1, i))]
     far = lax.ppermute(far, "tm", links)

time: 56.5 us -> 52.3 us (0.926)
  local copies, waits for them, and re-layouts: 6.52 us -> 3.32 us
  other arithmetic: 3.32 us -> 2.3 us
    unnamed x24 -> x14, local copies, waits for them, and re-layouts: 5.17 us -> 3 us
    slice x1, local copies, waits for them, and re-layouts: 1.12 us -> 0.09 us  [local(): grid[0]]
    select_n x1, other arithmetic: 1.05 us -> 0.03 us  [local(): above, below = (jnp.where(first, far, near), jnp.where(first, near, far))]
  transfers between devices with their start and end apart: 12 -> 12, of which waited for: 4 -> 4; matrix products, arithmetic and copies ran while one was open for 8% -> 5% of each run, Pallas kernels for 24% -> 20%
where the time goes in v5:
time: 52.3 us; the launch traced here: 51.9 us
  starting transfers between devices  20.1 us (38%)
  Pallas kernels  14.8 us (28%)
  waiting for transfers between devices  10.5 us (20%)
  local copies, waits for them, and re-layouts  3.32 us (6%)
  other arithmetic  2.3 us (4%)
  between operations  0.89 us (2%)
    ppermute x11, starting transfers between devices, swap(): return lax.ppermute(x, 'tm', [(i, i ^ pick(i % 2)) for i in range(count)])  15.6 us
    ppermute x11, waiting for transfers between devices, swap(): return lax.ppermute(x, 'tm', [(i, i ^ pick(i % 2)) for i in range(count)])  10.5 us
    pallas_call x1, Pallas kernels, project(): pl.pallas_call(functools.partial(project_kernel, chunks), out_shape=jax.S...  5.13 us
    ppermute x1, starting transfers between devices, local(): far = lax.ppermute(far, 'tm', links)  4.53 us
    pallas_call x3, Pallas kernels, local_states(): pl.pallas_call(kernel, out_shape=(packed,) * outs + copies, in_specs=[pl....  3.25 us
    unnamed x14, local copies, waits for them, and re-layouts  3 us
    pallas_call x1, Pallas kernels, stage(): pl.pallas_call(stage_kernel, out_shape=jax.ShapeDtypeStruct(weight.shape,...  2.47 us
    add x2, other arithmetic, convolve(): summed + widened[tap_row:tap_row + ROWS_DEV, tap_col:tap_col + COLS] * co...  1.78 us
  transfers between devices with their start and end apart: 12, of which 4 were waited for; matrix products, arithmetic and copies ran while one was open for 5% of the time, Pallas kernels for 20%

profile of v5, /device:TPU:1, one launch (start us, length us, event | category | flops | bytes accessed | tf_op | source)
XLA Modules:
  0.0 51.9 jit_solution(7724651716789223603)
XLA Ops:
  0.6 1.5 %shard_map.94 = (f32[328,128]{1,0:T(8,128)S(1)}, bf16[1120,256]{1,0:T(8,128)(2,1)S(1)}, bf16[1120,256]{1,0:T(8,128)(2,1)S(1)}) custom-call(bf16[2,1120,256]{2,1,0:T(8,128)(2,1)} %bitcast.20, bf16[2,1120,256]{2,1,0:T(8,128)(2,1)} %bitcast.22), custom_call_target="tpu_custom_call" | custom-call | flops 300000000 | bytes 1200000 | tf_op jit(solution)/shard_map/pallas_call | solution.py:127
  2.1 0.0 copy-start.3
  2.1 1.3 %shard_map.95 = (f32[328,128]{1,0:T(8,128)S(1)}, bf16[1120,256]{1,0:T(8,128)(2,1)S(1)}, bf16[1120,256]{1,0:T(8,128)(2,1)S(1)}) custom-call(bf16[2,1120,256]{2,1,0:T(8,128)(2,1)} %bitcast.21, bf16[2,1120,256]{2,1,0:T(8,128)(2,1)} %bitcast.23, bf16[1120,256]{1,0:T(8,128)(2,1)S(1)} %get-tuple-element.25.key0, bf16[1120,256]{1,0:T(8,128)(2,1)S(1)} %get-tuple-element.24.value0), custom_call_target="tpu_custom_call" | custom-call | flops 300000000 | bytes 1200000 | tf_op jit(solution)/shard_map/pallas_call | solution.py:127
  3.4 0.4 plain_values.1
  3.8 0.1 collective-permute-start.1
  3.9 4.5 %collective-permute-start = (bf16[64,1120]{1,0:T(8,128)(2,1)S(1)}, bf16[64,1120]{1,0:T(8,128)(2,1)S(1)}, u32[]{:S(2)}, u32[]{:S(2)}) collective-permute-start(bf16[64,1120]{1,0:T(8,128)(2,1)S(1)} %get-tuple-element.28), channel_id=1, source_target_pairs={{1,2},{2,1},{3,4},{4,3},{5,6},{6,5},{7,8},{8,7},{9,10},{10,9},{11,... | collective-permute-start | bytes 430088 | tf_op jit(solution)/shard_map/ppermute | solution.py:418
  8.4 0.1 collective-permute-start.2
  8.5 0.5 shard_map.96
  9.0 0.5 collective-permute-start.7
  9.5 0.1 fusion.28
  9.6 2.5 %stage.1.weight = bf16[1120,2240]{1,0:T(8,128)(2,1)S(1)} custom-call(bf16[1120,2240]{1,0:T(8,128)(2,1)} %weight_hbm.1), custom_call_target="tpu_custom_call" | custom-call | bytes 5000000 | tf_op jit(solution)/shard_map/stage/pallas_call | solution.py:286
  12.1 2.3 %copy-done = bf16[1120,2240]{1,0:T(8,128)(2,1)} copy-done((bf16[1120,2240]{1,0:T(8,128)(2,1)}, bf16[1120,2240]{1,0:T(8,128)(2,1)S(1)}, u32[]{:S(2)}) %copy-start) | copy-done | bytes 5017624
  14.3 0.1 slice_reduce_fusion.17
  14.5 0.0 collective-permute-done.1
  14.5 0.0 collective-permute-done
  14.5 0.0 collective-permute-done.2
  14.6 1.4 %collective-permute-start.3 = (f32[328,128]{1,0:T(8,128)S(1)}, f32[328,128]{1,0:T(8,128)S(1)}, u32[]{:S(2)}, u32[]{:S(2)}) collective-permute-start(f32[328,128]{1,0:T(8,128)S(1)} %add.92), channel_id=1, source_target_pairs={{0,2},{1,5},{2,0},{3,7},{4,6},{5,1},{6,4},{7,3},{8,10},{9,13},{10,... | collective-permute-start | bytes 503816 | tf_op jit(solution)/shard_map/ppermute | solution.py:397
  15.9 0.1 maximum_convert_fusion
  16.1 1.3 %collective-permute-start.8 = (f32[328,128]{1,0:T(8,128)S(1)}, f32[328,128]{1,0:T(8,128)S(1)}, u32[]{:S(2)}, u32[]{:S(2)}) collective-permute-start(f32[328,128]{1,0:T(8,128)S(1)} %add.96), channel_id=1, source_target_pairs={{0,8},{1,3},{2,10},{3,1},{4,12},{5,7},{6,14},{7,5},{8,0},{9,11},{1... | collective-permute-start | bytes 503816 | tf_op jit(solution)/shard_map/ppermute | solution.py:397
  17.4 1.7 %collective-permute-done.3 = f32[328,128]{1,0:T(8,128)S(1)} collective-permute-done((f32[328,128]{1,0:T(8,128)S(1)}, f32[328,128]{1,0:T(8,128)S(1)}, u32[]{:S(2)}, u32[]{:S(2)}) %collective-permute-start.3) | collective-permute-done | bytes 167968 | tf_op jit(solution)/shard_map/ppermute | solution.py:397
  19.2 2.4 %collective-permute-start.4 = (f32[328,128]{1,0:T(8,128)S(1)}, f32[328,128]{1,0:T(8,128)S(1)}, u32[]{:S(2)}, u32[]{:S(2)}) collective-permute-start(f32[328,128]{1,0:T(8,128)S(1)} %add.93), channel_id=1, source_target_pairs={{0,4},{1,9},{2,6},{3,11},{4,0},{5,13},{6,2},{7,15},{8,12},{9,1},{1... | collective-permute-start | bytes 503816 | tf_op jit(solution)/shard_map/ppermute | solution.py:397
  21.5 0.9 %fusion.8 = f32[4,64,1120]{2,1,0:T(8,128)S(1)} fusion(f32[6,64,1120]{2,1,0:T(8,128)S(1)} %maximum_convert_fusion, f32[1120]{0:T(1024)S(1)} %get-tuple-element.55, f32[1120]{0:T(1024)S(1)} %get-tuple-element.56, f32[1120]{0:T(1024)S(1)} %get-tuple-element.57, f32[1120]{0:T(1024)S(1)} %get-tuple-element.58, f32[1120]{0:T(1024)S(1)} %get-tuple-element.59, ...), kind=kLoop, calls=%fused_computation.20 | loop fusion | flops 4874240 | bytes 6529024 | tf_op jit(solution)/shard_map/add | solution.py:169
  22.5 1.4 %collective-permute-start.9 = (f32[328,128]{1,0:T(8,128)S(1)}, f32[328,128]{1,0:T(8,128)S(1)}, u32[]{:S(2)}, u32[]{:S(2)}) collective-permute-start(f32[328,128]{1,0:T(8,128)S(1)} %add.97), channel_id=1, source_target_pairs={{0,2},{1,5},{2,0},{3,7},{4,6},{5,1},{6,4},{7,3},{8,10},{9,13},{10,... | collective-permute-start | bytes 503816 | tf_op jit(solution)/shard_map/ppermute | solution.py:397
  23.8 3.7 %collective-permute-done.4 = f32[328,128]{1,0:T(8,128)S(1)} collective-permute-done((f32[328,128]{1,0:T(8,128)S(1)}, f32[328,128]{1,0:T(8,128)S(1)}, u32[]{:S(2)}, u32[]{:S(2)}) %collective-permute-start.4) | collective-permute-done | bytes 167968 | tf_op jit(solution)/shard_map/ppermute | solution.py:397
  27.5 0.3 collective-permute-start.5
  27.8 0.1 maximum_convert_fusion.1
  28.0 0.1 slice_reduce_fusion.8
  28.1 1.8 %collective-permute-done.9 = f32[328,128]{1,0:T(8,128)S(1)} collective-permute-done((f32[328,128]{1,0:T(8,128)S(1)}, f32[328,128]{1,0:T(8,128)S(1)}, u32[]{:S(2)}, u32[]{:S(2)}) %collective-permute-start.9) | collective-permute-done | bytes 167968 | tf_op jit(solution)/shard_map/ppermute | solution.py:397
  29.9 0.6 %collective-permute-start.10 = (f32[328,128]{1,0:T(8,128)S(1)}, f32[328,128]{1,0:T(8,128)S(1)}, u32[]{:S(2)}, u32[]{:S(2)}) collective-permute-start(f32[328,128]{1,0:T(8,128)S(1)} %add.98), channel_id=1, source_target_pairs={{0,4},{1,9},{2,6},{3,11},{4,0},{5,13},{6,2},{7,15},{8,12},{9,1},{1... | collective-permute-start | bytes 503816 | tf_op jit(solution)/shard_map/ppermute | solution.py:397
  30.6 3.3 %collective-permute-done.5 = f32[328,128]{1,0:T(8,128)S(1)} collective-permute-done((f32[328,128]{1,0:T(8,128)S(1)}, f32[328,128]{1,0:T(8,128)S(1)}, u32[]{:S(2)}, u32[]{:S(2)}) %collective-permute-start.5) | collective-permute-done | bytes 167968 | tf_op jit(solution)/shard_map/ppermute | solution.py:397
  33.9 7.5 %collective-permute-start.6 = (f32[328,128]{1,0:T(8,128)S(1)}, f32[328,128]{1,0:T(8,128)S(1)}, u32[]{:S(2)}, u32[]{:S(2)}) collective-permute-start(f32[328,128]{1,0:T(8,128)S(1)} %add.95.whole_ref), channel_id=1, source_target_pairs={{0,1},{1,0},{2,3},{3,2},{4,5},{5,4},{6,7},{7,6},{8,9},{9,8},{10,11... | collective-permute-start | bytes 503816 | tf_op jit(solution)/shard_map/ppermute | solution.py:397
  41.4 0.9 %fusion.22 = f32[4,64,1120]{2,1,0:T(8,128)S(1)} fusion(f32[6,64,1120]{2,1,0:T(8,128)S(1)} %maximum_convert_fusion.1, f32[1120]{0:T(1024)S(1)} %get-tuple-element.46, f32[1120]{0:T(1024)S(1)} %get-tuple-element.47, f32[1120]{0:T(1024)S(1)} %get-tuple-element.48, f32[1120]{0:T(1024)S(1)} %get-tuple-element.49, f32[1120]{0:T(1024)S(1)} %get-tuple-element.50, ...), kind=kLoop, calls=%fused_computation.34 | loop fusion | flops 4874240 | bytes 6529024 | tf_op jit(solution)/shard_map/add | solution.py:169
  42.3 0.0 copy-start.1
  42.3 0.7 %turn.1.conv_ref = f32[2,1120,256]{2,1,0:T(8,128)S(1)} custom-call(f32[256,1120]{1,0:T(8,128)S(1)} %bitcast.15, f32[256,1120]{1,0:T(8,128)S(1)} %bitcast.16), custom_call_target="tpu_custom_call" | custom-call | flops 1000000 | bytes 4600000 | tf_op jit(solution)/shard_map/turn/pallas_call | solution.py:243
  43.0 0.0 slice-start
  43.0 0.1 collective-permute-start.11
  43.1 0.3 fresh_own.1
  43.5 0.1 copy-done.1
  43.5 0.7 %spread.2.own_ref = bf16[560,512]{1,0:T(8,128)(2,1)S(1)} custom-call(bf16[2,1120,256]{2,1,0:T(8,128)(2,1)S(1)} %bitcast.17, f32[2,1120,256]{2,1,0:T(8,128)S(1)} %turn.1.conv_ref, f32[328,128]{1,0:T(8,128)S(1)} %add.95.whole_ref, f32[328,128]{1,0:T(8,128)S(1)} %get-tuple-element.36.zero_ref, f32[328,128]{1,0:T(8,128)S(1)} %get-tuple-element.39.one_ref), custom_call_target="tpu_custom_call" | custom-call | flops 800000000 | bytes 2000000 | tf_op jit(solution)/shard_map/spread/pallas_call | solution.py:223
  44.3 0.0 copy-start.2
  44.3 0.0 copy-start.4
  44.3 0.0 collective-permute-done.6.whole_ref
  44.3 0.7 %spread.3.other_ref = bf16[560,512]{1,0:T(8,128)(2,1)S(1)} custom-call(bf16[2,1120,256]{2,1,0:T(8,128)(2,1)S(1)} %bitcast.18, f32[2,1120,256]{2,1,0:T(8,128)S(1)} %turn.1.conv_ref, f32[328,128]{1,0:T(8,128)S(1)} %collective-permute-done.6.whole_ref, f32[328,128]{1,0:T(8,128)S(1)} %get-tuple-element.37.zero_ref, f32[328,128]{1,0:T(8,128)S(1)} %get-tuple-element.40.one_ref), custom_call_target="tpu_custom_call" | custom-call | flops 800000000 | bytes 2000000 | tf_op jit(solution)/shard_map/spread/pallas_call | solution.py:223
  45.0 0.2 slice-done
  45.3 0.3 slice-done.1
  45.5 0.1 copy-done.2
  45.7 5.1 %project.1 = f32[2,2240,256]{2,1,0:T(8,128)} custom-call(s32[2]{0:T(128)S(1)} %copy-done.4, bf16[1120,2240]{1,0:T(8,128)(2,1)S(1)} %bitcast.14, f32[20,2240]{1,0:T(8,128)S(1)} %copy-done.2, bf16[560,512]{1,0:T(8,128)(2,1)S(1)} %spread.2.own_ref, bf16[560,512]{1,0:T(8,128)(2,1)S(1)} %spread.3.other_ref), custom_call_target="tpu_custom_call" | custom-call | flops 3000000000 | bytes 14000000 | tf_op jit(solution)/shard_map/project/pallas_call | solution.py:303
  50.8 1.1 %fresh_rest.1 = (f32[70,16,70]{2,1,0:T(8,128)}, f32[16,70]{1,0:T(8,128)}) custom-call(f32[328,128]{1,0:T(8,128)S(1)} %collective-permute-done.11.packed_ref, f32[70,8,70]{2,1,0:T(8,128)S(1)} %get-tuple-element.41.own_state, f32[8,70]{1,0:T(8,128)S(1)} %get-tuple-element.42.own_total), custom_call_target="tpu_custom_call" | custom-call | flops 1000000 | bytes 600000 | tf_op jit(solution)/shard_map/fresh_rest/pallas_call | solution.py:374
  (18 shorter events, 0.2 us)
Async XLA Ops:
  2.1 1.3 %copy-start.3 = (f32[9,1120]{1,0:T(8,128)S(1)}, f32[9,1120]{1,0:T(8,128)}, u32[]{:S(2)}) copy-start(f32[9,1120]{1,0:T(8,128)} %weight_ref.1) | copy-start | bytes 120964
  3.8 10.7 %collective-permute-start.1 = (bf16[64,1120]{1,0:T(8,128)(2,1)S(1)}, bf16[64,1120]{1,0:T(8,128)(2,1)S(1)}, u32[]{:S(2)}, u32[]{:S(2)}) collective-permute-start(bf16[64,1120]{1,0:T(8,128)(2,1)S(1)} %get-tuple-element.29), channel_id=1, source_target_pairs={{0,1},{1,0},{2,3},{3,2},{4,5},{5,4},{6,7},{7,6},{8,9},{9,8},{10,11... | collective-permute-start | bytes 430088 | tf_op jit(solution)/shard_map/ppermute | solution.py:397
  3.9 10.6 %collective-permute-start = (bf16[64,1120]{1,0:T(8,128)(2,1)S(1)}, bf16[64,1120]{1,0:T(8,128)(2,1)S(1)}, u32[]{:S(2)}, u32[]{:S(2)}) collective-permute-start(bf16[64,1120]{1,0:T(8,128)(2,1)S(1)} %get-tuple-element.28), channel_id=1, source_target_pairs={{1,2},{2,1},{3,4},{4,3},{5,6},{6,5},{7,8},{8,7},{9,10},{10,9},{11,... | collective-permute-start | bytes 430088 | tf_op jit(solution)/shard_map/ppermute | solution.py:418
  8.4 6.1 %collective-permute-start.2 = (f32[328,128]{1,0:T(8,128)S(1)}, f32[328,128]{1,0:T(8,128)S(1)}, u32[]{:S(2)}, u32[]{:S(2)}) collective-permute-start(f32[328,128]{1,0:T(8,128)S(1)} %get-tuple-element.37.zero_ref), channel_id=1, source_target_pairs={{0,1},{1,0},{2,3},{3,2},{4,5},{5,4},{6,7},{7,6},{8,9},{9,8},{10,11... | collective-permute-start | bytes 503816 | tf_op jit(solution)/shard_map/ppermute | solution.py:397
  9.0 7.1 %collective-permute-start.7 = (f32[328,128]{1,0:T(8,128)S(1)}, f32[328,128]{1,0:T(8,128)S(1)}, u32[]{:S(2)}, u32[]{:S(2)}) collective-permute-start(f32[328,128]{1,0:T(8,128)S(1)} %get-tuple-element.40.one_ref), channel_id=1, source_target_pairs={{0,1},{1,0},{2,3},{3,2},{4,5},{5,4},{6,7},{7,6},{8,9},{9,8},{10,11... | collective-permute-start | bytes 503816 | tf_op jit(solution)/shard_map/ppermute | solution.py:397
  12.1 2.3 %copy-start = (bf16[1120,2240]{1,0:T(8,128)(2,1)}, bf16[1120,2240]{1,0:T(8,128)(2,1)S(1)}, u32[]{:S(2)}) copy-start(bf16[1120,2240]{1,0:T(8,128)(2,1)S(1)} %stage.1.weight) | copy-start | bytes 15052804
  14.6 4.6 %collective-permute-start.3 = (f32[328,128]{1,0:T(8,128)S(1)}, f32[328,128]{1,0:T(8,128)S(1)}, u32[]{:S(2)}, u32[]{:S(2)}) collective-permute-start(f32[328,128]{1,0:T(8,128)S(1)} %add.92), channel_id=1, source_target_pairs={{0,2},{1,5},{2,0},{3,7},{4,6},{5,1},{6,4},{7,3},{8,10},{9,13},{10,... | collective-permute-start | bytes 503816 | tf_op jit(solution)/shard_map/ppermute | solution.py:397
  16.1 6.3 %collective-permute-start.8 = (f32[328,128]{1,0:T(8,128)S(1)}, f32[328,128]{1,0:T(8,128)S(1)}, u32[]{:S(2)}, u32[]{:S(2)}) collective-permute-start(f32[328,128]{1,0:T(8,128)S(1)} %add.96), channel_id=1, source_target_pairs={{0,8},{1,3},{2,10},{3,1},{4,12},{5,7},{6,14},{7,5},{8,0},{9,11},{1... | collective-permute-start | bytes 503816 | tf_op jit(solution)/shard_map/ppermute | solution.py:397
  19.2 8.3 %collective-permute-start.4 = (f32[328,128]{1,0:T(8,128)S(1)}, f32[328,128]{1,0:T(8,128)S(1)}, u32[]{:S(2)}, u32[]{:S(2)}) collective-permute-start(f32[328,128]{1,0:T(8,128)S(1)} %add.93), channel_id=1, source_target_pairs={{0,4},{1,9},{2,6},{3,11},{4,0},{5,13},{6,2},{7,15},{8,12},{9,1},{1... | collective-permute-start | bytes 503816 | tf_op jit(solution)/shard_map/ppermute | solution.py:397
  22.5 7.5 %collective-permute-start.9 = (f32[328,128]{1,0:T(8,128)S(1)}, f32[328,128]{1,0:T(8,128)S(1)}, u32[]{:S(2)}, u32[]{:S(2)}) collective-permute-start(f32[328,128]{1,0:T(8,128)S(1)} %add.97), channel_id=1, source_target_pairs={{0,2},{1,5},{2,0},{3,7},{4,6},{5,1},{6,4},{7,3},{8,10},{9,13},{10,... | collective-permute-start | bytes 503816 | tf_op jit(solution)/shard_map/ppermute | solution.py:397
  27.5 6.3 %collective-permute-start.5 = (f32[328,128]{1,0:T(8,128)S(1)}, f32[328,128]{1,0:T(8,128)S(1)}, u32[]{:S(2)}, u32[]{:S(2)}) collective-permute-start(f32[328,128]{1,0:T(8,128)S(1)} %add.94), channel_id=1, source_target_pairs={{0,8},{1,3},{2,10},{3,1},{4,12},{5,7},{6,14},{7,5},{8,0},{9,11},{1... | collective-permute-start | bytes 503816 | tf_op jit(solution)/shard_map/ppermute | solution.py:397
  29.9 13.0 %collective-permute-start.10 = (f32[328,128]{1,0:T(8,128)S(1)}, f32[328,128]{1,0:T(8,128)S(1)}, u32[]{:S(2)}, u32[]{:S(2)}) collective-permute-start(f32[328,128]{1,0:T(8,128)S(1)} %add.98), channel_id=1, source_target_pairs={{0,4},{1,9},{2,6},{3,11},{4,0},{5,13},{6,2},{7,15},{8,12},{9,1},{1... | collective-permute-start | bytes 503816 | tf_op jit(solution)/shard_map/ppermute | solution.py:397
  33.9 10.4 %collective-permute-start.6 = (f32[328,128]{1,0:T(8,128)S(1)}, f32[328,128]{1,0:T(8,128)S(1)}, u32[]{:S(2)}, u32[]{:S(2)}) collective-permute-start(f32[328,128]{1,0:T(8,128)S(1)} %add.95.whole_ref), channel_id=1, source_target_pairs={{0,1},{1,0},{2,3},{3,2},{4,5},{5,4},{6,7},{7,6},{8,9},{9,8},{10,11... | collective-permute-start | bytes 503816 | tf_op jit(solution)/shard_map/ppermute | solution.py:397
  42.3 1.3 %copy-start.1 = (bf16[2,256,1120]{1,2,0:T(8,128)(2,1)S(1)}, bf16[2,256,1120]{1,2,0:T(8,128)(2,1)}, u32[]{:S(2)}) copy-start(bf16[2,256,1120]{1,2,0:T(8,128)(2,1)} %param.7) | copy-start | bytes 3440644
  43.0 2.3 %slice-start = ((s8[5160960]{0:T(1024)(128)(4,1)}), s8[4194304]{0:T(1024)(128)(4,1)S(1)}, s32[]{:S(2)}) async-start(s8[5160960]{0:T(1024)(128)(4,1)} %bitcast.13), calls=%async_computation | async-start | bytes 8388608
  43.0 7.8 %collective-permute-start.11 = (f32[328,128]{1,0:T(8,128)S(1)}, f32[328,128]{1,0:T(8,128)S(1)}, u32[]{:S(2)}, u32[]{:S(2)}) collective-permute-start(f32[328,128]{1,0:T(8,128)S(1)} %add.99.packed_ref), channel_id=1, source_target_pairs={{0,1},{1,0},{2,3},{3,2},{4,5},{5,4},{6,7},{7,6},{8,9},{9,8},{10,11... | collective-permute-start | bytes 503816 | tf_op jit(solution)/shard_map/ppermute | solution.py:397
  43.5 2.0 %slice-start.1 = ((s8[5160960]{0:T(1024)(128)(4,1)}), s8[966656]{0:T(1024)(128)(4,1)S(1)}, s32[]{:S(2)}) async-start(s8[5160960]{0:T(1024)(128)(4,1)} %bitcast.13), calls=%async_computation.1 | async-start | bytes 1933312
  44.3 1.4 %copy-start.2 = (f32[20,2240]{1,0:T(8,128)S(1)}, f32[20,2240]{1,0:T(8,128)}, u32[]{:S(2)}) copy-start(f32[20,2240]{1,0:T(8,128)} %gate_ref.1) | copy-start | bytes 537604
  44.3 1.4 %copy-start.4 = (s32[2]{0:T(128)S(1)}, s32[2]{0:T(128)}, u32[]{:S(2)}) copy-start(s32[2]{0:T(128)} %step_ref.1) | copy-start | bytes 28
